TPU v7x, 512 devices: a whole 4x4x16 slice. The times are simulated.
512 devices in a mesh: dp: 16 (over z_lo, x), tensor: 32 (over y, z_hi, core).
Axes of the slice: x: 4, y: 4, z: 16 (z_hi: 4, z_lo: 4; z = z_hi * 4 + z_lo), core: 2. Of those that a mesh axis runs over, the one named last changes fastest.
Arguments:
- hidden_states: bfloat16 [4096, 2048], P(('dp', 'tensor')), may hold values from -36 to 36
- attention_gain: float32 [2048], replicated, may hold values from 0.4 to 2.5
- feedforward_gain: float32 [2048], replicated, may hold values from 0.4 to 2.5
- heads_weight: bfloat16 [2048, 6144], P(None, 'tensor'), may hold values from -1.9887378 to 1.9887378
- output_weight: bfloat16 [2048, 2048], P('tensor'), may hold values from -0.125 to 0.125
- upward_weight: bfloat16 [2048, 8192], P(None, 'tensor'), may hold values from -0.125 to 0.125
- downward_weight: bfloat16 [8192, 2048], P('tensor'), may hold values from -0.0625 to 0.0625
- segments: int32 [16, 256], P('dp'), may hold values from 0 to 7, never falling along the last dimension, each value on 1 to 128 neighbouring positions
- page_targets: int32 [256, 1], P('dp'), may hold values from 0 to 15; in each aligned block of 16 rows (0 to 15, 16 to 31, ...) at most 2 rows name the same one
Outputs:
- layer_output: float32 [4096, 2048], P(('dp', 'tensor'))
- cache_pages: bfloat16 [16, 16, 2, 16, 4096], P('dp', None, None, None, 'tensor')
Inputs may be any that keep to these rules, and one draw needn't show every extreme that they name: `segments`: in each group's row the numbers never fall, every number below 8 occurs, no prompt has more than 128 tokens, and one has exactly 128. `page_targets`: among the 16 pages of one request group no target is named more than 2 times, a bound that some block reaches.
All inputs are finite; a program needn't handle non-finite values.
Results may differ from a plain program's by a relative error of at most 0.011.
Values may be sent and summed in bfloat16 or wider, within the bound.
A program may use at most 64 MiB of HBM per device.

v0:
```python
import math

import jax
import jax.numpy as jnp
from jax import lax
from jax.sharding import PartitionSpec as P

H = 8
HD = 256
ROT = 64
PAGE = 16


epsilon = 1e-05
rotary_base = 10000.0
key_block = 256


def swapped(block, axis, apart):
    count = lax.axis_size(axis)
    route = []
    for low in range(count):
        high = low | 1 << apart
        if high != low and high < count:
            route += [(low, high), (high, low)]
    return lax.ppermute(block, axis, route)


def layer_norm(values, gain):
    floats = values.astype(jnp.float32)
    center = jnp.mean(floats, axis=-1, keepdims=True)
    shifted = floats - center
    spread = jnp.mean(shifted * shifted, axis=-1, keepdims=True)
    return (shifted * lax.rsqrt(spread + epsilon) * gain).astype(jnp.bfloat16)


def positions_of(stream):
    indices = jnp.arange(stream.shape[0], dtype=jnp.int32)
    boundary = jnp.concatenate([jnp.ones((1,), dtype=bool), stream[1:] != stream[:-1]])
    starting = lax.cummax(jnp.where(boundary, indices, jnp.zeros_like(indices)), axis=0)
    return (indices, starting)


def rotate_heads(vectors, offsets, rotary_dims):
    half_dims = rotary_dims // 2
    frequency = jnp.exp(
        jnp.arange(half_dims, dtype=jnp.float32) * (-2.0 * math.log(rotary_base) / rotary_dims)
    )
    angles = offsets.astype(jnp.float32)[:, None] * frequency[None, :]
    cosine = jnp.cos(angles)
    sine = jnp.sin(angles)
    floats = vectors.astype(jnp.float32)
    leading = floats[..., :half_dims]
    trailing = floats[..., half_dims:rotary_dims]
    rotated = jnp.concatenate(
        [
            leading * cosine - trailing * sine,
            trailing * cosine + leading * sine,
            floats[..., rotary_dims:],
        ],
        axis=-1,
    )
    return rotated.astype(jnp.bfloat16)


def shards(
    hidden_states,
    attention_gain,
    feedforward_gain,
    heads_weight,
    output_weight,
    upward_weight,
    downward_weight,
    segments,
    page_targets,
):
    tensor_count = lax.axis_size("tensor")
    replica_count = lax.axis_size("dp")
    tensor_index = lax.axis_index("tensor")
    quarters = tensor_count // H
    quarter_width = HD // quarters
    quarter_index = tensor_index % quarters
    stream = segments[0]
    tokens_total = stream.shape[0]
    level_count = quarters.bit_length() - 1
    normed_attention = layer_norm(hidden_states, attention_gain)
    normed_feedforward = layer_norm(hidden_states, feedforward_gain)
    shard_rows = lax.all_gather(
        (normed_attention, normed_feedforward), "tensor", axis=0, tiled=True
    )
    joined_rows = jnp.dot(shard_rows[0], heads_weight, preferred_element_type=jnp.float32).astype(
        jnp.bfloat16
    )
    upward = jnp.dot(shard_rows[1], upward_weight, preferred_element_type=jnp.float32)
    hidden_rows = jax.nn.gelu(upward, approximate=False).astype(jnp.bfloat16)
    hidden = hidden_rows
    pieces = (
        joined_rows.reshape(tokens_total, 3, quarter_width)
        .transpose(1, 0, 2)
        .reshape(1, 3, tokens_total * quarter_width)
    )
    for bit_number in range(level_count):
        partner = swapped(pieces, "tensor", bit_number)
        lower = tensor_index >> bit_number & 1 == 0
        pieces = jnp.where(
            lower, jnp.concatenate([pieces, partner], 0), jnp.concatenate([partner, pieces], 0)
        )
    whole_head = (
        pieces.reshape(quarters, 3, tokens_total, quarter_width)
        .transpose(1, 2, 0, 3)
        .reshape(3, tokens_total, HD)
    )
    indices, starting = positions_of(stream)
    offsets = indices - starting
    queries = rotate_heads(whole_head[0], offsets, ROT)
    keys = rotate_heads(whole_head[1], offsets, ROT)
    values = whole_head[2]
    block_rows = tokens_total // (2 * quarters)
    score_scale = HD ** (-0.5)

    def attend_block(block_number):
        first_row = block_number * block_rows
        block_queries = lax.dynamic_slice_in_dim(queries, first_row, block_rows, 0)
        query_segments = lax.dynamic_slice_in_dim(stream, first_row, block_rows, 0)
        query_indices = first_row + jnp.arange(block_rows, dtype=jnp.int32)
        lowest = lax.dynamic_index_in_dim(starting, first_row, 0, keepdims=False) // key_block
        highest = (first_row + block_rows + key_block - 1) // key_block

        def scores_of(key_number):
            key_first = key_number * key_block
            key_indices = key_first + jnp.arange(key_block, dtype=jnp.int32)
            scores = (
                jnp.dot(block_queries, keys.T, preferred_element_type=jnp.float32) * score_scale
            )
            allowed = (stream[None, :] == query_segments[:, None]) & (
                key_indices[None, :] <= query_indices[:, None]
            )
            return (scores, allowed)

        def find_peak(key_number, peak):
            scores, allowed = scores_of(key_number)
            return jnp.maximum(peak, jnp.max(jnp.where(allowed, scores, -jnp.inf), axis=1))

        peak = lax.fori_loop(
            lowest, highest, find_peak, jnp.full((block_rows,), -jnp.inf, jnp.float32)
        )

        def accumulate(key_number, state):
            weight_sum, mixed_sum = state
            scores, allowed = scores_of(key_number)
            weights = jnp.where(allowed, jnp.exp(scores - peak[:, None]), 0.0)
            mixed_next = mixed_sum + jnp.dot(
                weights.astype(jnp.bfloat16), values, preferred_element_type=jnp.float32
            )
            return (weight_sum + jnp.sum(weights, axis=1), mixed_next)

        start_state = (
            jnp.zeros((block_rows,), jnp.float32),
            jnp.zeros((block_rows, HD), jnp.float32),
        )
        weight_sum, mixed_sum = lax.fori_loop(lowest, highest, accumulate, start_state)
        return (mixed_sum / weight_sum[:, None]).astype(jnp.bfloat16)

    own_blocks = (2 * quarter_index, 2 * quarter_index + 1)
    own_rows = jnp.concatenate([attend_block(own_blocks[0]), attend_block(own_blocks[1])], 0)[None]
    for bit_number in range(level_count):
        partner = swapped(own_rows, "tensor", bit_number)
        lower = tensor_index >> bit_number & 1 == 0
        own_rows = jnp.where(
            lower, jnp.concatenate([own_rows, partner], 0), jnp.concatenate([partner, own_rows], 0)
        )
    attended = own_rows.reshape(tokens_total, HD)
    attended_quarter = lax.dynamic_slice_in_dim(
        attended, quarter_index * quarter_width, quarter_width, 1
    )
    hidden_rows = hidden
    summed = lax.psum_scatter(
        (
            jnp.dot(attended_quarter, output_weight, preferred_element_type=jnp.float32)
            + jnp.dot(hidden_rows, downward_weight, preferred_element_type=jnp.float32)
        ).astype(jnp.bfloat16),
        "tensor",
        scatter_dimension=0,
        tiled=True,
    ).astype(jnp.float32)
    layer_output = hidden_states.astype(jnp.float32) + summed
    key_quarter = lax.dynamic_slice_in_dim(keys, quarter_index * quarter_width, quarter_width, 1)
    value_quarter = joined_rows[:, 2 * quarter_width :]
    page_count = tokens_total // PAGE
    page_rows = jnp.concatenate([key_quarter, value_quarter], 1).reshape(
        page_count, PAGE * 2 * quarter_width
    )
    targets = page_targets[:, 0]
    page_numbers = jnp.arange(page_count, dtype=jnp.int32)
    earlier = jnp.sum(
        (
            (targets[None, :] == targets[:, None]) & (page_numbers[None, :] < page_numbers[:, None])
        ).astype(jnp.int32),
        axis=1,
    )
    capacity = 2 * page_count // replica_count
    slot_numbers = targets * capacity + earlier
    placing = (
        jnp.arange(replica_count * capacity, dtype=jnp.int32)[:, None] == slot_numbers[None, :]
    ).astype(jnp.bfloat16)
    outgoing = jnp.dot(placing, page_rows, preferred_element_type=jnp.float32).astype(jnp.bfloat16)
    outgoing = outgoing.reshape(replica_count, capacity, PAGE * 2 * quarter_width)
    incoming = lax.all_to_all(outgoing, "dp", split_axis=0, concat_axis=0, tiled=True)
    cache_pages = incoming.reshape(1, replica_count, capacity, PAGE, 2 * quarter_width)
    return (layer_output, cache_pages)


def solution(mesh):
    in_specs = (
        P(("dp", "tensor"), None),
        P(),
        P(),
        P(None, "tensor"),
        P("tensor", None),
        P(None, "tensor"),
        P("tensor", None),
        P("dp", None),
        P("dp", None),
    )
    out_specs = (P(("dp", "tensor"), None), P("dp", None, None, None, "tensor"))
    return jax.shard_map(shards, mesh=mesh, in_specs=in_specs, out_specs=out_specs, check_vma=False)
```

profile of v0, /device:TPU:1, one launch (start us, length us, event | category | flops | bytes accessed | tf_op | source)
XLA Modules:
  0.0 285.2 jit_solution(10149111964489272222)
XLA Ops:
  7.2 1.0 convert_reduce_fusion
  8.2 1.0 fusion.82
  9.2 1.5 fusion.80
  10.7 0.7 all-gather.5.cloned.1.call-update
  11.5 0.8 compare_reduce_fusion
  12.4 0.3 reduce-window.9
  13.1 0.6 fusion.143
  18.5 70.7 %all-gather.3.cloned.1.call-done = bf16[256,2048]{1,0:T(8,128)(2,1)} async-done(((bf16[8,2048]{1,0:T(8,128)(2,1)}), bf16[256,2048]{1,0:T(8,128)(2,1)}) %all-gather.3.cloned.1.call-update) | async-done | bytes 1048592 | tf_op jit(solution)/shard_map/all_gather | solution.py:88
  89.2 1.9 convolution_convert_fusion.1
  91.2 0.2 copy.22
  91.4 0.2 reshape.138
  91.6 2.2 collective-permute-start
  93.8 1.0 collective-permute-done
  94.8 0.2 maximum_select_fusion.2
  95.0 4.0 %collective-permute-start.1 = (bf16[2,3,16384]{2,1,0:T(4,128)(2,1)S(1)}, bf16[2,3,16384]{2,1,0:T(4,128)(2,1)S(1)}, u32[]{:S(2)}, u32[]{:S(2)}) collective-permute-start(bf16[2,3,16384]{2,1,0:T(4,128)(2,1)S(1)} %maximum_select_fusion.2), channel_id=1, source_target_pairs={{0,2},{2,0},{1,3},{3,1},{4,6},{6,4},{5,7},{7,5},{8,10},{10,8},{9,1... | collective-permute-start | bytes 589832 | tf_op jit(solution)/shard_map/ppermute | solution.py:26
  99.0 0.2 concatenate.60
  99.3 27.2 %collective-permute-done.1 = bf16[2,3,16384]{2,1,0:T(4,128)(2,1)S(1)} collective-permute-done((bf16[2,3,16384]{2,1,0:T(4,128)(2,1)S(1)}, bf16[2,3,16384]{2,1,0:T(4,128)(2,1)S(1)}, u32[]{:S(2)}, u32[]{:S(2)}) %collective-permute-start.1) | collective-permute-done | bytes 196640 | tf_op jit(solution)/shard_map/ppermute | solution.py:26
  126.5 0.4 reshape.142
  126.9 0.3 fusion.33
  127.7 0.2 fusion.101
  127.9 0.7 pad_maximum_fusion
  128.6 0.2 fusion.84
  128.8 0.2 fusion.86
  129.3 0.2 while.56
  129.4 0.2 select_reduce_fusion.4
  129.6 0.5 while.57
  129.7 0.2 fusion.163
  129.8 0.2 convolution_add_fusion.5
  130.1 0.2 while.58
  130.1 0.2 select_reduce_fusion.5
  130.4 0.5 while.59
  130.4 0.2 fusion.166
  130.6 0.2 convolution_add_fusion.6
  130.9 2.3 collective-permute-start.2
  133.2 0.8 collective-permute-done.2
  134.1 0.6 maximum_select_fusion.4
  134.7 2.0 collective-permute-start.3
  136.7 29.7 %all-gather.5.cloned.1.call-done = bf16[256,2048]{1,0:T(8,128)(2,1)} async-done(((bf16[8,2048]{1,0:T(8,128)(2,1)}), bf16[256,2048]{1,0:T(8,128)(2,1)}) %all-gather.5.cloned.1.call-update) | async-done | bytes 1048592 | tf_op jit(solution)/shard_map/all_gather | solution.py:88
  166.5 3.3 %fusion.44 = f32[256,2048]{1,0:T(8,128)S(1)} fusion(bf16[256,2048]{1,0:T(8,128)(2,1)S(1)} %copy-done, bf16[256,2048]{1,0:T(8,128)(2,1)} %all-gather.5.cloned.1.call-done, bf16[2048,256]{1,0:T(8,128)(2,1)} %param.22), kind=kOutput, calls=%fused_computation.67 | convolution fusion | flops 541130752 | bytes 5242880 | tf_op jit(solution)/shard_map/dot_general | solution.py:180
  169.8 1.0 maximum_select_fusion.3
  170.8 1.5 fusion.32
  172.3 0.2 convert_reduce_fusion.1
  172.5 0.8 constant_dynamic-slice_fusion
  173.5 0.2 convolution_convert_fusion
  173.7 12.1 %all_to_all.5 = bf16[16,2,2048]{2,1,0:T(2,128)(2,1)S(1)} all-to-all(bf16[16,2,2048]{2,1,0:T(2,128)(2,1)S(1)} %reshape.140), channel_id=1, replica_groups=mesh['dp'=16,'tensor'=32] {'dp'}, dimensions={0} | all-to-all | bytes 262144 | tf_op jit(solution)/shard_map/all_to_all | solution.py:208
  185.9 0.7 reshape.141
  186.6 90.7 %reduce-scatter.2.cloned.1.call-done = bf16[8,2048]{1,0:T(8,128)(2,1)} async-done(((bf16[256,2048]{1,0:T(8,128)(2,1)}), bf16[8,2048]{1,0:T(8,128)(2,1)}) %reduce-scatter.2.cloned.1.call-update) | async-done | bytes 32784 | tf_op jit(solution)/shard_map/reduce_scatter | solution.py:177
  277.3 1.4 convert_add_fusion
  (62 shorter events, 2.0 us)
Async XLA Ops:
  7.2 159.3 %copy-start = (bf16[256,2048]{1,0:T(8,128)(2,1)S(1)}, bf16[256,2048]{1,0:T(8,128)(2,1)}, u32[]{:S(2)}) copy-start(bf16[256,2048]{1,0:T(8,128)(2,1)} %param.23) | copy-start | bytes 3145732
  7.2 86.5 %copy-start.1 = (s32[1,256]{1,0:T(1,128)S(1)}, s32[1,256]{1,0:T(1,128)}, u32[]{:S(2)}) copy-start(s32[1,256]{1,0:T(1,128)} %param.24) | copy-start | bytes 3076
  7.2 82.1 %all-gather.3.cloned.1.call-start = ((), (), s32[]{:S(2)}) async-start(), calls=%async_computation.2 | async-start | bytes 1081344 | tf_op jit(solution)/shard_map/all_gather | solution.py:88
  10.7 155.8 %all-gather.5.cloned.1.call-start = ((), (), s32[]{:S(2)}) async-start(), calls=%async_computation.3 | async-start | bytes 1081344 | tf_op jit(solution)/shard_map/all_gather | solution.py:88
  11.4 265.8 %reduce-scatter.2.cloned.1.call-start = ((), (), s32[]{:S(2)}) async-start(), calls=%async_computation.4 | async-start | bytes 1081344 | tf_op jit(solution)/shard_map/reduce_scatter | solution.py:177
  91.6 3.2 %collective-permute-start = (bf16[1,3,16384]{2,1,0:T(4,128)(2,1)S(1)}, bf16[1,3,16384]{2,1,0:T(4,128)(2,1)S(1)}, u32[]{:S(2)}, u32[]{:S(2)}) collective-permute-start(bf16[1,3,16384]{2,1,0:T(4,128)(2,1)S(1)} %reshape.138), channel_id=1, source_target_pairs={{0,1},{1,0},{2,3},{3,2},{4,5},{5,4},{6,7},{7,6},{8,9},{9,8},{10,11... | collective-permute-start | bytes 294920 | tf_op jit(solution)/shard_map/ppermute | solution.py:26
  95.0 31.5 %collective-permute-start.1 = (bf16[2,3,16384]{2,1,0:T(4,128)(2,1)S(1)}, bf16[2,3,16384]{2,1,0:T(4,128)(2,1)S(1)}, u32[]{:S(2)}, u32[]{:S(2)}) collective-permute-start(bf16[2,3,16384]{2,1,0:T(4,128)(2,1)S(1)} %maximum_select_fusion.2), channel_id=1, source_target_pairs={{0,2},{2,0},{1,3},{3,1},{4,6},{6,4},{5,7},{7,5},{8,10},{10,8},{9,1... | collective-permute-start | bytes 589832 | tf_op jit(solution)/shard_map/ppermute | solution.py:26
  130.9 3.1 %collective-permute-start.2 = (bf16[1,64,256]{2,1,0:T(8,128)(2,1)S(1)}, bf16[1,64,256]{2,1,0:T(8,128)(2,1)S(1)}, u32[]{:S(2)}, u32[]{:S(2)}) collective-permute-start(bf16[1,64,256]{2,1,0:T(8,128)(2,1)S(1)} %maximum_bitcast_fusion), channel_id=1, source_target_pairs={{0,1},{1,0},{2,3},{3,2},{4,5},{5,4},{6,7},{7,6},{8,9},{9,8},{10,11... | collective-permute-start | bytes 98312 | tf_op jit(solution)/shard_map/ppermute | solution.py:26
  134.7 36.1 %copy-start.3 = (bf16[64,2048]{1,0:T(8,128)(2,1)S(1)}, bf16[64,2048]{1,0:T(8,128)(2,1)}, u32[]{:S(2)}) copy-start(bf16[64,2048]{1,0:T(8,128)(2,1)} %param.21) | copy-start | bytes 786436
  134.7 35.1 %collective-permute-start.3 = (bf16[2,64,256]{2,1,0:T(8,128)(2,1)}, bf16[2,64,256]{2,1,0:T(8,128)(2,1)}, u32[]{:S(2)}, u32[]{:S(2)}) collective-permute-start(bf16[2,64,256]{2,1,0:T(8,128)(2,1)} %maximum_select_fusion.4), channel_id=1, source_target_pairs={{0,2},{2,0},{1,3},{3,1},{4,6},{6,4},{5,7},{7,5},{8,10},{10,8},{9,1... | collective-permute-start | bytes 196616 | tf_op jit(solution)/shard_map/ppermute | solution.py:26
  170.8 1.5 copy-start.4
  172.3 105.0 %copy-start.2 = (bf16[8,2048]{1,0:T(8,128)(2,1)S(1)}, bf16[8,2048]{1,0:T(8,128)(2,1)}, u32[]{:S(2)}) copy-start(bf16[8,2048]{1,0:T(8,128)(2,1)} %param.17) | copy-start | bytes 98308
Sparse Core Ops, SparseCore 0:
  11.7 77.4 all-gather.2
  92.4 74.0 all-gather.4
  172.4 104.7 reduce-scatter.1
where the time goes:
time: 287 us; the launch traced here: 285 us
  waiting for transfers between devices  221 us (77%)
  between operations  19 us (7%)
  blocking collectives  12.1 us (4%)
  starting transfers between devices  10.6 us (4%)
  other arithmetic  10.5 us (4%)
  matrix products  7.82 us (3%)
  local copies, waits for them, and re-layouts  4.15 us (1%)
    all_gather x2, waiting for transfers between devices, shards(): lax.all_gather((normed_attention, normed_feedforward), 'tensor', axis=0,...  100 us
    reduce_scatter x1, waiting for transfers between devices, shards(): lax.psum_scatter((jnp.dot(attended_quarter, output_weight, preferred_elem...  90.7 us
    ppermute x4, waiting for transfers between devices, swapped(): return lax.ppermute(block, axis, route)  29 us
    all_to_all x1, blocking collectives, shards(): lax.all_to_all(outgoing, 'dp', split_axis=0, concat_axis=0, tiled=True)  12.1 us
    ppermute x4, starting transfers between devices, swapped(): return lax.ppermute(block, axis, route)  10.5 us
  transfers between devices with their start and end apart: 7, of which 6 were waited for; matrix products, arithmetic and copies ran while one was open for 5% of the time, Pallas kernels for 0%

commit v1 on v0

v1 whole, which is shorter than its diff:
```python
import functools
import math

import jax
import jax.numpy as jnp
from jax import lax
from jax.experimental import pallas as pl
from jax.experimental.pallas import tpu as pltpu
from jax.sharding import PartitionSpec as P

H = 8
HD = 256
ROT = 64
PAGE = 16


epsilon = 1e-05
rotary_base = 10000.0


def layer_norm(values, gain):
    floats = values.astype(jnp.float32)
    center = jnp.mean(floats, axis=-1, keepdims=True)
    shifted = floats - center
    spread = jnp.mean(shifted * shifted, axis=-1, keepdims=True)
    return (shifted * lax.rsqrt(spread + epsilon) * gain).astype(jnp.bfloat16)


def positions_of(stream):
    indices = jnp.arange(stream.shape[0], dtype=jnp.int32)
    boundary = jnp.concatenate([jnp.ones((1,), dtype=bool), stream[1:] != stream[:-1]])
    starting = lax.cummax(jnp.where(boundary, indices, jnp.zeros_like(indices)), axis=0)
    return (indices, starting)


def rotate_leading(vectors, offsets, rotary_dims):
    half_dims = rotary_dims // 2
    frequency = jnp.exp(
        jnp.arange(half_dims, dtype=jnp.float32) * (-2.0 * math.log(rotary_base) / rotary_dims)
    )
    angles = offsets.astype(jnp.float32)[:, None] * frequency[None, :]
    cosine = jnp.cos(angles)
    sine = jnp.sin(angles)
    floats = vectors.astype(jnp.float32)
    leading = floats[..., :half_dims]
    trailing = floats[..., half_dims:rotary_dims]
    rotated = jnp.concatenate(
        [
            leading * cosine - trailing * sine,
            trailing * cosine + leading * sine,
            floats[..., rotary_dims:],
        ],
        axis=-1,
    )
    return rotated.astype(jnp.bfloat16)


def _exchange_kernel(axis, n, shared, src_ref, out_ref, local_sem, send_sem, recv_sem):
    index = lax.axis_index(axis)
    pos = index % n
    base = index - pos
    mesh_ids = pl.DeviceIdType.MESH

    def source(q):
        return src_ref.at[0] if shared else src_ref.at[q]

    def peer_copy(q, slot):
        return pltpu.make_async_remote_copy(
            src_ref=source(q),
            dst_ref=out_ref.at[slot],
            send_sem=send_sem.at[q],
            recv_sem=recv_sem.at[slot],
            device_id={axis: base + q},
            device_id_type=mesh_ids,
        )

    barrier = pltpu.get_barrier_semaphore()

    def greet(k, carry):
        q = (pos + k) % n
        pl.semaphore_signal(barrier, inc=1, device_id={axis: base + q}, device_id_type=mesh_ids)
        return carry

    lax.fori_loop(1, n, greet, 0)
    pl.semaphore_wait(barrier, n - 1)

    local = pltpu.make_async_copy(source(pos), out_ref.at[pos], local_sem)
    local.start()

    def send(k, carry):
        q = (pos + k) % n
        peer_copy(q, pos).start()
        return carry

    lax.fori_loop(1, n, send, 0)

    def finish(k, carry):
        q = (pos + k) % n
        peer_copy(q, pos).wait_send()
        peer_copy(q, q).wait_recv()
        return carry

    lax.fori_loop(1, n, finish, 0)
    local.wait()


def exchange(blocks, axis, n, shared, collective_id):
    block_shape = blocks.shape[1:]
    return pl.pallas_call(
        functools.partial(_exchange_kernel, axis, n, shared),
        out_shape=jax.ShapeDtypeStruct((n,) + block_shape, blocks.dtype),
        in_specs=[pl.BlockSpec(memory_space=pltpu.VMEM)],
        out_specs=pl.BlockSpec(memory_space=pltpu.VMEM),
        scratch_shapes=[
            pltpu.SemaphoreType.DMA,
            pltpu.SemaphoreType.DMA((n,)),
            pltpu.SemaphoreType.DMA((n,)),
        ],
        compiler_params=pltpu.CompilerParams(collective_id=collective_id, has_side_effects=True),
    )(blocks)


def shards(
    hidden_states,
    attention_gain,
    feedforward_gain,
    heads_weight,
    output_weight,
    upward_weight,
    downward_weight,
    segments,
    page_targets,
):
    tensor_count = lax.axis_size("tensor")
    replica_count = lax.axis_size("dp")
    tensor_index = lax.axis_index("tensor")
    quarters = tensor_count // H
    quarter_width = HD // quarters
    quarter_index = tensor_index % quarters
    stream = segments[0]
    tokens_total = stream.shape[0]
    local_rows = hidden_states.shape[0]

    gathered = exchange(hidden_states[None], "tensor", tensor_count, True, 0)
    tokens = gathered.reshape(tokens_total, hidden_states.shape[1])
    normed_attention = layer_norm(tokens, attention_gain)
    normed_feedforward = layer_norm(tokens, feedforward_gain)
    joined = jnp.dot(normed_attention, heads_weight, preferred_element_type=jnp.float32).astype(
        jnp.bfloat16
    )
    upward = jnp.dot(normed_feedforward, upward_weight, preferred_element_type=jnp.float32)
    hidden = jax.nn.gelu(upward, approximate=False).astype(jnp.bfloat16)

    indices, starting = positions_of(stream)
    offsets = indices - starting
    query_piece = joined[:, :quarter_width]
    key_piece = joined[:, quarter_width : 2 * quarter_width]
    value_piece = joined[:, 2 * quarter_width :]
    leading = quarter_index == 0
    query_piece = jnp.where(leading, rotate_leading(query_piece, offsets, ROT), query_piece)
    key_piece = jnp.where(leading, rotate_leading(key_piece, offsets, ROT), key_piece)

    head_pieces = exchange(
        jnp.concatenate([query_piece, key_piece], 1)[None], "tensor", quarters, True, 1
    )
    queries = head_pieces[:, :, :quarter_width].transpose(1, 0, 2).reshape(tokens_total, HD)
    keys = head_pieces[:, :, quarter_width:].transpose(1, 0, 2).reshape(tokens_total, HD)

    scores = jnp.dot(queries, keys.T, preferred_element_type=jnp.float32) * HD ** (-0.5)
    allowed = (stream[None, :] == stream[:, None]) & (indices[None, :] <= indices[:, None])
    peak = jnp.max(jnp.where(allowed, scores, -jnp.inf), axis=1, keepdims=True)
    weights = jnp.where(allowed, jnp.exp(scores - peak), 0.0)
    weight_sum = jnp.sum(weights, axis=1, keepdims=True)
    mixed = jnp.dot(weights.astype(jnp.bfloat16), value_piece, preferred_element_type=jnp.float32)
    attended = (mixed / weight_sum).astype(jnp.bfloat16)

    partial = (
        jnp.dot(attended, output_weight, preferred_element_type=jnp.float32)
        + jnp.dot(hidden, downward_weight, preferred_element_type=jnp.float32)
    ).astype(jnp.bfloat16)
    arriving = exchange(
        partial.reshape(tensor_count, local_rows, partial.shape[1]), "tensor", tensor_count, False, 2
    )
    layer_output = hidden_states.astype(jnp.float32) + jnp.sum(
        arriving.astype(jnp.float32), axis=0
    )

    page_count = tokens_total // PAGE
    page_rows = jnp.concatenate([key_piece, value_piece], 1).reshape(
        page_count, PAGE * 2 * quarter_width
    )
    targets = page_targets[:, 0]
    page_numbers = jnp.arange(page_count, dtype=jnp.int32)
    earlier = jnp.sum(
        (
            (targets[None, :] == targets[:, None]) & (page_numbers[None, :] < page_numbers[:, None])
        ).astype(jnp.int32),
        axis=1,
    )
    capacity = 2 * page_count // replica_count
    slot_numbers = targets * capacity + earlier
    placing = (
        jnp.arange(replica_count * capacity, dtype=jnp.int32)[:, None] == slot_numbers[None, :]
    ).astype(jnp.bfloat16)
    outgoing = jnp.dot(placing, page_rows, preferred_element_type=jnp.float32).astype(jnp.bfloat16)
    outgoing = outgoing.reshape(replica_count, capacity * PAGE, 2 * quarter_width)
    incoming = exchange(outgoing, "dp", replica_count, False, 3)
    cache_pages = incoming.reshape(1, replica_count, capacity, PAGE, 2 * quarter_width)
    return (layer_output, cache_pages)


def solution(mesh):
    in_specs = (
        P(("dp", "tensor"), None),
        P(),
        P(),
        P(None, "tensor"),
        P("tensor", None),
        P(None, "tensor"),
        P("tensor", None),
        P("dp", None),
        P("dp", None),
    )
    out_specs = (P(("dp", "tensor"), None), P("dp", None, None, None, "tensor"))
    return jax.shard_map(shards, mesh=mesh, in_specs=in_specs, out_specs=out_specs, check_vma=False)
```

time: 287 us -> 170 us (0.59)
  waiting for transfers between devices: 221 us -> 0 us
  Pallas kernels: 0 us -> 147 us
  between operations: 19 us -> 0.81 us
  blocking collectives: 12.1 us -> 0 us
  starting transfers between devices: 10.6 us -> 0 us
    pallas_call x0 -> x4, Pallas kernels: none -> 147 us  [exchange(): pl.pallas_call(functools.partial(_exchange_kernel, axis, n, shared), out_...]
    all_gather x2 -> x0, waiting for transfers between devices: 100 us -> none  [shards(): lax.all_gather((normed_attention, normed_feedforward), 'tensor', axis=0,...]
    reduce_scatter x1 -> x0, waiting for transfers between devices: 90.7 us -> none  [shards(): lax.psum_scatter((jnp.dot(attended_quarter, output_weight, preferred_elem...]
    ppermute x4 -> x0, waiting for transfers between devices: 29 us -> none  [swapped(): return lax.ppermute(block, axis, route)]
    all_to_all x1 -> x0, blocking collectives: 12.1 us -> none  [shards(): lax.all_to_all(outgoing, 'dp', split_axis=0, concat_axis=0, tiled=True)]
    ppermute x4 -> x0, starting transfers between devices: 10.5 us -> none  [swapped(): return lax.ppermute(block, axis, route)]
    dot_general x7 -> x4, matrix products: 7.66 us -> 9.04 us  [the longest x1 3.37 us: shards(): jnp.dot(hidden, downward_weight, preferred_element_type=jnp.float32)]
  transfers between devices with their start and end apart: 7 -> 0, of which waited for: 6 -> 0; matrix products, arithmetic and copies ran while one was open for 5% -> 0% of each run, Pallas kernels for 0% -> 0%
where the time goes in v1:
time: 170 us; the launch traced here: 169 us
  Pallas kernels  147 us (86%)
  other arithmetic  9.31 us (5%)
  matrix products  9.2 us (5%)
  local copies, waits for them, and re-layouts  2.74 us (2%)
    pallas_call x4, Pallas kernels, exchange(): pl.pallas_call(functools.partial(_exchange_kernel, axis, n, shared), out_...  147 us

profile of v1, /device:TPU:1, one launch (start us, length us, event | category | flops | bytes accessed | tf_op | source)
XLA Modules:
  0.0 169.3 jit_solution(15118750442177817285)
XLA Ops:
  0.6 0.0 copy-start
  0.6 0.0 copy-start.6
  0.7 0.0 copy-start.7
  0.7 66.6 %shard_map.104 = bf16[32,8,2048]{2,1,0:T(8,128)(2,1)} custom-call(bf16[1,8,2048]{2,1,0:T(8,128)(2,1)} %bitcast.57), custom_call_target="tpu_custom_call" | custom-call | tf_op jit(solution)/shard_map/pallas_call | solution.py:109
  67.2 0.0 copy-start.1
  67.3 1.5 convert_reduce_fusion
  68.8 1.6 fusion.9
  70.4 0.1 rsqrt.13
  70.5 0.1 div.19
  70.6 0.0 copy-done
  70.6 0.0 copy-done.6
  70.6 0.0 copy-done.7
  70.7 0.0 copy-done.1
  70.7 0.0 copy-start.8
  70.7 3.4 %fusion.39 = f32[256,2048]{1,0:T(8,128)} fusion(bf16[256,2048]{1,0:T(8,128)(2,1)S(1)} %copy-done, bf16[2048,256]{1,0:T(8,128)(2,1)S(1)} %copy-done.6, bf16[32,8,2048]{2,1,0:T(8,128)(2,1)S(1)} %copy-done.1, f32[2048]{0:T(1024)S(1)} %copy-done.7, f32[256]{0:T(256)S(1)} %rsqrt.13, f32[256]{0:T(256)S(1)} %div.19), kind=kOutput, calls=%fused_computation.55 | convolution fusion | flops 543752192 | bytes 5253120 | tf_op jit(solution)/shard_map/dot_general | solution.py:179
  74.1 0.0 copy-start.5
  74.1 0.0 copy-done.8
  74.1 1.7 convolution_convert_fusion.1
  75.7 0.0 copy-start.2
  75.8 0.1 slice_convert_fusion.1
  75.8 0.0 copy-done.5
  75.9 0.1 compare_reduce_fusion
  75.9 0.1 fusion.102
  76.0 0.3 reduce-window.9
  76.3 0.1 slice.46
  76.5 0.1 slice_reduce_fusion
  76.6 0.1 fusion.103
  76.7 1.3 fusion.54
  77.9 1.1 fusion.138
  79.0 0.8 pad_maximum_fusion
  79.8 17.2 %shard_map.105 = bf16[4,256,128]{2,1,0:T(8,128)(2,1)} custom-call(bf16[1,256,128]{2,1,0:T(8,128)(2,1)} %get-tuple-element.12.src_ref), custom_call_target="tpu_custom_call" | custom-call | tf_op jit(solution)/shard_map/pallas_call | solution.py:109
  96.9 1.3 select_reduce_fusion
  98.3 0.1 fusion.49
  98.4 0.0 copy-done.2
  98.4 2.7 %fusion.1.src_ref = bf16[32,8,2048]{2,1,0:T(8,128)(2,1)} fusion(f32[256,2048]{1,0:T(8,128)S(1)} %copy-done.2, bf16[64,2048]{1,0:T(8,128)(2,1)} %param.13, f32[256,256]{0,1:T(8,128)S(1)} %get-tuple-element.16, f32[256]{0:T(256)S(1)} %get-tuple-element.15, s32[256]{0:T(256)S(1)} %bitcast.60, f32[256]{0:T(256)S(1)} %fusion.49, ...), kind=kOutput, calls=%fused_computation.5 | convolution fusion | flops 76972032 | bytes 3739648 | tf_op jit(solution)/shard_map/dot_general | solution.py:178
  101.1 0.0 copy-start.4
  101.1 0.0 copy-start.3
  101.1 50.6 %shard_map.106 = bf16[32,8,2048]{2,1,0:T(8,128)(2,1)} custom-call(bf16[32,8,2048]{2,1,0:T(8,128)(2,1)} %fusion.1.src_ref), custom_call_target="tpu_custom_call" | custom-call | tf_op jit(solution)/shard_map/pallas_call | solution.py:109
  151.7 1.4 convert_reduce_fusion.1
  153.1 0.0 copy-done.4
  153.1 0.6 convert_add_fusion
  153.7 0.0 copy-done.3
  153.8 0.0 copy-done.9
  153.8 0.2 convert_reduce_fusion.2
  154.0 0.2 convolution_convert_fusion
  154.1 0.7 reshape.107.src_ref
  154.9 12.8 %shard_map.107 = bf16[16,32,128]{2,1,0:T(8,128)(2,1)} custom-call(bf16[16,32,128]{2,1,0:T(8,128)(2,1)} %reshape.107.src_ref), custom_call_target="tpu_custom_call" | custom-call | tf_op jit(solution)/shard_map/pallas_call | solution.py:109
  167.7 1.6 copy.37
  (7 shorter events, 0.1 us)
Async XLA Ops:
  0.6 70.0 %copy-start = (bf16[256,2048]{1,0:T(8,128)(2,1)S(1)}, bf16[256,2048]{1,0:T(8,128)(2,1)}, u32[]{:S(2)}) copy-start(bf16[256,2048]{1,0:T(8,128)(2,1)} %param.15) | copy-start | bytes 3145732
  0.6 70.0 %copy-start.6 = (bf16[2048,256]{1,0:T(8,128)(2,1)S(1)}, bf16[2048,256]{1,0:T(8,128)(2,1)}, u32[]{:S(2)}) copy-start(bf16[2048,256]{1,0:T(8,128)(2,1)} %param.14) | copy-start | bytes 3145732
  0.7 70.0 %copy-start.7 = (f32[2048]{0:T(1024)S(1)}, f32[2048]{0:T(1024)}, u32[]{:S(2)}) copy-start(f32[2048]{0:T(1024)} %param.11) | copy-start | bytes 24580
  67.2 3.4 %copy-start.1 = (bf16[32,8,2048]{2,1,0:T(8,128)(2,1)S(1)}, bf16[32,8,2048]{2,1,0:T(8,128)(2,1)}, u32[]{:S(2)}) copy-start(bf16[32,8,2048]{2,1,0:T(8,128)(2,1)} %shard_map.104) | copy-start | bytes 3145732
  70.7 3.4 %copy-start.8 = (f32[2048]{0:T(1024)S(1)}, f32[2048]{0:T(1024)}, u32[]{:S(2)}) copy-start(f32[2048]{0:T(1024)} %param.10) | copy-start | bytes 24580
  74.1 1.8 %copy-start.5 = (s32[1,256]{1,0:T(1,128)S(1)}, s32[1,256]{1,0:T(1,128)}, u32[]{:S(2)}) copy-start(s32[1,256]{1,0:T(1,128)} %param.16) | copy-start | bytes 3076
  75.7 22.7 %copy-start.2 = (f32[256,2048]{1,0:T(8,128)S(1)}, f32[256,2048]{1,0:T(8,128)}, u32[]{:S(2)}) copy-start(f32[256,2048]{1,0:T(8,128)} %fusion.39) | copy-start | bytes 6291460
  101.1 52.0 %copy-start.4 = (bf16[8,2048]{1,0:T(8,128)(2,1)S(1)}, bf16[8,2048]{1,0:T(8,128)(2,1)}, u32[]{:S(2)}) copy-start(bf16[8,2048]{1,0:T(8,128)(2,1)} %param.9) | copy-start | bytes 98308
  101.1 52.7 %copy-start.3 = (bf16[256,128]{1,0:T(8,128)(2,1)S(1)}, bf16[256,128]{1,0:T(8,128)(2,1)}, u32[]{:S(2)}) copy-start(bf16[256,128]{1,0:T(8,128)(2,1)} %get-tuple-element.11) | copy-start | bytes 196612
  101.1 52.7 %copy-start.9 = (s32[16,1]{0,1:T(1,128)S(1)}, s32[16,1]{0,1:T(1,128)}, u32[]{:S(2)}) copy-start(s32[16,1]{0,1:T(1,128)} %param.17) | copy-start | bytes 196

commit v2 on v1

--- a/solution.py
+++ b/solution.py
@@ -55,10 +55,9 @@
     return rotated.astype(jnp.bfloat16)
 
 
-def _exchange_kernel(axis, n, shared, src_ref, out_ref, local_sem, send_sem, recv_sem):
+def _exchange_kernel(axis, n, shared, position, member, src_ref, out_ref, local_sem, send_sem, recv_sem):
     index = lax.axis_index(axis)
-    pos = index % n
-    base = index - pos
+    pos = position(index)
     mesh_ids = pl.DeviceIdType.MESH
 
     def source(q):
@@ -70,7 +69,7 @@
             dst_ref=out_ref.at[slot],
             send_sem=send_sem.at[q],
             recv_sem=recv_sem.at[slot],
-            device_id={axis: base + q},
+            device_id={axis: member(index, q)},
             device_id_type=mesh_ids,
         )
 
@@ -78,7 +77,9 @@
 
     def greet(k, carry):
         q = (pos + k) % n
-        pl.semaphore_signal(barrier, inc=1, device_id={axis: base + q}, device_id_type=mesh_ids)
+        pl.semaphore_signal(
+            barrier, inc=1, device_id={axis: member(index, q)}, device_id_type=mesh_ids
+        )
         return carry
 
     lax.fori_loop(1, n, greet, 0)
@@ -104,10 +105,31 @@
     local.wait()
 
 
-def exchange(blocks, axis, n, shared, collective_id):
+def contiguous(n):
+    return (lambda index: index % n, lambda index, q: index - index % n + q)
+
+
+def plane_group(index):
+    return (index // 8) * 2 + index % 2
+
+
+def plane_member(index, q):
+    return ((q // 2) * 4 + (index // 2) % 4) * 2 + q % 2
+
+
+def column_group(index):
+    return (index // 2) % 4
+
+
+def column_member(index, q):
+    return ((index // 8) * 4 + q) * 2 + index % 2
+
+
+def exchange(blocks, axis, n, shared, collective_id, group=None):
+    position, member = group if group is not None else contiguous(n)
     block_shape = blocks.shape[1:]
     return pl.pallas_call(
-        functools.partial(_exchange_kernel, axis, n, shared),
+        functools.partial(_exchange_kernel, axis, n, shared, position, member),
         out_shape=jax.ShapeDtypeStruct((n,) + block_shape, blocks.dtype),
         in_specs=[pl.BlockSpec(memory_space=pltpu.VMEM)],
         out_specs=pl.BlockSpec(memory_space=pltpu.VMEM),
@@ -141,8 +163,15 @@
     tokens_total = stream.shape[0]
     local_rows = hidden_states.shape[0]
 
-    gathered = exchange(hidden_states[None], "tensor", tensor_count, True, 0)
-    tokens = gathered.reshape(tokens_total, hidden_states.shape[1])
+    width = hidden_states.shape[1]
+    planes = tensor_count // 8
+    by_column = exchange(hidden_states[None], "tensor", planes, True, 0, (column_group, column_member))
+    by_plane = exchange(by_column[None], "tensor", 8, True, 4, (plane_group, plane_member))
+    tokens = (
+        by_plane.reshape(4, 2, planes, local_rows, width)
+        .transpose(0, 2, 1, 3, 4)
+        .reshape(tokens_total, width)
+    )
     normed_attention = layer_norm(tokens, attention_gain)
     normed_feedforward = layer_norm(tokens, feedforward_gain)
     joined = jnp.dot(normed_attention, heads_weight, preferred_element_type=jnp.float32).astype(
@@ -178,12 +207,21 @@
         jnp.dot(attended, output_weight, preferred_element_type=jnp.float32)
         + jnp.dot(hidden, downward_weight, preferred_element_type=jnp.float32)
     ).astype(jnp.bfloat16)
-    arriving = exchange(
-        partial.reshape(tensor_count, local_rows, partial.shape[1]), "tensor", tensor_count, False, 2
-    )
-    layer_output = hidden_states.astype(jnp.float32) + jnp.sum(
-        arriving.astype(jnp.float32), axis=0
-    )
+    outgoing_rows = (
+        partial.reshape(4, planes, 2, local_rows, width)
+        .transpose(0, 2, 1, 3, 4)
+        .reshape(8, planes, local_rows, width)
+    )
+    plane_sums = jnp.sum(
+        exchange(outgoing_rows, "tensor", 8, False, 2, (plane_group, plane_member)).astype(
+            jnp.float32
+        ),
+        axis=0,
+    )
+    column_sums = jnp.sum(
+        exchange(plane_sums, "tensor", planes, False, 5, (column_group, column_member)), axis=0
+    )
+    layer_output = hidden_states.astype(jnp.float32) + column_sums
 
     page_count = tokens_total // PAGE
     page_rows = jnp.concatenate([key_piece, value_piece], 1).reshape(

time: 170 us -> 139 us (0.82)
  Pallas kernels: 147 us -> 114 us
  local copies, waits for them, and re-layouts: 2.74 us -> 5.06 us
    pallas_call x4 -> x6, Pallas kernels: 147 us -> 114 us  [exchange(): pl.pallas_call(functools.partial(_exchange_kernel, axis, n, shared, posit...]
    convert_element_type x0 -> x2, other arithmetic: none -> 1.99 us  [the longest x1 1.46 us: layer_norm(): floats = values.astype(jnp.float32)]
    reduce_sum x1 -> x2, other arithmetic: 1.38 us -> 3.08 us  [the longest x1 2.11 us: shards(): jnp.sum(exchange(outgoing_rows, 'tensor', 8, False, 2, (plane_group, plan...]
where the time goes in v2:
time: 139 us; the launch traced here: 138 us
  Pallas kernels  114 us (82%)
  matrix products  8.81 us (6%)
  other arithmetic  8.78 us (6%)
  local copies, waits for them, and re-layouts  5.06 us (4%)
    pallas_call x6, Pallas kernels, exchange(): pl.pallas_call(functools.partial(_exchange_kernel, axis, n, shared, posit...  114 us
    dot_general x1, matrix products, shards(): jnp.dot(hidden, downward_weight, preferred_element_type=jnp.float32)  4.56 us

profile of v2, /device:TPU:1, one launch (start us, length us, event | category | flops | bytes accessed | tf_op | source)
XLA Modules:
  0.0 138.0 jit_solution(6093111171019702137)
XLA Ops:
  0.6 0.0 copy-start
  0.7 20.5 %shard_map.104 = bf16[4,8,2048]{2,1,0:T(8,128)(2,1)} custom-call(bf16[1,8,2048]{2,1,0:T(8,128)(2,1)} %bitcast.65), custom_call_target="tpu_custom_call" | custom-call | tf_op jit(solution)/shard_map/pallas_call | solution.py:131
  21.2 22.3 %shard_map.105 = bf16[8,4,8,2048]{3,2,1,0:T(8,128)(2,1)} custom-call(bf16[1,4,8,2048]{3,2,1,0:T(8,128)(2,1)} %bitcast.63), custom_call_target="tpu_custom_call" | custom-call | tf_op jit(solution)/shard_map/pallas_call | solution.py:131
  43.5 1.5 %bitcast_convert_fusion = f32[4,2,4,8,2048]{4,3,2,1,0:T(8,128)S(1)} fusion(bf16[8,4,8,2048]{3,2,1,0:T(8,128)(2,1)} %shard_map.105), kind=kLoop, calls=%fused_computation.156 | loop fusion | flops 524288 | bytes 3145728 | tf_op jit(solution)/shard_map/convert_element_type | solution.py:22
  44.9 0.0 copy-start.1
  45.0 0.2 bitcast_reduce_fusion
  45.2 0.4 fusion.3
  45.6 0.1 rsqrt.13
  45.7 0.1 div.19
  45.8 0.4 copy-done.1
  46.2 0.2 copy.31
  46.4 0.0 copy-done.5
  46.4 0.0 copy-done.6
  46.4 0.0 copy-start.7
  46.4 0.5 multiply_convert_fusion.1
  47.0 0.0 copy-start.4
  47.0 0.6 copy-done.7
  47.6 0.5 convolution_convert_fusion.1
  48.0 0.1 slice_convert_fusion.1
  48.1 0.0 copy-done.4
  48.1 0.1 compare_reduce_fusion
  48.2 0.1 fusion.84
  48.3 0.3 reduce-window.9
  48.6 0.1 slice.46
  48.7 0.1 slice_reduce_fusion
  48.8 0.1 fusion.85
  48.9 0.6 fusion.36
  49.5 0.1 fusion.120
  49.7 0.7 pad_maximum_fusion
  50.4 19.9 %shard_map.106 = bf16[4,256,128]{2,1,0:T(8,128)(2,1)} custom-call(bf16[1,256,128]{2,1,0:T(8,128)(2,1)} %get-tuple-element.14.src_ref), custom_call_target="tpu_custom_call" | custom-call | tf_op jit(solution)/shard_map/pallas_call | solution.py:131
  70.4 1.3 select_reduce_fusion
  71.7 0.1 fusion.29
  71.8 0.0 copy-done
  71.8 0.0 copy-start.2
  71.8 4.6 %fusion.31 = f32[256,2048]{1,0:T(8,128)} fusion(bf16[256,2048]{1,0:T(8,128)(2,1)S(1)} %copy-done, bf16[256,2048]{1,0:T(8,128)(2,1)S(1)} %get-tuple-element.3, bf16[2048,256]{1,0:T(8,128)(2,1)} %param.14), kind=kOutput, calls=%fused_computation.56 | convolution fusion | flops 541130752 | bytes 5242880 | tf_op jit(solution)/shard_map/dot_general | solution.py:208
  76.4 0.0 copy-done.2
  76.4 2.3 %fusion = bf16[256,2048]{1,0:T(8,128)(2,1)S(1)} fusion(f32[256,2048]{1,0:T(8,128)} %fusion.31, bf16[64,2048]{1,0:T(8,128)(2,1)S(1)} %copy-done.2, f32[256,256]{0,1:T(8,128)S(1)} %get-tuple-element.18, f32[256]{0:T(256)S(1)} %get-tuple-element.17, s32[256]{0:T(256)S(1)} %bitcast.68, f32[256]{0:T(256)S(1)} %fusion.29, ...), kind=kOutput, calls=%fused_computation.1 | convolution fusion | flops 76972032 | bytes 3739648 | tf_op jit(solution)/shard_map/dot_general | solution.py:207
  78.7 1.1 copy.38
  79.8 18.5 %shard_map.107 = bf16[8,4,8,2048]{3,2,1,0:T(8,128)(2,1)} custom-call(bf16[8,4,8,2048]{3,2,1,0:T(8,128)(2,1)} %bitcast.62), custom_call_target="tpu_custom_call" | custom-call | tf_op jit(solution)/shard_map/pallas_call | solution.py:131
  98.4 2.1 %convert_reduce_fusion.src_ref = f32[4,8,2048]{2,1,0:T(8,128)} fusion(bf16[8,4,8,2048]{3,2,1,0:T(8,128)(2,1)} %shard_map.107), kind=kLoop, calls=%fused_computation.9 | loop fusion | flops 983040 | bytes 1310720 | tf_op jit(solution)/shard_map/reduce_sum | solution.py:215
  100.5 23.0 %shard_map.108 = f32[4,8,2048]{2,1,0:T(8,128)} custom-call(f32[4,8,2048]{2,1,0:T(8,128)} %convert_reduce_fusion.src_ref), custom_call_target="tpu_custom_call" | custom-call | tf_op jit(solution)/shard_map/pallas_call | solution.py:131
  123.5 1.0 reduce_sum.66
  124.5 0.6 convert_add_fusion
  125.2 0.2 convert_reduce_fusion.1
  125.4 0.2 convolution_convert_fusion
  125.5 0.7 reshape.116.src_ref
  126.3 10.2 %shard_map.109 = bf16[16,32,128]{2,1,0:T(8,128)(2,1)} custom-call(bf16[16,32,128]{2,1,0:T(8,128)(2,1)} %reshape.116.src_ref), custom_call_target="tpu_custom_call" | custom-call | tf_op jit(solution)/shard_map/pallas_call | solution.py:131
  136.4 1.6 %copy.46 = bf16[1,16,2,16,128]{4,3,2,1,0:T(8,128)(2,1)} copy(bf16[1,16,2,16,128]{4,3,2,1,0:T(8,128)(2,1)} %bitcast.64) | data formatting | bytes 262144
  (12 shorter events, 0.1 us)
Async XLA Ops:
  0.6 71.2 %copy-start = (bf16[256,2048]{1,0:T(8,128)(2,1)S(1)}, bf16[256,2048]{1,0:T(8,128)(2,1)}, u32[]{:S(2)}) copy-start(bf16[256,2048]{1,0:T(8,128)(2,1)} %param.15) | copy-start | bytes 3145732
  44.9 1.2 copy-start.1
  45.5 0.9 copy-start.5
  45.5 0.9 copy-start.6
  46.4 1.1 copy-start.7
  47.0 1.1 copy-start.4
  71.8 4.6 %copy-start.2 = (bf16[64,2048]{1,0:T(8,128)(2,1)S(1)}, bf16[64,2048]{1,0:T(8,128)(2,1)}, u32[]{:S(2)}) copy-start(bf16[64,2048]{1,0:T(8,128)(2,1)} %param.13) | copy-start | bytes 786436
  79.8 44.7 %copy-start.3 = (bf16[8,2048]{1,0:T(8,128)(2,1)S(1)}, bf16[8,2048]{1,0:T(8,128)(2,1)}, u32[]{:S(2)}) copy-start(bf16[8,2048]{1,0:T(8,128)(2,1)} %param.9) | copy-start | bytes 98308
  79.8 45.4 %copy-start.8 = (s32[16,1]{0,1:T(1,128)S(1)}, s32[16,1]{0,1:T(1,128)}, u32[]{:S(2)}) copy-start(s32[16,1]{0,1:T(1,128)} %param.17) | copy-start | bytes 196

commit v3 on v2

--- a/solution.py
+++ b/solution.py
@@ -55,54 +55,62 @@
     return rotated.astype(jnp.bfloat16)
 
 
-def _exchange_kernel(axis, n, shared, position, member, src_ref, out_ref, local_sem, send_sem, recv_sem):
-    index = lax.axis_index(axis)
-    pos = position(index)
+def _exchange_kernel(plans, *refs):
+    count = len(plans)
+    sources, outs, semaphores = refs[:count], refs[count : 2 * count], refs[2 * count :]
     mesh_ids = pl.DeviceIdType.MESH
-
-    def source(q):
-        return src_ref.at[0] if shared else src_ref.at[q]
-
-    def peer_copy(q, slot):
-        return pltpu.make_async_remote_copy(
-            src_ref=source(q),
-            dst_ref=out_ref.at[slot],
-            send_sem=send_sem.at[q],
-            recv_sem=recv_sem.at[slot],
-            device_id={axis: member(index, q)},
-            device_id_type=mesh_ids,
+    barrier = pltpu.get_barrier_semaphore()
+    steps = []
+    for number, (axis, n, shared, position, member) in enumerate(plans):
+        src_ref, out_ref = sources[number], outs[number]
+        local_sem, send_sem, recv_sem = semaphores[3 * number : 3 * number + 3]
+        index = lax.axis_index(axis)
+        pos = position(index)
+
+        def peer_copy(q, slot, src_ref=src_ref, out_ref=out_ref, send_sem=send_sem,
+                      recv_sem=recv_sem, axis=axis, member=member, index=index, shared=shared):
+            return pltpu.make_async_remote_copy(
+                src_ref=src_ref.at[0] if shared else src_ref.at[q],
+                dst_ref=out_ref.at[slot],
+                send_sem=send_sem.at[q],
+                recv_sem=recv_sem.at[slot],
+                device_id={axis: member(index, q)},
+                device_id_type=mesh_ids,
+            )
+
+        def greet(k, carry, n=n, pos=pos, axis=axis, member=member, index=index):
+            q = (pos + k) % n
+            pl.semaphore_signal(
+                barrier, inc=1, device_id={axis: member(index, q)}, device_id_type=mesh_ids
+            )
+            return carry
+
+        lax.fori_loop(1, n, greet, 0)
+        local = pltpu.make_async_copy(
+            src_ref.at[0] if shared else src_ref.at[pos], out_ref.at[pos], local_sem
         )
-
-    barrier = pltpu.get_barrier_semaphore()
-
-    def greet(k, carry):
-        q = (pos + k) % n
-        pl.semaphore_signal(
-            barrier, inc=1, device_id={axis: member(index, q)}, device_id_type=mesh_ids
-        )
-        return carry
-
-    lax.fori_loop(1, n, greet, 0)
-    pl.semaphore_wait(barrier, n - 1)
-
-    local = pltpu.make_async_copy(source(pos), out_ref.at[pos], local_sem)
-    local.start()
-
-    def send(k, carry):
-        q = (pos + k) % n
-        peer_copy(q, pos).start()
-        return carry
-
-    lax.fori_loop(1, n, send, 0)
-
-    def finish(k, carry):
-        q = (pos + k) % n
-        peer_copy(q, pos).wait_send()
-        peer_copy(q, q).wait_recv()
-        return carry
-
-    lax.fori_loop(1, n, finish, 0)
-    local.wait()
+        steps.append((n, pos, peer_copy, local))
+    pl.semaphore_wait(barrier, sum(plan[1] - 1 for plan in plans))
+
+    for n, pos, peer_copy, local in steps:
+        local.start()
+
+        def send(k, carry, n=n, pos=pos, peer_copy=peer_copy):
+            peer_copy((pos + k) % n, pos).start()
+            return carry
+
+        lax.fori_loop(1, n, send, 0)
+
+    for n, pos, peer_copy, local in steps:
+
+        def finish(k, carry, n=n, pos=pos, peer_copy=peer_copy):
+            q = (pos + k) % n
+            peer_copy(q, pos).wait_send()
+            peer_copy(q, q).wait_recv()
+            return carry
+
+        lax.fori_loop(1, n, finish, 0)
+        local.wait()
 
 
 def contiguous(n):
@@ -125,21 +133,30 @@
     return ((index // 8) * 4 + q) * 2 + index % 2
 
 
-def exchange(blocks, axis, n, shared, collective_id, group=None):
-    position, member = group if group is not None else contiguous(n)
-    block_shape = blocks.shape[1:]
-    return pl.pallas_call(
-        functools.partial(_exchange_kernel, axis, n, shared, position, member),
-        out_shape=jax.ShapeDtypeStruct((n,) + block_shape, blocks.dtype),
-        in_specs=[pl.BlockSpec(memory_space=pltpu.VMEM)],
-        out_specs=pl.BlockSpec(memory_space=pltpu.VMEM),
-        scratch_shapes=[
+def exchange_all(collective_id, *requests):
+    plans, blocks, shapes, scratch = [], [], [], []
+    for data, axis, n, shared, group in requests:
+        position, member = group if group is not None else contiguous(n)
+        plans.append((axis, n, shared, position, member))
+        blocks.append(data)
+        shapes.append(jax.ShapeDtypeStruct((n,) + data.shape[1:], data.dtype))
+        scratch += [
             pltpu.SemaphoreType.DMA,
             pltpu.SemaphoreType.DMA((n,)),
             pltpu.SemaphoreType.DMA((n,)),
-        ],
+        ]
+    return pl.pallas_call(
+        functools.partial(_exchange_kernel, tuple(plans)),
+        out_shape=tuple(shapes),
+        in_specs=[pl.BlockSpec(memory_space=pltpu.VMEM)] * len(blocks),
+        out_specs=tuple(pl.BlockSpec(memory_space=pltpu.VMEM) for _ in blocks),
+        scratch_shapes=scratch,
         compiler_params=pltpu.CompilerParams(collective_id=collective_id, has_side_effects=True),
-    )(blocks)
+    )(*blocks)
+
+
+def exchange(blocks, axis, n, shared, collective_id, group=None):
+    return exchange_all(collective_id, (blocks, axis, n, shared, group))[0]
 
 
 def shards(
@@ -189,8 +206,29 @@
     query_piece = jnp.where(leading, rotate_leading(query_piece, offsets, ROT), query_piece)
     key_piece = jnp.where(leading, rotate_leading(key_piece, offsets, ROT), key_piece)
 
-    head_pieces = exchange(
-        jnp.concatenate([query_piece, key_piece], 1)[None], "tensor", quarters, True, 1
+    page_count = tokens_total // PAGE
+    page_rows = jnp.concatenate([key_piece, value_piece], 1).reshape(
+        page_count, PAGE * 2 * quarter_width
+    )
+    targets = page_targets[:, 0]
+    page_numbers = jnp.arange(page_count, dtype=jnp.int32)
+    earlier = jnp.sum(
+        (
+            (targets[None, :] == targets[:, None]) & (page_numbers[None, :] < page_numbers[:, None])
+        ).astype(jnp.int32),
+        axis=1,
+    )
+    capacity = 2 * page_count // replica_count
+    slot_numbers = targets * capacity + earlier
+    placing = (
+        jnp.arange(replica_count * capacity, dtype=jnp.int32)[:, None] == slot_numbers[None, :]
+    ).astype(jnp.bfloat16)
+    outgoing = jnp.dot(placing, page_rows, preferred_element_type=jnp.float32).astype(jnp.bfloat16)
+    outgoing = outgoing.reshape(replica_count, capacity * PAGE, 2 * quarter_width)
+    head_pieces, incoming = exchange_all(
+        1,
+        (jnp.concatenate([query_piece, key_piece], 1)[None], "tensor", quarters, True, None),
+        (outgoing, "dp", replica_count, False, None),
     )
     queries = head_pieces[:, :, :quarter_width].transpose(1, 0, 2).reshape(tokens_total, HD)
     keys = head_pieces[:, :, quarter_width:].transpose(1, 0, 2).reshape(tokens_total, HD)
@@ -219,30 +257,13 @@
         axis=0,
     )
     column_sums = jnp.sum(
-        exchange(plane_sums, "tensor", planes, False, 5, (column_group, column_member)), axis=0
+        exchange(
+            plane_sums.astype(jnp.bfloat16), "tensor", planes, False, 5, (column_group, column_member)
+        ).astype(jnp.float32),
+        axis=0,
     )
     layer_output = hidden_states.astype(jnp.float32) + column_sums
 
-    page_count = tokens_total // PAGE
-    page_rows = jnp.concatenate([key_piece, value_piece], 1).reshape(
-        page_count, PAGE * 2 * quarter_width
-    )
-    targets = page_targets[:, 0]
-    page_numbers = jnp.arange(page_count, dtype=jnp.int32)
-    earlier = jnp.sum(
-        (
-            (targets[None, :] == targets[:, None]) & (page_numbers[None, :] < page_numbers[:, None])
-        ).astype(jnp.int32),
-        axis=1,
-    )
-    capacity = 2 * page_count // replica_count
-    slot_numbers = targets * capacity + earlier
-    placing = (
-        jnp.arange(replica_count * capacity, dtype=jnp.int32)[:, None] == slot_numbers[None, :]
-    ).astype(jnp.bfloat16)
-    outgoing = jnp.dot(placing, page_rows, preferred_element_type=jnp.float32).astype(jnp.bfloat16)
-    outgoing = outgoing.reshape(replica_count, capacity * PAGE, 2 * quarter_width)
-    incoming = exchange(outgoing, "dp", replica_count, False, 3)
     cache_pages = incoming.reshape(1, replica_count, capacity, PAGE, 2 * quarter_width)
     return (layer_output, cache_pages)
 

time: 139 us -> 124 us (0.89)
  Pallas kernels: 114 us -> 101 us
    pallas_call x6 -> x5, Pallas kernels: 114 us -> 101 us  [exchange_all(): pl.pallas_call(functools.partial(_exchange_kernel, tuple(plans)), out_sha...]
where the time goes in v3:
time: 124 us
  Pallas kernels  101 us (81%)
  matrix products  8.81 us (7%)
  other arithmetic  8.69 us (7%)
  local copies, waits for them, and re-layouts  4.11 us (3%)
    pallas_call x5, Pallas kernels, exchange_all(): pl.pallas_call(functools.partial(_exchange_kernel, tuple(plans)), out_sha...  101 us
    dot_general x1, matrix products, shards(): jnp.dot(hidden, downward_weight, preferred_element_type=jnp.float32)  4.56 us

profile of v3, /device:TPU:1, one launch (start us, length us, event | category | flops | bytes accessed | tf_op | source)
XLA Modules:
  0.0 123.6 jit_solution(1739522138239739668)
XLA Ops:
  0.6 0.0 copy-start
  0.7 20.5 %shard_map.104 = bf16[4,8,2048]{2,1,0:T(8,128)(2,1)} custom-call(bf16[1,8,2048]{2,1,0:T(8,128)(2,1)} %bitcast.64), custom_call_target="tpu_custom_call" | custom-call | tf_op jit(solution)/shard_map/pallas_call | solution.py:148
  21.2 22.3 %shard_map.105 = bf16[8,4,8,2048]{3,2,1,0:T(8,128)(2,1)} custom-call(bf16[1,4,8,2048]{3,2,1,0:T(8,128)(2,1)} %bitcast.63), custom_call_target="tpu_custom_call" | custom-call | tf_op jit(solution)/shard_map/pallas_call | solution.py:148
  43.5 1.5 %bitcast_convert_fusion = f32[4,2,4,8,2048]{4,3,2,1,0:T(8,128)S(1)} fusion(bf16[8,4,8,2048]{3,2,1,0:T(8,128)(2,1)} %shard_map.105), kind=kLoop, calls=%fused_computation.156 | loop fusion | flops 524288 | bytes 3145728 | tf_op jit(solution)/shard_map/convert_element_type | solution.py:22
  44.9 0.0 copy-start.1
  45.0 0.2 bitcast_reduce_fusion
  45.2 0.4 fusion.3
  45.6 0.1 rsqrt.13
  45.7 0.1 div.19
  45.8 0.4 copy-done.1
  46.2 0.2 copy.31
  46.4 0.0 copy-done.6
  46.4 0.0 copy-done.7
  46.4 0.0 copy-start.8
  46.4 0.5 multiply_convert_fusion.1
  47.0 0.0 copy-start.5
  47.0 0.6 copy-done.8
  47.6 0.5 convolution_convert_fusion.1
  48.0 0.1 slice_convert_fusion.1
  48.1 0.0 copy-done.5
  48.1 0.1 compare_reduce_fusion
  48.2 0.1 fusion.84
  48.3 0.3 reduce-window.9
  48.6 0.1 slice.46
  48.7 0.1 slice_reduce_fusion
  48.8 0.1 fusion.85
  48.9 0.6 fusion.36
  49.5 0.1 fusion.120
  49.7 0.7 pad_maximum_fusion
  50.4 0.0 copy-done.9
  50.4 0.2 convert_reduce_fusion.1
  50.6 0.2 convolution_convert_fusion
  50.8 0.7 reshape.114.refs_1_
  51.5 23.0 %shard_map.106 = (bf16[4,256,128]{2,1,0:T(8,128)(2,1)}, bf16[16,32,128]{2,1,0:T(8,128)(2,1)}) custom-call(bf16[1,256,128]{2,1,0:T(8,128)(2,1)} %get-tuple-element.18.refs_0_, bf16[16,32,128]{2,1,0:T(8,128)(2,1)} %reshape.114.refs_1_), custom_call_target="tpu_custom_call" | custom-call | tf_op jit(solution)/shard_map/pallas_call | solution.py:148
  74.5 1.3 %select_reduce_fusion = (f32[256]{0:T(256)S(1)}, f32[256,256]{0,1:T(8,128)S(1)}) fusion(s32[256]{0:T(256)S(1)} %bitcast.66, bf16[4,256,128]{2,1,0:T(8,128)(2,1)} %get-tuple-element.4), kind=kOutput, calls=%fused_computation.37 | convolution fusion | flops 33947392 | bytes 789504 | tf_op jit(solution)/shard_map/dot_general | solution.py:236
  75.9 0.1 fusion.29
  76.0 0.0 copy-done
  76.0 0.0 copy-start.2
  76.0 4.6 %fusion.31 = f32[256,2048]{1,0:T(8,128)} fusion(bf16[256,2048]{1,0:T(8,128)(2,1)S(1)} %copy-done, bf16[256,2048]{1,0:T(8,128)(2,1)S(1)} %get-tuple-element.7, bf16[2048,256]{1,0:T(8,128)(2,1)} %param.14), kind=kOutput, calls=%fused_computation.56 | convolution fusion | flops 541130752 | bytes 5242880 | tf_op jit(solution)/shard_map/dot_general | solution.py:246
  80.6 0.0 copy-done.2
  80.6 2.3 %fusion = bf16[256,2048]{1,0:T(8,128)(2,1)S(1)} fusion(f32[256,2048]{1,0:T(8,128)} %fusion.31, bf16[64,2048]{1,0:T(8,128)(2,1)S(1)} %copy-done.2, f32[256,256]{0,1:T(8,128)S(1)} %get-tuple-element.22, f32[256]{0:T(256)S(1)} %get-tuple-element.21, s32[256]{0:T(256)S(1)} %bitcast.68, f32[256]{0:T(256)S(1)} %fusion.29, ...), kind=kOutput, calls=%fused_computation.1 | convolution fusion | flops 76972032 | bytes 3739648 | tf_op jit(solution)/shard_map/dot_general | solution.py:245
  82.9 1.1 copy.38
  84.0 18.6 %shard_map.107 = bf16[8,4,8,2048]{3,2,1,0:T(8,128)(2,1)} custom-call(bf16[8,4,8,2048]{3,2,1,0:T(8,128)(2,1)} %bitcast.62), custom_call_target="tpu_custom_call" | custom-call | tf_op jit(solution)/shard_map/pallas_call | solution.py:148
  102.5 2.1 %reduce_sum.69.refs_0_ = bf16[4,8,2048]{2,1,0:T(8,128)(2,1)} reduce(bf16[8,4,8,2048]{3,2,1,0:T(8,128)(2,1)} %shard_map.107, bf16[]{:T(256)} %constant.102.clone.1), dimensions={0}, to_apply=%region_7.8 | reduce | flops 458752 | bytes 1179650 | tf_op jit(solution)/shard_map/reduce_sum | solution.py:253
  104.6 16.7 %shard_map.108 = bf16[4,8,2048]{2,1,0:T(8,128)(2,1)} custom-call(bf16[4,8,2048]{2,1,0:T(8,128)(2,1)} %reduce_sum.69.refs_0_), custom_call_target="tpu_custom_call" | custom-call | tf_op jit(solution)/shard_map/pallas_call | solution.py:148
  121.3 0.9 convert_reduce_fusion
  122.3 0.6 convert_add_fusion
  122.9 0.7 copy.46
  (13 shorter events, 0.1 us)
Async XLA Ops:
  0.6 75.4 %copy-start = (bf16[256,2048]{1,0:T(8,128)(2,1)S(1)}, bf16[256,2048]{1,0:T(8,128)(2,1)}, u32[]{:S(2)}) copy-start(bf16[256,2048]{1,0:T(8,128)(2,1)} %param.15) | copy-start | bytes 3145732
  44.9 1.2 copy-start.1
  45.5 0.9 copy-start.6
  45.5 0.9 copy-start.7
  46.4 1.1 copy-start.8
  47.0 1.1 copy-start.5
  47.6 2.9 %copy-start.9 = (s32[16,1]{0,1:T(1,128)S(1)}, s32[16,1]{0,1:T(1,128)}, u32[]{:S(2)}) copy-start(s32[16,1]{0,1:T(1,128)} %param.17) | copy-start | bytes 196
  76.0 4.6 %copy-start.2 = (bf16[64,2048]{1,0:T(8,128)(2,1)S(1)}, bf16[64,2048]{1,0:T(8,128)(2,1)}, u32[]{:S(2)}) copy-start(bf16[64,2048]{1,0:T(8,128)(2,1)} %param.13) | copy-start | bytes 786436
  84.0 38.3 %copy-start.3 = (bf16[8,2048]{1,0:T(8,128)(2,1)S(1)}, bf16[8,2048]{1,0:T(8,128)(2,1)}, u32[]{:S(2)}) copy-start(bf16[8,2048]{1,0:T(8,128)(2,1)} %param.9) | copy-start | bytes 98308
  84.0 39.0 %copy-start.4 = (bf16[16,32,128]{2,1,0:T(8,128)(2,1)S(1)}, bf16[16,32,128]{2,1,0:T(8,128)(2,1)}, u32[]{:S(2)}) copy-start(bf16[16,32,128]{2,1,0:T(8,128)(2,1)} %get-tuple-element.5) | copy-start | bytes 393220

commit v4 on v3

--- a/solution.py
+++ b/solution.py
@@ -159,6 +159,213 @@
     return exchange_all(collective_id, (blocks, axis, n, shared, group))[0]
 
 
+def _greet(barrier, groups):
+    index = lax.axis_index("tensor")
+    total = 0
+    for n, position, member in groups:
+        pos = position(index)
+
+        def greet(k, carry, n=n, pos=pos, member=member):
+            pl.semaphore_signal(
+                barrier,
+                inc=1,
+                device_id={"tensor": member(index, (pos + k) % n)},
+                device_id_type=pl.DeviceIdType.MESH,
+            )
+            return carry
+
+        lax.fori_loop(1, n, greet, 0)
+        total += n - 1
+    pl.semaphore_wait(barrier, total)
+
+
+def _gather_kernel(n_col, n_plane, col, plane, x_ref, out_ref, local_sem, send_sem, relay_sem, recv_sem):
+    index = lax.axis_index("tensor")
+    cpos, ppos = col[0](index), plane[0](index)
+    mesh_ids = pl.DeviceIdType.MESH
+    _greet(pltpu.get_barrier_semaphore(), [(n_col, *col), (n_plane, *plane)])
+
+    def col_copy(q):
+        return pltpu.make_async_remote_copy(
+            x_ref, out_ref.at[cpos, ppos], send_sem.at[q], recv_sem.at[cpos, ppos],
+            device_id={"tensor": col[1](index, q)}, device_id_type=mesh_ids,
+        )
+
+    def plane_copy(q):
+        return pltpu.make_async_remote_copy(
+            x_ref, out_ref.at[cpos, ppos], send_sem.at[n_col + q], recv_sem.at[cpos, ppos],
+            device_id={"tensor": plane[1](index, q)}, device_id_type=mesh_ids,
+        )
+
+    def relay_copy(zc, q):
+        return pltpu.make_async_remote_copy(
+            out_ref.at[zc, ppos], out_ref.at[zc, ppos], relay_sem.at[zc, q], recv_sem.at[zc, ppos],
+            device_id={"tensor": plane[1](index, q)}, device_id_type=mesh_ids,
+        )
+
+    def arrival(zc, p):
+        return pltpu.make_async_remote_copy(
+            x_ref, out_ref.at[zc, p], send_sem.at[0], recv_sem.at[zc, p],
+            device_id={"tensor": index}, device_id_type=mesh_ids,
+        )
+
+    local = pltpu.make_async_copy(x_ref, out_ref.at[cpos, ppos], local_sem)
+    local.start()
+
+    def send_col(k, carry):
+        col_copy((cpos + k) % n_col).start()
+        return carry
+
+    def send_plane(k, carry):
+        plane_copy((ppos + k) % n_plane).start()
+        return carry
+
+    lax.fori_loop(1, n_col, send_col, 0)
+    lax.fori_loop(1, n_plane, send_plane, 0)
+
+    def relay(k, carry):
+        zc = (cpos + k) % n_col
+        arrival(zc, ppos).wait_recv()
+
+        def forward(m, inner):
+            relay_copy(zc, (ppos + m) % n_plane).start()
+            return inner
+
+        return lax.fori_loop(1, n_plane, forward, carry)
+
+    lax.fori_loop(1, n_col, relay, 0)
+
+    def finish_col(k, carry):
+        col_copy((cpos + k) % n_col).wait_send()
+        return carry
+
+    def finish_plane(m, carry):
+        q = (ppos + m) % n_plane
+        plane_copy(q).wait_send()
+        arrival(cpos, q).wait_recv()
+        return carry
+
+    def finish_relay(k, carry):
+        zc = (cpos + k) % n_col
+
+        def inner(m, c):
+            q = (ppos + m) % n_plane
+            relay_copy(zc, q).wait_send()
+            arrival(zc, q).wait_recv()
+            return c
+
+        return lax.fori_loop(1, n_plane, inner, carry)
+
+    lax.fori_loop(1, n_col, finish_col, 0)
+    lax.fori_loop(1, n_plane, finish_plane, 0)
+    lax.fori_loop(1, n_col, finish_relay, 0)
+    local.wait()
+
+
+def gather_tokens(x, col, plane, n_col, n_plane, collective_id):
+    return pl.pallas_call(
+        functools.partial(_gather_kernel, n_col, n_plane, col, plane),
+        out_shape=jax.ShapeDtypeStruct((n_col, n_plane) + x.shape, x.dtype),
+        in_specs=[pl.BlockSpec(memory_space=pltpu.VMEM)],
+        out_specs=pl.BlockSpec(memory_space=pltpu.VMEM),
+        scratch_shapes=[
+            pltpu.SemaphoreType.DMA,
+            pltpu.SemaphoreType.DMA((n_col + n_plane,)),
+            pltpu.SemaphoreType.DMA((n_col, n_plane)),
+            pltpu.SemaphoreType.DMA((n_col, n_plane)),
+        ],
+        compiler_params=pltpu.CompilerParams(collective_id=collective_id, has_side_effects=True),
+    )(x)
+
+
+def _reduce_kernel(n_col, n_plane, col, plane, rows_ref, out_ref, inbox, stage, inbox2,
+                   local_sem, send_sem, recv_sem, local2_sem, send2_sem, recv2_sem):
+    index = lax.axis_index("tensor")
+    cpos, ppos = col[0](index), plane[0](index)
+    mesh_ids = pl.DeviceIdType.MESH
+    _greet(pltpu.get_barrier_semaphore(), [(n_col, *col), (n_plane, *plane)])
+
+    def plane_copy(q, slot):
+        return pltpu.make_async_remote_copy(
+            rows_ref.at[q], inbox.at[slot], send_sem.at[q], recv_sem.at[slot],
+            device_id={"tensor": plane[1](index, q)}, device_id_type=mesh_ids,
+        )
+
+    def col_copy(q, slot):
+        return pltpu.make_async_remote_copy(
+            stage.at[q], inbox2.at[slot], send2_sem.at[q], recv2_sem.at[slot],
+            device_id={"tensor": col[1](index, q)}, device_id_type=mesh_ids,
+        )
+
+    local = pltpu.make_async_copy(rows_ref.at[ppos], inbox.at[ppos], local_sem)
+    local.start()
+
+    def send_plane(m, carry):
+        plane_copy((ppos + m) % n_plane, ppos).start()
+        return carry
+
+    lax.fori_loop(1, n_plane, send_plane, 0)
+
+    def finish_plane(m, carry):
+        q = (ppos + m) % n_plane
+        plane_copy(q, ppos).wait_send()
+        plane_copy(q, q).wait_recv()
+        return carry
+
+    lax.fori_loop(1, n_plane, finish_plane, 0)
+    local.wait()
+
+    total = inbox[0].astype(jnp.float32)
+    for sender in range(1, n_plane):
+        total = total + inbox[sender].astype(jnp.float32)
+    stage[...] = total.astype(stage.dtype)
+
+    local2 = pltpu.make_async_copy(stage.at[cpos], inbox2.at[cpos], local2_sem)
+    local2.start()
+
+    def send_col(k, carry):
+        col_copy((cpos + k) % n_col, cpos).start()
+        return carry
+
+    lax.fori_loop(1, n_col, send_col, 0)
+
+    def finish_col(k, carry):
+        q = (cpos + k) % n_col
+        col_copy(q, cpos).wait_send()
+        col_copy(q, q).wait_recv()
+        return carry
+
+    lax.fori_loop(1, n_col, finish_col, 0)
+    local2.wait()
+
+    result = inbox2[0].astype(jnp.float32)
+    for sender in range(1, n_col):
+        result = result + inbox2[sender].astype(jnp.float32)
+    out_ref[...] = result
+
+
+def reduce_rows(rows, col, plane, n_col, n_plane, collective_id):
+    block = rows.shape[2:]
+    return pl.pallas_call(
+        functools.partial(_reduce_kernel, n_col, n_plane, col, plane),
+        out_shape=jax.ShapeDtypeStruct(block, jnp.float32),
+        in_specs=[pl.BlockSpec(memory_space=pltpu.VMEM)],
+        out_specs=pl.BlockSpec(memory_space=pltpu.VMEM),
+        scratch_shapes=[
+            pltpu.VMEM(rows.shape, rows.dtype),
+            pltpu.VMEM((n_col,) + block, rows.dtype),
+            pltpu.VMEM((n_col,) + block, rows.dtype),
+            pltpu.SemaphoreType.DMA,
+            pltpu.SemaphoreType.DMA((n_plane,)),
+            pltpu.SemaphoreType.DMA((n_plane,)),
+            pltpu.SemaphoreType.DMA,
+            pltpu.SemaphoreType.DMA((n_col,)),
+            pltpu.SemaphoreType.DMA((n_col,)),
+        ],
+        compiler_params=pltpu.CompilerParams(collective_id=collective_id, has_side_effects=True),
+    )(rows)
+
+
 def shards(
     hidden_states,
     attention_gain,
@@ -182,11 +389,12 @@
 
     width = hidden_states.shape[1]
     planes = tensor_count // 8
-    by_column = exchange(hidden_states[None], "tensor", planes, True, 0, (column_group, column_member))
-    by_plane = exchange(by_column[None], "tensor", 8, True, 4, (plane_group, plane_member))
+    gathered = gather_tokens(
+        hidden_states, (column_group, column_member), (plane_group, plane_member), planes, 8, 0
+    )
     tokens = (
-        by_plane.reshape(4, 2, planes, local_rows, width)
-        .transpose(0, 2, 1, 3, 4)
+        gathered.reshape(planes, 4, 2, local_rows, width)
+        .transpose(1, 0, 2, 3, 4)
         .reshape(tokens_total, width)
     )
     normed_attention = layer_norm(tokens, attention_gain)
@@ -250,17 +458,8 @@
         .transpose(0, 2, 1, 3, 4)
         .reshape(8, planes, local_rows, width)
     )
-    plane_sums = jnp.sum(
-        exchange(outgoing_rows, "tensor", 8, False, 2, (plane_group, plane_member)).astype(
-            jnp.float32
-        ),
-        axis=0,
-    )
-    column_sums = jnp.sum(
-        exchange(
-            plane_sums.astype(jnp.bfloat16), "tensor", planes, False, 5, (column_group, column_member)
-        ).astype(jnp.float32),
-        axis=0,
+    column_sums = reduce_rows(
+        outgoing_rows, (column_group, column_member), (plane_group, plane_member), planes, 8, 2
     )
     layer_output = hidden_states.astype(jnp.float32) + column_sums
 

time: 124 us -> 110 us (0.89)
  Pallas kernels: 101 us -> 88.7 us
  other arithmetic: 8.69 us -> 6.45 us
    pallas_call x5 -> x1, Pallas kernels: 101 us -> 21.9 us  [exchange_all(): pl.pallas_call(functools.partial(_exchange_kernel, tuple(plans)), out_sha...]
    pallas_call x0 -> x2, Pallas kernels: none -> 66.8 us  [the longest x1 33.6 us: gather_tokens(): pl.pallas_call(functools.partial(_gather_kernel, n_col, n_plane, col, pla...]
    reduce_sum x2 -> x0, other arithmetic: 2.99 us -> none  [the longest x1 2.06 us: shards(): jnp.sum(exchange(outgoing_rows, 'tensor', 8, False, 2, (plane_group, plan...]
    convert_element_type x1 -> x0, other arithmetic: 1.46 us -> none  [layer_norm(): floats = values.astype(jnp.float32)]
    convert_element_type x1, local copies, waits for them, and re-layouts: 0.22 us -> 1.54 us  [layer_norm(): floats = values.astype(jnp.float32)]
    convert_element_type x1, other arithmetic: 0.52 us -> 1.82 us  [layer_norm(): return (shifted * lax.rsqrt(spread + epsilon) * gain).astype(jnp.bfloat16)]
where the time goes in v4:
time: 110 us
  Pallas kernels  88.7 us (81%)
  matrix products  9.22 us (8%)
  other arithmetic  6.45 us (6%)
  local copies, waits for them, and re-layouts  4.54 us (4%)
    pallas_call x1, Pallas kernels, gather_tokens(): pl.pallas_call(functools.partial(_gather_kernel, n_col, n_plane, col, pla...  33.6 us
    pallas_call x1, Pallas kernels, reduce_rows(): pl.pallas_call(functools.partial(_reduce_kernel, n_col, n_plane, col, pla...  33.1 us
    pallas_call x1, Pallas kernels, exchange_all(): pl.pallas_call(functools.partial(_exchange_kernel, tuple(plans)), out_sha...  21.9 us
    dot_general x1, matrix products, shards(): jnp.dot(hidden, downward_weight, preferred_element_type=jnp.float32)  4.97 us
    dot_general x1, matrix products, shards(): jnp.dot(attended, output_weight, preferred_element_type=jnp.float32)  2.31 us

profile of v4, /device:TPU:1, one launch (start us, length us, event | category | flops | bytes accessed | tf_op | source)
XLA Modules:
  0.0 109.8 jit_solution(6336815165652931281)
XLA Ops:
  0.6 0.0 copy-start
  0.6 33.6 %shard_map.104 = bf16[4,8,8,2048]{3,2,1,0:T(8,128)(2,1)} custom-call(bf16[8,2048]{1,0:T(8,128)(2,1)} %x_ref.1), custom_call_target="tpu_custom_call" | custom-call | tf_op jit(solution)/shard_map/pallas_call | solution.py:266
  34.3 0.0 copy-start.1
  34.3 0.0 copy-start.7
  34.3 0.0 copy-start.8
  34.3 1.5 %copy.31 = f32[4,4,2,8,2048]{4,3,2,0,1:T(8,128)S(1)} copy(bf16[4,4,2,8,2048]{4,3,2,1,0:T(8,128)(2,1)} %bitcast.57) | data formatting | bytes 3145728 | tf_op jit(solution)/shard_map/convert_element_type | solution.py:22
  35.9 0.0 copy-done.1
  35.9 0.2 bitcast_reduce_fusion
  36.1 0.4 fusion.3
  36.6 0.1 rsqrt.13
  36.7 0.1 div.19
  36.8 0.0 copy-done.7
  36.8 0.0 copy-done.8
  36.8 1.8 %multiply_convert_fusion.1 = (bf16[256,2048]{1,0:T(8,128)(2,1)}, bf16[256,2048]{1,0:T(8,128)(2,1)}) fusion(f32[4,4,2,8,2048]{4,3,2,0,1:T(8,128)S(1)} %copy.31, f32[2048]{0:T(1024)S(1)} %copy-done.7, f32[256]{0:T(256)S(1)} %rsqrt.13, f32[256]{0:T(256)S(1)} %div.19, f32[2048]{0:T(1024)S(1)} %copy-done.8), kind=kLoop, calls=%fused_computation.10 | loop fusion | flops 3145728 | bytes 4212736 | tf_op jit(solution)/shard_map/convert_element_type | solution.py:26
  38.6 0.0 copy-done
  38.6 5.0 %fusion.31 = f32[256,2048]{1,0:T(8,128)} fusion(bf16[256,2048]{1,0:T(8,128)(2,1)S(1)} %copy-done, bf16[256,2048]{1,0:T(8,128)(2,1)} %get-tuple-element.7, bf16[2048,256]{1,0:T(8,128)(2,1)} %param.14), kind=kOutput, calls=%fused_computation.55 | convolution fusion | flops 541130752 | bytes 5242880 | tf_op jit(solution)/shard_map/dot_general | solution.py:454
  43.6 0.0 copy-done.2
  43.6 0.0 copy-done.9
  43.6 0.0 copy-start.10
  43.6 0.5 convolution_convert_fusion.1
  44.1 0.1 slice_convert_fusion.1
  44.1 0.0 copy-start.3
  44.2 0.1 copy-done.6
  44.3 0.1 compare_reduce_fusion
  44.3 0.1 fusion.84
  44.4 0.3 reduce-window.9
  44.7 0.1 slice.46
  44.9 0.1 slice_reduce_fusion
  45.0 0.1 fusion.85
  45.1 0.6 fusion.36
  45.7 0.1 fusion.120
  45.8 0.7 pad_maximum_fusion
  46.6 0.0 copy-done.10
  46.6 0.2 convert_reduce_fusion
  46.8 0.2 convolution_convert_fusion
  47.0 0.7 reshape.114.refs_1_
  47.7 21.9 %shard_map.105 = (bf16[4,256,128]{2,1,0:T(8,128)(2,1)}, bf16[16,32,128]{2,1,0:T(8,128)(2,1)}) custom-call(bf16[1,256,128]{2,1,0:T(8,128)(2,1)} %get-tuple-element.18.refs_0_, bf16[16,32,128]{2,1,0:T(8,128)(2,1)} %reshape.114.refs_1_), custom_call_target="tpu_custom_call" | custom-call | tf_op jit(solution)/shard_map/pallas_call | solution.py:148
  69.6 1.3 %select_reduce_fusion = (f32[256]{0:T(256)S(1)}, f32[256,256]{0,1:T(8,128)S(1)}) fusion(s32[256]{0:T(256)S(1)} %bitcast.63, bf16[4,256,128]{2,1,0:T(8,128)(2,1)} %get-tuple-element.4), kind=kOutput, calls=%fused_computation.36 | convolution fusion | flops 33947392 | bytes 789504 | tf_op jit(solution)/shard_map/dot_general | solution.py:444
  71.0 0.1 fusion.29
  71.1 0.0 copy-done.3
  71.1 2.3 %fusion = bf16[256,2048]{1,0:T(8,128)(2,1)S(1)} fusion(f32[256,2048]{1,0:T(8,128)} %fusion.31, bf16[64,2048]{1,0:T(8,128)(2,1)S(1)} %copy-done.3, f32[256,256]{0,1:T(8,128)S(1)} %get-tuple-element.22, f32[256]{0:T(256)S(1)} %get-tuple-element.21, s32[256]{0:T(256)S(1)} %bitcast.65, f32[256]{0:T(256)S(1)} %fusion.29, ...), kind=kOutput, calls=%fused_computation.1 | convolution fusion | flops 76972032 | bytes 3739648 | tf_op jit(solution)/shard_map/dot_general | solution.py:453
  73.4 0.0 copy-start.4
  73.4 0.0 copy-start.5
  73.4 1.1 copy.38
  74.5 33.1 %shard_map.106 = f32[8,2048]{1,0:T(8,128)} custom-call(bf16[8,4,8,2048]{3,2,1,0:T(8,128)(2,1)} %bitcast.61), custom_call_target="tpu_custom_call" | custom-call | tf_op jit(solution)/shard_map/pallas_call | solution.py:349
  107.6 1.5 %convert_add_fusion = f32[8,2048]{1,0:T(8,128)} fusion(f32[8,2048]{1,0:T(8,128)} %shard_map.106, bf16[8,2048]{1,0:T(8,128)(2,1)S(1)} %copy-done.4), kind=kLoop, calls=%fused_computation.102 | loop fusion | flops 32768 | bytes 163840 | tf_op jit(solution)/shard_map/add | solution.py:464
  109.1 0.0 copy-done.5
  109.1 0.7 copy.46
  (10 shorter events, 0.1 us)
Async XLA Ops:
  0.6 38.0 %copy-start = (bf16[256,2048]{1,0:T(8,128)(2,1)S(1)}, bf16[256,2048]{1,0:T(8,128)(2,1)}, u32[]{:S(2)}) copy-start(bf16[256,2048]{1,0:T(8,128)(2,1)} %param.15) | copy-start | bytes 3145732
  34.3 1.6 %copy-start.1 = (bf16[4,8,8,2048]{3,2,1,0:T(8,128)(2,1)S(1)}, bf16[4,8,8,2048]{3,2,1,0:T(8,128)(2,1)}, u32[]{:S(2)}) copy-start(bf16[4,8,8,2048]{3,2,1,0:T(8,128)(2,1)} %shard_map.104) | copy-start | bytes 3145732
  34.3 2.5 %copy-start.7 = (f32[2048]{0:T(1024)S(1)}, f32[2048]{0:T(1024)}, u32[]{:S(2)}) copy-start(f32[2048]{0:T(1024)} %param.10) | copy-start | bytes 24580
  34.3 2.5 %copy-start.8 = (f32[2048]{0:T(1024)S(1)}, f32[2048]{0:T(1024)}, u32[]{:S(2)}) copy-start(f32[2048]{0:T(1024)} %param.11) | copy-start | bytes 24580
  38.6 5.0 %copy-start.2 = (bf16[256,2048]{1,0:T(8,128)(2,1)S(1)}, bf16[256,2048]{1,0:T(8,128)(2,1)}, u32[]{:S(2)}) copy-start(bf16[256,2048]{1,0:T(8,128)(2,1)} %get-tuple-element.6) | copy-start | bytes 3145732
  38.6 5.0 %copy-start.9 = (bf16[2048,192]{0,1:T(8,128)(2,1)S(1)}, bf16[2048,192]{0,1:T(8,128)(2,1)}, u32[]{:S(2)}) copy-start(bf16[2048,192]{0,1:T(8,128)(2,1)} %param.12) | copy-start | bytes 2359300
  43.6 0.7 copy-start.6
  43.6 3.0 %copy-start.10 = (s32[16,1]{0,1:T(1,128)S(1)}, s32[16,1]{0,1:T(1,128)}, u32[]{:S(2)}) copy-start(s32[16,1]{0,1:T(1,128)} %param.17) | copy-start | bytes 196
  44.1 26.9 %copy-start.3 = (bf16[64,2048]{1,0:T(8,128)(2,1)S(1)}, bf16[64,2048]{1,0:T(8,128)(2,1)}, u32[]{:S(2)}) copy-start(bf16[64,2048]{1,0:T(8,128)(2,1)} %param.13) | copy-start | bytes 786436
  73.4 34.2 %copy-start.4 = (bf16[8,2048]{1,0:T(8,128)(2,1)S(1)}, bf16[8,2048]{1,0:T(8,128)(2,1)}, u32[]{:S(2)}) copy-start(bf16[8,2048]{1,0:T(8,128)(2,1)} %x_ref.1) | copy-start | bytes 98308
  73.4 35.7 %copy-start.5 = (bf16[16,32,128]{2,1,0:T(8,128)(2,1)S(1)}, bf16[16,32,128]{2,1,0:T(8,128)(2,1)}, u32[]{:S(2)}) copy-start(bf16[16,32,128]{2,1,0:T(8,128)(2,1)} %get-tuple-element.5) | copy-start | bytes 393220

commit v5 on v4

--- a/solution.py
+++ b/solution.py
@@ -55,9 +55,12 @@
     return rotated.astype(jnp.bfloat16)
 
 
-def _exchange_kernel(plans, *refs):
+def _exchange_kernel(plans, work, extra_in, extra_out, *refs):
     count = len(plans)
-    sources, outs, semaphores = refs[:count], refs[count : 2 * count], refs[2 * count :]
+    sources, refs = refs[:count], refs[count:]
+    inputs, refs = refs[:extra_in], refs[extra_in:]
+    outs, refs = refs[:count], refs[count:]
+    results, semaphores = refs[:extra_out], refs[extra_out:]
     mesh_ids = pl.DeviceIdType.MESH
     barrier = pltpu.get_barrier_semaphore()
     steps = []
@@ -101,6 +104,9 @@
 
         lax.fori_loop(1, n, send, 0)
 
+    if work is not None:
+        work(*inputs, *results)
+
     for n, pos, peer_copy, local in steps:
 
         def finish(k, carry, n=n, pos=pos, peer_copy=peer_copy):
@@ -125,6 +131,14 @@
     return ((q // 2) * 4 + (index // 2) % 4) * 2 + q % 2
 
 
+def token_block(zc, p):
+    return ((p // 2) * 4 + zc) * 2 + p % 2
+
+
+def plane_rows(rows_ref, q):
+    return rows_ref.at[q // 2, :, q % 2]
+
+
 def column_group(index):
     return (index // 2) % 4
 
@@ -133,7 +147,7 @@
     return ((index // 8) * 4 + q) * 2 + index % 2
 
 
-def exchange_all(collective_id, *requests):
+def exchange_all(collective_id, *requests, work=None, inputs=(), results=()):
     plans, blocks, shapes, scratch = [], [], [], []
     for data, axis, n, shared, group in requests:
         position, member = group if group is not None else contiguous(n)
@@ -145,18 +159,26 @@
             pltpu.SemaphoreType.DMA((n,)),
             pltpu.SemaphoreType.DMA((n,)),
         ]
+    operands = blocks + list(inputs)
+    out_shapes = shapes + list(results)
     return pl.pallas_call(
-        functools.partial(_exchange_kernel, tuple(plans)),
-        out_shape=tuple(shapes),
-        in_specs=[pl.BlockSpec(memory_space=pltpu.VMEM)] * len(blocks),
-        out_specs=tuple(pl.BlockSpec(memory_space=pltpu.VMEM) for _ in blocks),
+        functools.partial(_exchange_kernel, tuple(plans), work, len(inputs), len(results)),
+        out_shape=tuple(out_shapes),
+        in_specs=[pl.BlockSpec(memory_space=pltpu.VMEM)] * len(operands),
+        out_specs=tuple(pl.BlockSpec(memory_space=pltpu.VMEM) for _ in out_shapes),
         scratch_shapes=scratch,
         compiler_params=pltpu.CompilerParams(collective_id=collective_id, has_side_effects=True),
-    )(*blocks)
+    )(*operands)
 
 
 def exchange(blocks, axis, n, shared, collective_id, group=None):
     return exchange_all(collective_id, (blocks, axis, n, shared, group))[0]
+
+
+def _feedforward(normed_ref, upward_ref, downward_ref, out_ref):
+    upward = jnp.dot(normed_ref[...], upward_ref[...], preferred_element_type=jnp.float32)
+    hidden = (0.5 * upward * (1.0 + lax.erf(upward * math.sqrt(0.5)))).astype(jnp.bfloat16)
+    out_ref[...] = jnp.dot(hidden, downward_ref[...], preferred_element_type=jnp.float32)
 
 
 def _greet(barrier, groups):
@@ -179,7 +201,7 @@
     pl.semaphore_wait(barrier, total)
 
 
-def _gather_kernel(n_col, n_plane, col, plane, x_ref, out_ref, local_sem, send_sem, relay_sem, recv_sem):
+def _gather_kernel(n_col, n_plane, col, plane, slot, x_ref, out_ref, local_sem, send_sem, relay_sem, recv_sem):
     index = lax.axis_index("tensor")
     cpos, ppos = col[0](index), plane[0](index)
     mesh_ids = pl.DeviceIdType.MESH
@@ -187,29 +209,29 @@
 
     def col_copy(q):
         return pltpu.make_async_remote_copy(
-            x_ref, out_ref.at[cpos, ppos], send_sem.at[q], recv_sem.at[cpos, ppos],
+            x_ref, out_ref.at[slot(cpos, ppos)], send_sem.at[q], recv_sem.at[cpos, ppos],
             device_id={"tensor": col[1](index, q)}, device_id_type=mesh_ids,
         )
 
     def plane_copy(q):
         return pltpu.make_async_remote_copy(
-            x_ref, out_ref.at[cpos, ppos], send_sem.at[n_col + q], recv_sem.at[cpos, ppos],
+            x_ref, out_ref.at[slot(cpos, ppos)], send_sem.at[n_col + q], recv_sem.at[cpos, ppos],
             device_id={"tensor": plane[1](index, q)}, device_id_type=mesh_ids,
         )
 
     def relay_copy(zc, q):
         return pltpu.make_async_remote_copy(
-            out_ref.at[zc, ppos], out_ref.at[zc, ppos], relay_sem.at[zc, q], recv_sem.at[zc, ppos],
+            out_ref.at[slot(zc, ppos)], out_ref.at[slot(zc, ppos)], relay_sem.at[zc, q], recv_sem.at[zc, ppos],
             device_id={"tensor": plane[1](index, q)}, device_id_type=mesh_ids,
         )
 
     def arrival(zc, p):
         return pltpu.make_async_remote_copy(
-            x_ref, out_ref.at[zc, p], send_sem.at[0], recv_sem.at[zc, p],
+            x_ref, out_ref.at[slot(zc, p)], send_sem.at[0], recv_sem.at[zc, p],
             device_id={"tensor": index}, device_id_type=mesh_ids,
         )
 
-    local = pltpu.make_async_copy(x_ref, out_ref.at[cpos, ppos], local_sem)
+    local = pltpu.make_async_copy(x_ref, out_ref.at[slot(cpos, ppos)], local_sem)
     local.start()
 
     def send_col(k, carry):
@@ -262,10 +284,10 @@
     local.wait()
 
 
-def gather_tokens(x, col, plane, n_col, n_plane, collective_id):
+def gather_tokens(x, col, plane, slot, n_col, n_plane, collective_id):
     return pl.pallas_call(
-        functools.partial(_gather_kernel, n_col, n_plane, col, plane),
-        out_shape=jax.ShapeDtypeStruct((n_col, n_plane) + x.shape, x.dtype),
+        functools.partial(_gather_kernel, n_col, n_plane, col, plane, slot),
+        out_shape=jax.ShapeDtypeStruct((n_col * n_plane,) + x.shape, x.dtype),
         in_specs=[pl.BlockSpec(memory_space=pltpu.VMEM)],
         out_specs=pl.BlockSpec(memory_space=pltpu.VMEM),
         scratch_shapes=[
@@ -278,7 +300,7 @@
     )(x)
 
 
-def _reduce_kernel(n_col, n_plane, col, plane, rows_ref, out_ref, inbox, stage, inbox2,
+def _reduce_kernel(n_col, n_plane, col, plane, pick, rows_ref, x_ref, out_ref, inbox, stage, inbox2,
                    local_sem, send_sem, recv_sem, local2_sem, send2_sem, recv2_sem):
     index = lax.axis_index("tensor")
     cpos, ppos = col[0](index), plane[0](index)
@@ -287,7 +309,7 @@
 
     def plane_copy(q, slot):
         return pltpu.make_async_remote_copy(
-            rows_ref.at[q], inbox.at[slot], send_sem.at[q], recv_sem.at[slot],
+            pick(rows_ref, q), inbox.at[slot], send_sem.at[q], recv_sem.at[slot],
             device_id={"tensor": plane[1](index, q)}, device_id_type=mesh_ids,
         )
 
@@ -297,7 +319,7 @@
             device_id={"tensor": col[1](index, q)}, device_id_type=mesh_ids,
         )
 
-    local = pltpu.make_async_copy(rows_ref.at[ppos], inbox.at[ppos], local_sem)
+    local = pltpu.make_async_copy(pick(rows_ref, ppos), inbox.at[ppos], local_sem)
     local.start()
 
     def send_plane(m, carry):
@@ -338,21 +360,21 @@
     lax.fori_loop(1, n_col, finish_col, 0)
     local2.wait()
 
-    result = inbox2[0].astype(jnp.float32)
+    result = x_ref[...].astype(jnp.float32) + inbox2[0].astype(jnp.float32)
     for sender in range(1, n_col):
         result = result + inbox2[sender].astype(jnp.float32)
     out_ref[...] = result
 
 
-def reduce_rows(rows, col, plane, n_col, n_plane, collective_id):
-    block = rows.shape[2:]
+def reduce_rows(rows, x, col, plane, pick, n_col, n_plane, collective_id):
+    block = x.shape
     return pl.pallas_call(
-        functools.partial(_reduce_kernel, n_col, n_plane, col, plane),
+        functools.partial(_reduce_kernel, n_col, n_plane, col, plane, pick),
         out_shape=jax.ShapeDtypeStruct(block, jnp.float32),
-        in_specs=[pl.BlockSpec(memory_space=pltpu.VMEM)],
+        in_specs=[pl.BlockSpec(memory_space=pltpu.VMEM)] * 2,
         out_specs=pl.BlockSpec(memory_space=pltpu.VMEM),
         scratch_shapes=[
-            pltpu.VMEM(rows.shape, rows.dtype),
+            pltpu.VMEM((n_plane, n_col) + block, rows.dtype),
             pltpu.VMEM((n_col,) + block, rows.dtype),
             pltpu.VMEM((n_col,) + block, rows.dtype),
             pltpu.SemaphoreType.DMA,
@@ -363,7 +385,7 @@
             pltpu.SemaphoreType.DMA((n_col,)),
         ],
         compiler_params=pltpu.CompilerParams(collective_id=collective_id, has_side_effects=True),
-    )(rows)
+    )(rows, x)
 
 
 def shards(
@@ -390,20 +412,20 @@
     width = hidden_states.shape[1]
     planes = tensor_count // 8
     gathered = gather_tokens(
-        hidden_states, (column_group, column_member), (plane_group, plane_member), planes, 8, 0
-    )
-    tokens = (
-        gathered.reshape(planes, 4, 2, local_rows, width)
-        .transpose(1, 0, 2, 3, 4)
-        .reshape(tokens_total, width)
-    )
+        hidden_states,
+        (column_group, column_member),
+        (plane_group, plane_member),
+        token_block,
+        planes,
+        8,
+        0,
+    )
+    tokens = gathered.reshape(tokens_total, width)
     normed_attention = layer_norm(tokens, attention_gain)
     normed_feedforward = layer_norm(tokens, feedforward_gain)
     joined = jnp.dot(normed_attention, heads_weight, preferred_element_type=jnp.float32).astype(
         jnp.bfloat16
     )
-    upward = jnp.dot(normed_feedforward, upward_weight, preferred_element_type=jnp.float32)
-    hidden = jax.nn.gelu(upward, approximate=False).astype(jnp.bfloat16)
 
     indices, starting = positions_of(stream)
     offsets = indices - starting
@@ -433,10 +455,13 @@
     ).astype(jnp.bfloat16)
     outgoing = jnp.dot(placing, page_rows, preferred_element_type=jnp.float32).astype(jnp.bfloat16)
     outgoing = outgoing.reshape(replica_count, capacity * PAGE, 2 * quarter_width)
-    head_pieces, incoming = exchange_all(
+    head_pieces, incoming, feedforward = exchange_all(
         1,
         (jnp.concatenate([query_piece, key_piece], 1)[None], "tensor", quarters, True, None),
         (outgoing, "dp", replica_count, False, None),
+        work=_feedforward,
+        inputs=(normed_feedforward, upward_weight, downward_weight),
+        results=(jax.ShapeDtypeStruct((tokens_total, width), jnp.float32),),
     )
     queries = head_pieces[:, :, :quarter_width].transpose(1, 0, 2).reshape(tokens_total, HD)
     keys = head_pieces[:, :, quarter_width:].transpose(1, 0, 2).reshape(tokens_total, HD)
@@ -450,18 +475,18 @@
     attended = (mixed / weight_sum).astype(jnp.bfloat16)
 
     partial = (
-        jnp.dot(attended, output_weight, preferred_element_type=jnp.float32)
-        + jnp.dot(hidden, downward_weight, preferred_element_type=jnp.float32)
+        jnp.dot(attended, output_weight, preferred_element_type=jnp.float32) + feedforward
     ).astype(jnp.bfloat16)
-    outgoing_rows = (
-        partial.reshape(4, planes, 2, local_rows, width)
-        .transpose(0, 2, 1, 3, 4)
-        .reshape(8, planes, local_rows, width)
-    )
-    column_sums = reduce_rows(
-        outgoing_rows, (column_group, column_member), (plane_group, plane_member), planes, 8, 2
-    )
-    layer_output = hidden_states.astype(jnp.float32) + column_sums
+    layer_output = reduce_rows(
+        partial.reshape(4, planes, 2, local_rows, width),
+        hidden_states,
+        (column_group, column_member),
+        (plane_group, plane_member),
+        plane_rows,
+        planes,
+        8,
+        2,
+    )
 
     cache_pages = incoming.reshape(1, replica_count, capacity, PAGE, 2 * quarter_width)
     return (layer_output, cache_pages)

time: 110 us -> 109 us (level)
  matrix products: 9.22 us -> 5.34 us
  other arithmetic: 6.45 us -> 9.18 us
  Pallas kernels: 88.7 us -> 90.4 us
  local copies, waits for them, and re-layouts: 4.54 us -> 3.29 us
    dot_general x1 -> x0, matrix products: 4.97 us -> none  [shards(): jnp.dot(hidden, downward_weight, preferred_element_type=jnp.float32)]
    pallas_call x1, Pallas kernels: 21.9 us -> 23.8 us  [exchange_all(): pl.pallas_call(functools.partial(_exchange_kernel, tuple(plans), work, le...]
    convert_element_type x1 -> x0, local copies, waits for them, and re-layouts: 1.54 us -> none  [layer_norm(): floats = values.astype(jnp.float32)]
    add x1 -> x0, other arithmetic: 1.48 us -> none  [shards(): layer_output = hidden_states.astype(jnp.float32) + column_sums]
    unnamed x23 -> x16, local copies, waits for them, and re-layouts: 0.81 us -> 2.17 us
    reduce_sum x1, other arithmetic: 0.22 us -> 1.53 us  [layer_norm(): center = jnp.mean(floats, axis=-1, keepdims=True)]
    reduce_sum x1, other arithmetic: 0.42 us -> 1.64 us  [layer_norm(): spread = jnp.mean(shifted * shifted, axis=-1, keepdims=True)]
where the time goes in v5:
time: 109 us
  Pallas kernels  90.4 us (83%)
  other arithmetic  9.18 us (8%)
  matrix products  5.34 us (5%)
  local copies, waits for them, and re-layouts  3.29 us (3%)
    pallas_call x1, Pallas kernels, gather_tokens(): pl.pallas_call(functools.partial(_gather_kernel, n_col, n_plane, col, pla...  33.5 us
    pallas_call x1, Pallas kernels, reduce_rows(): pl.pallas_call(functools.partial(_reduce_kernel, n_col, n_plane, col, pla...  33.1 us
    pallas_call x1, Pallas kernels, exchange_all(): pl.pallas_call(functools.partial(_exchange_kernel, tuple(plans), work, le...  23.8 us
    dot_general x1, matrix products, shards(): jnp.dot(attended, output_weight, preferred_element_type=jnp.float32)  3.32 us

profile of v5, /device:TPU:1, one launch (start us, length us, event | category | flops | bytes accessed | tf_op | source)
XLA Modules:
  0.0 109.0 jit_solution(5620002857221311054)
XLA Ops:
  0.6 0.0 copy-start
  0.6 0.0 copy-start.6
  0.7 0.9 convert_reduce_fusion.1
  1.6 0.7 multiply_add_fusion
  2.3 0.8 compare_reduce_fusion
  3.1 0.1 fusion.51
  3.2 0.3 reduce-window.9
  3.5 0.1 slice.46
  3.6 0.1 slice_reduce_fusion
  3.7 0.1 fusion.52
  3.8 33.5 %shard_map.104 = bf16[32,8,2048]{2,1,0:T(8,128)(2,1)} custom-call(bf16[8,2048]{1,0:T(8,128)(2,1)} %x_ref.3), custom_call_target="tpu_custom_call" | custom-call | tf_op jit(solution)/shard_map/pallas_call | solution.py:288
  37.3 0.0 copy-start.1
  37.3 1.5 %convert_reduce_fusion = f32[32,8]{1,0:T(8,128)S(1)} fusion(bf16[32,8,2048]{2,1,0:T(8,128)(2,1)} %shard_map.104), kind=kLoop, calls=%fused_computation.1 | loop fusion | flops 1048320 | bytes 1049600 | tf_op jit(solution)/shard_map/reduce_sum | solution.py:23
  38.9 0.1 div.19
  39.0 0.0 copy-start.5
  39.0 1.6 %fusion.8 = f32[32,8]{1,0:T(8,128)S(1)} fusion(bf16[32,8,2048]{2,1,0:T(8,128)(2,1)} %shard_map.104, f32[32,8]{1,0:T(8,128)S(1)} %broadcast_multiply_fusion), kind=kLoop, calls=%fused_computation.13 | loop fusion | flops 2096896 | bytes 1050624 | tf_op jit(solution)/shard_map/reduce_sum | solution.py:25
  40.6 0.1 rsqrt.13
  40.7 0.0 copy-done
  40.7 0.0 copy-done.6
  40.7 0.0 copy-done.1
  40.8 0.5 convolution_convert_fusion.1
  41.3 0.0 copy-done.5
  41.3 1.4 %fusion.6.refs_2_ = bf16[256,2048]{1,0:T(8,128)(2,1)} fusion(bf16[32,8,2048]{2,1,0:T(8,128)(2,1)S(1)} %copy-done.1, f32[2048]{0:T(1024)S(1)} %copy-done.5, f32[256]{0:T(256)S(1)} %rsqrt.13, f32[256]{0:T(256)S(1)} %div.19), kind=kLoop, calls=%fused_computation.11 | loop fusion | flops 2621440 | bytes 2107392 | tf_op jit(solution)/shard_map/convert_element_type | solution.py:26
  42.7 0.1 slice_convert_fusion.1
  42.8 0.6 fusion.33
  43.4 0.1 fusion.57
  43.5 0.0 copy-start.4
  43.5 0.7 pad_maximum_fusion
  44.3 0.2 convolution_convert_fusion
  44.5 0.7 reshape.106.refs_1_
  45.2 0.0 copy-start.2
  45.2 23.8 %shard_map.105 = (bf16[4,256,128]{2,1,0:T(8,128)(2,1)}, bf16[16,32,128]{2,1,0:T(8,128)(2,1)}, f32[256,2048]{1,0:T(8,128)}) custom-call(bf16[1,256,128]{2,1,0:T(8,128)(2,1)} %get-tuple-element.18.refs_0_, bf16[16,32,128]{2,1,0:T(8,128)(2,1)} %reshape.106.refs_1_, bf16[256,2048]{1,0:T(8,128)(2,1)} %fusion.6.refs_2_, bf16[2048,256]{1,0:T(8,128)(2,1)} %refs_3_.1, ...), custom_call_target="tpu_custom_call" | custom-call | tf_op jit(solution)/shard_map/pallas_call | solution.py:164
  69.0 0.0 copy-done.4
  69.0 1.3 %select_reduce_fusion = (f32[256]{0:T(256)S(1)}, f32[256,256]{0,1:T(8,128)S(1)}) fusion(s32[256]{0:T(256)S(1)} %bitcast.49, bf16[4,256,128]{2,1,0:T(8,128)(2,1)} %get-tuple-element.5), kind=kOutput, calls=%fused_computation.25 | convolution fusion | flops 33947392 | bytes 789504 | tf_op jit(solution)/shard_map/dot_general | solution.py:469
  70.3 0.1 fusion.28
  70.4 0.0 copy-done.2
  70.5 0.0 copy-start.3
  70.5 3.3 %fusion = bf16[256,2048]{1,0:T(8,128)(2,1)} fusion(f32[256,2048]{1,0:T(8,128)} %get-tuple-element.6, bf16[64,2048]{1,0:T(8,128)(2,1)S(1)} %copy-done.2, f32[256,256]{0,1:T(8,128)S(1)} %get-tuple-element.22, f32[256]{0:T(256)S(1)} %get-tuple-element.21, s32[256]{0:T(256)S(1)} %bitcast.51, f32[256]{0:T(256)S(1)} %fusion.28, ...), kind=kOutput, calls=%fused_computation.4 | convolution fusion | flops 76972032 | bytes 3739648 | tf_op jit(solution)/shard_map/dot_general | solution.py:478
  73.8 33.1 %shard_map.106 = f32[8,2048]{1,0:T(8,128)} custom-call(bf16[4,4,2,8,2048]{4,3,2,1,0:T(8,128)(2,1)} %bitcast.47, bf16[8,2048]{1,0:T(8,128)(2,1)} %x_ref.3), custom_call_target="tpu_custom_call" | custom-call | tf_op jit(solution)/shard_map/pallas_call | solution.py:371
  106.9 1.5 %copy.29 = f32[8,2048]{1,0:T(8,128)} copy(f32[8,2048]{1,0:T(8,128)} %shard_map.106) | data formatting | bytes 131072
  108.3 0.0 copy-done.3
  108.3 0.7 copy.30
  (5 shorter events, 0.1 us)
Async XLA Ops:
  0.6 40.1 %copy-start = (bf16[2048,192]{0,1:T(8,128)(2,1)S(1)}, bf16[2048,192]{0,1:T(8,128)(2,1)}, u32[]{:S(2)}) copy-start(bf16[2048,192]{0,1:T(8,128)(2,1)} %param.12) | copy-start | bytes 2359300
  0.6 40.1 %copy-start.6 = (f32[2048]{0:T(1024)S(1)}, f32[2048]{0:T(1024)}, u32[]{:S(2)}) copy-start(f32[2048]{0:T(1024)} %param.10) | copy-start | bytes 24580
  37.3 3.4 %copy-start.1 = (bf16[32,8,2048]{2,1,0:T(8,128)(2,1)S(1)}, bf16[32,8,2048]{2,1,0:T(8,128)(2,1)}, u32[]{:S(2)}) copy-start(bf16[32,8,2048]{2,1,0:T(8,128)(2,1)} %shard_map.104) | copy-start | bytes 3145732
  39.0 2.3 %copy-start.5 = (f32[2048]{0:T(1024)S(1)}, f32[2048]{0:T(1024)}, u32[]{:S(2)}) copy-start(f32[2048]{0:T(1024)} %param.11) | copy-start | bytes 24580
  43.5 25.5 %copy-start.4 = (s32[1,256]{1,0:T(1,128)S(1)}, s32[1,256]{1,0:T(1,128)}, u32[]{:S(2)}) copy-start(s32[1,256]{1,0:T(1,128)} %param.16) | copy-start | bytes 3076
  45.2 25.3 %copy-start.2 = (bf16[64,2048]{1,0:T(8,128)(2,1)S(1)}, bf16[64,2048]{1,0:T(8,128)(2,1)}, u32[]{:S(2)}) copy-start(bf16[64,2048]{1,0:T(8,128)(2,1)} %param.13) | copy-start | bytes 786436
  70.5 37.9 %copy-start.3 = (bf16[16,32,128]{2,1,0:T(8,128)(2,1)S(1)}, bf16[16,32,128]{2,1,0:T(8,128)(2,1)}, u32[]{:S(2)}) copy-start(bf16[16,32,128]{2,1,0:T(8,128)(2,1)} %get-tuple-element.7) | copy-start | bytes 393220

commit v6 on v5

--- a/solution.py
+++ b/solution.py
@@ -423,18 +423,34 @@
     tokens = gathered.reshape(tokens_total, width)
     normed_attention = layer_norm(tokens, attention_gain)
     normed_feedforward = layer_norm(tokens, feedforward_gain)
+    partner_weight = lax.ppermute(
+        heads_weight[:, : 2 * quarter_width],
+        "tensor",
+        [(source, source ^ 2) for source in range(tensor_count)],
+    )
     joined = jnp.dot(normed_attention, heads_weight, preferred_element_type=jnp.float32).astype(
         jnp.bfloat16
     )
+    partner_joined = jnp.dot(
+        normed_attention, partner_weight, preferred_element_type=jnp.float32
+    ).astype(jnp.bfloat16)
 
     indices, starting = positions_of(stream)
     offsets = indices - starting
     query_piece = joined[:, :quarter_width]
     key_piece = joined[:, quarter_width : 2 * quarter_width]
     value_piece = joined[:, 2 * quarter_width :]
+    partner_query = partner_joined[:, :quarter_width]
+    partner_key = partner_joined[:, quarter_width:]
     leading = quarter_index == 0
+    partner_leading = quarter_index == 2
     query_piece = jnp.where(leading, rotate_leading(query_piece, offsets, ROT), query_piece)
     key_piece = jnp.where(leading, rotate_leading(key_piece, offsets, ROT), key_piece)
+    partner_query = jnp.where(
+        partner_leading, rotate_leading(partner_query, offsets, ROT), partner_query
+    )
+    partner_key = jnp.where(partner_leading, rotate_leading(partner_key, offsets, ROT), partner_key)
+    held = jnp.concatenate([query_piece, key_piece, partner_query, partner_key], 1)
 
     page_count = tokens_total // PAGE
     page_rows = jnp.concatenate([key_piece, value_piece], 1).reshape(
@@ -457,14 +473,16 @@
     outgoing = outgoing.reshape(replica_count, capacity * PAGE, 2 * quarter_width)
     head_pieces, incoming, feedforward = exchange_all(
         1,
-        (jnp.concatenate([query_piece, key_piece], 1)[None], "tensor", quarters, True, None),
+        (held[None], "tensor", 2, True, None),
         (outgoing, "dp", replica_count, False, None),
         work=_feedforward,
         inputs=(normed_feedforward, upward_weight, downward_weight),
         results=(jax.ShapeDtypeStruct((tokens_total, width), jnp.float32),),
     )
-    queries = head_pieces[:, :, :quarter_width].transpose(1, 0, 2).reshape(tokens_total, HD)
-    keys = head_pieces[:, :, quarter_width:].transpose(1, 0, 2).reshape(tokens_total, HD)
+    pieces = head_pieces.reshape(2, tokens_total, 2, 2, quarter_width)
+    pieces = jnp.where(quarter_index // 2 == 0, pieces, pieces[:, :, ::-1])
+    queries = pieces[:, :, :, 0].transpose(1, 2, 0, 3).reshape(tokens_total, HD)
+    keys = pieces[:, :, :, 1].transpose(1, 2, 0, 3).reshape(tokens_total, HD)
 
     scores = jnp.dot(queries, keys.T, preferred_element_type=jnp.float32) * HD ** (-0.5)
     allowed = (stream[None, :] == stream[:, None]) & (indices[None, :] <= indices[:, None])

time: 109 us -> 141 us (1.29)
  Pallas kernels: 90.4 us -> 112 us
  starting transfers between devices: 0 us -> 9.65 us
  local copies, waits for them, and re-layouts: 3.29 us -> 5.69 us
    pallas_call x1, Pallas kernels: 33.5 us -> 65.1 us  [gather_tokens(): pl.pallas_call(functools.partial(_gather_kernel, n_col, n_plane, col, pla...]
    pallas_call x1, Pallas kernels: 23.8 us -> 12.3 us  [exchange_all(): pl.pallas_call(functools.partial(_exchange_kernel, tuple(plans), work, le...]
    ppermute x0 -> x1, starting transfers between devices: none -> 9.65 us  [shards(): lax.ppermute(heads_weight[:, :2 * quarter_width], 'tensor', [(source, sou...]
    pallas_call x1, Pallas kernels: 33.1 us -> 35.1 us  [reduce_rows(): pl.pallas_call(functools.partial(_reduce_kernel, n_col, n_plane, col, pla...]
    dot_general x1, matrix products: 3.32 us -> 1.7 us  [shards(): jnp.dot(attended, output_weight, preferred_element_type=jnp.float32)]
    dot_general x0 -> x1, matrix products: none -> 1.56 us  [shards(): jnp.dot(normed_attention, partner_weight, preferred_element_type=jnp.floa...]
  transfers between devices with their start and end apart: 0 -> 1, of which waited for: 0 -> 0; matrix products, arithmetic and copies ran while one was open for 0% -> 4% of each run, Pallas kernels for 0% -> 46%
where the time goes in v6:
time: 141 us
  Pallas kernels  112 us (79%)
  starting transfers between devices  9.65 us (7%)
  other arithmetic  7.98 us (6%)
  local copies, waits for them, and re-layouts  5.69 us (4%)
  matrix products  4.21 us (3%)
    pallas_call x1, Pallas kernels, gather_tokens(): pl.pallas_call(functools.partial(_gather_kernel, n_col, n_plane, col, pla...  65.1 us
    pallas_call x1, Pallas kernels, reduce_rows(): pl.pallas_call(functools.partial(_reduce_kernel, n_col, n_plane, col, pla...  35.1 us
    pallas_call x1, Pallas kernels, exchange_all(): pl.pallas_call(functools.partial(_exchange_kernel, tuple(plans), work, le...  12.3 us
    ppermute x1, starting transfers between devices, shards(): lax.ppermute(heads_weight[:, :2 * quarter_width], 'tensor', [(source, sou...  9.65 us
  transfers between devices with their start and end apart: 1, of which 0 were waited for; matrix products, arithmetic and copies ran while one was open for 4% of the time, Pallas kernels for 46%

profile of v6, /device:TPU:1, one launch (start us, length us, event | category | flops | bytes accessed | tf_op | source)
XLA Modules:
  0.0 141.0 jit_solution(17990481938585206125)
XLA Ops:
  0.6 0.0 copy-start
  0.6 0.0 copy-start.3
  0.7 0.0 copy-start.8
  0.7 0.0 copy-start.5
  0.7 0.0 copy-start.7
  0.7 1.2 slice.73
  1.8 9.6 %collective-permute-start = (bf16[2048,128]{0,1:T(8,128)(2,1)S(1)}, bf16[2048,128]{0,1:T(8,128)(2,1)}, u32[]{:S(2)}, u32[]{:S(2)}) collective-permute-start(bf16[2048,128]{0,1:T(8,128)(2,1)S(1)} %slice.73), channel_id=1, source_target_pairs={{0,2},{1,3},{2,0},{3,1},{4,6},{5,7},{6,4},{7,5},{8,10},{9,11},{10,... | collective-permute-start | bytes 1572872 | tf_op jit(solution)/shard_map/ppermute | solution.py:426
  11.5 65.1 %shard_map.104 = bf16[32,8,2048]{2,1,0:T(8,128)(2,1)} custom-call(bf16[8,2048]{1,0:T(8,128)(2,1)} %x_ref.3), custom_call_target="tpu_custom_call" | custom-call | tf_op jit(solution)/shard_map/pallas_call | solution.py:288
  76.6 0.0 copy-start.1
  76.6 1.5 %convert_reduce_fusion = f32[32,8]{1,0:T(8,128)S(1)} fusion(bf16[32,8,2048]{2,1,0:T(8,128)(2,1)} %shard_map.104), kind=kLoop, calls=%fused_computation.1 | loop fusion | flops 1048320 | bytes 1049600 | tf_op jit(solution)/shard_map/reduce_sum | solution.py:23
  78.2 0.1 div.30
  78.3 1.6 %fusion.8 = f32[32,8]{1,0:T(8,128)S(1)} fusion(bf16[32,8,2048]{2,1,0:T(8,128)(2,1)} %shard_map.104, f32[32,8]{1,0:T(8,128)S(1)} %broadcast_multiply_fusion), kind=kLoop, calls=%fused_computation.13 | loop fusion | flops 2096896 | bytes 1050624 | tf_op jit(solution)/shard_map/reduce_sum | solution.py:25
  79.9 0.0 copy-done.8
  79.9 0.2 convert_reduce_fusion.1
  80.1 0.0 copy-done.5
  80.1 0.1 compare_reduce_fusion
  80.2 0.1 fusion.59
  80.3 0.3 reduce-window.9
  80.6 0.1 slice.67
  80.7 0.1 slice_reduce_fusion
  80.8 0.1 fusion.60
  80.9 0.1 rsqrt.13
  81.0 0.0 copy-done.3
  81.0 0.0 copy-done.7
  81.0 0.0 copy-done.1
  81.0 0.5 convolution_convert_fusion.1
  81.6 0.1 slice_convert_fusion.3
  81.7 0.0 copy-done.6
  81.7 1.4 fusion.6.refs_2_
  83.1 0.0 collective-permute-done
  83.1 1.6 %convolution_convert_fusion.2 = bf16[256,128]{1,0:T(8,128)(2,1)S(1)} fusion(bf16[2048,128]{0,1:T(8,128)(2,1)} %collective-permute-done, bf16[32,8,2048]{2,1,0:T(8,128)(2,1)S(1)} %copy-done.1, f32[2048]{0:T(1024)S(1)} %copy-done.7, f32[256]{0:T(256)S(1)} %rsqrt.13, f32[256]{0:T(256)S(1)} %div.30), kind=kOutput, calls=%fused_computation.17 | convolution fusion | flops 136871936 | bytes 1648640 | tf_op jit(solution)/shard_map/dot_general | solution.py:434
  84.7 0.6 fusion.41
  85.3 0.1 maximum_select_fusion.2
  85.4 0.6 fusion.33
  86.0 0.2 fusion.67
  86.2 0.1 pad_maximum_fusion
  86.3 0.2 convolution_convert_fusion
  86.5 0.7 reshape.109.refs_1_
  87.2 0.8 maximum_bitcast_fusion.refs_0_
  88.0 12.3 %shard_map.105 = (bf16[2,256,256]{2,1,0:T(8,128)(2,1)}, bf16[16,32,128]{2,1,0:T(8,128)(2,1)}, f32[256,2048]{1,0:T(8,128)}) custom-call(bf16[1,256,256]{2,1,0:T(8,128)(2,1)} %maximum_bitcast_fusion.refs_0_, bf16[16,32,128]{2,1,0:T(8,128)(2,1)} %reshape.109.refs_1_, bf16[256,2048]{1,0:T(8,128)(2,1)} %fusion.6.refs_2_, bf16[2048,256]{1,0:T(8,128)(2,1)} %refs_3_.1, ...), custom_call_target="tpu_custom_call" | custom-call | tf_op jit(solution)/shard_map/pallas_call | solution.py:164
  100.3 0.0 copy-start.2
  100.3 1.2 copy.28
  101.6 0.3 select_reduce_fusion
  101.9 0.1 fusion.28
  102.0 1.7 %fusion = bf16[256,2048]{1,0:T(8,128)(2,1)} fusion(f32[256,2048]{1,0:T(8,128)S(1)} %copy-done.2, bf16[64,2048]{1,0:T(8,128)(2,1)S(1)} %copy-done, f32[256,256]{0,1:T(8,128)S(1)} %get-tuple-element.28, f32[256]{0:T(256)S(1)} %get-tuple-element.27, s32[256]{0:T(256)S(1)} %bitcast.61, f32[256]{0:T(256)S(1)} %fusion.28, ...), kind=kOutput, calls=%fused_computation.4 | convolution fusion | flops 76972032 | bytes 3739648 | tf_op jit(solution)/shard_map/dot_general | solution.py:496
  103.7 35.1 %shard_map.106 = f32[8,2048]{1,0:T(8,128)} custom-call(bf16[4,4,2,8,2048]{4,3,2,1,0:T(8,128)(2,1)} %bitcast.56, bf16[8,2048]{1,0:T(8,128)(2,1)} %x_ref.3), custom_call_target="tpu_custom_call" | custom-call | tf_op jit(solution)/shard_map/pallas_call | solution.py:371
  138.8 1.5 %copy.36 = f32[8,2048]{1,0:T(8,128)} copy(f32[8,2048]{1,0:T(8,128)} %shard_map.106) | data formatting | bytes 131072
  140.3 0.7 copy.37
  (14 shorter events, 0.2 us)
Async XLA Ops:
  0.6 101.4 %copy-start = (bf16[64,2048]{1,0:T(8,128)(2,1)S(1)}, bf16[64,2048]{1,0:T(8,128)(2,1)}, u32[]{:S(2)}) copy-start(bf16[64,2048]{1,0:T(8,128)(2,1)} %param.13) | copy-start | bytes 786436
  0.6 80.4 %copy-start.3 = (bf16[2048,192]{0,1:T(8,128)(2,1)S(1)}, bf16[2048,192]{0,1:T(8,128)(2,1)}, u32[]{:S(2)}) copy-start(bf16[2048,192]{0,1:T(8,128)(2,1)} %param.12) | copy-start | bytes 2359300
  0.7 79.3 %copy-start.8 = (s32[16,1]{0,1:T(1,128)S(1)}, s32[16,1]{0,1:T(1,128)}, u32[]{:S(2)}) copy-start(s32[16,1]{0,1:T(1,128)} %param.17) | copy-start | bytes 196
  0.7 79.4 %copy-start.5 = (s32[1,256]{1,0:T(1,128)S(1)}, s32[1,256]{1,0:T(1,128)}, u32[]{:S(2)}) copy-start(s32[1,256]{1,0:T(1,128)} %param.16) | copy-start | bytes 3076
  0.7 80.4 %copy-start.7 = (f32[2048]{0:T(1024)S(1)}, f32[2048]{0:T(1024)}, u32[]{:S(2)}) copy-start(f32[2048]{0:T(1024)} %param.10) | copy-start | bytes 24580
  1.8 81.3 %collective-permute-start = (bf16[2048,128]{0,1:T(8,128)(2,1)S(1)}, bf16[2048,128]{0,1:T(8,128)(2,1)}, u32[]{:S(2)}, u32[]{:S(2)}) collective-permute-start(bf16[2048,128]{0,1:T(8,128)(2,1)S(1)} %slice.73), channel_id=1, source_target_pairs={{0,2},{1,3},{2,0},{3,1},{4,6},{5,7},{6,4},{7,5},{8,10},{9,11},{10,... | collective-permute-start | bytes 1572872 | tf_op jit(solution)/shard_map/ppermute | solution.py:426
  76.6 4.4 %copy-start.1 = (bf16[32,8,2048]{2,1,0:T(8,128)(2,1)S(1)}, bf16[32,8,2048]{2,1,0:T(8,128)(2,1)}, u32[]{:S(2)}) copy-start(bf16[32,8,2048]{2,1,0:T(8,128)(2,1)} %shard_map.104) | copy-start | bytes 3145732
  79.9 1.8 %copy-start.6 = (f32[2048]{0:T(1024)S(1)}, f32[2048]{0:T(1024)}, u32[]{:S(2)}) copy-start(f32[2048]{0:T(1024)} %param.11) | copy-start | bytes 24580
  100.3 1.7 %copy-start.2 = (f32[256,2048]{1,0:T(8,128)S(1)}, f32[256,2048]{1,0:T(8,128)}, u32[]{:S(2)}) copy-start(f32[256,2048]{1,0:T(8,128)} %get-tuple-element.6) | copy-start | bytes 6291460
  102.0 38.3 %copy-start.4 = (bf16[16,32,128]{2,1,0:T(8,128)(2,1)S(1)}, bf16[16,32,128]{2,1,0:T(8,128)(2,1)}, u32[]{:S(2)}) copy-start(bf16[16,32,128]{2,1,0:T(8,128)(2,1)} %get-tuple-element.7) | copy-start | bytes 393220

commit v7 on v5

--- a/solution.py
+++ b/solution.py
@@ -135,8 +135,8 @@
     return ((p // 2) * 4 + zc) * 2 + p % 2
 
 
-def plane_rows(rows_ref, q):
-    return rows_ref.at[q // 2, :, q % 2]
+def plane_rows(rows_ref, q, z):
+    return rows_ref.at[q // 2, z, q % 2]
 
 
 def column_group(index):
@@ -301,15 +301,15 @@
 
 
 def _reduce_kernel(n_col, n_plane, col, plane, pick, rows_ref, x_ref, out_ref, inbox, stage, inbox2,
-                   local_sem, send_sem, recv_sem, local2_sem, send2_sem, recv2_sem):
+                   local_sem, send_sem, recv_sem, send2_sem, recv2_sem):
     index = lax.axis_index("tensor")
     cpos, ppos = col[0](index), plane[0](index)
     mesh_ids = pl.DeviceIdType.MESH
     _greet(pltpu.get_barrier_semaphore(), [(n_col, *col), (n_plane, *plane)])
 
-    def plane_copy(q, slot):
+    def plane_copy(q, z, slot):
         return pltpu.make_async_remote_copy(
-            pick(rows_ref, q), inbox.at[slot], send_sem.at[q], recv_sem.at[slot],
+            pick(rows_ref, q, z), inbox.at[z, slot], send_sem.at[z, q], recv_sem.at[z, slot],
             device_id={"tensor": plane[1](index, q)}, device_id_type=mesh_ids,
         )
 
@@ -319,50 +319,49 @@
             device_id={"tensor": col[1](index, q)}, device_id_type=mesh_ids,
         )
 
-    local = pltpu.make_async_copy(pick(rows_ref, ppos), inbox.at[ppos], local_sem)
-    local.start()
-
-    def send_plane(m, carry):
-        plane_copy((ppos + m) % n_plane, ppos).start()
-        return carry
-
-    lax.fori_loop(1, n_plane, send_plane, 0)
+    order = [(cpos + 1 + k) % n_col for k in range(n_col)]
+    locals_ = []
+    for z in order:
+        local = pltpu.make_async_copy(pick(rows_ref, ppos, z), inbox.at[z, ppos], local_sem.at[z])
+        local.start()
+        locals_.append(local)
+
+        def send_plane(m, carry, z=z):
+            plane_copy((ppos + m) % n_plane, z, ppos).start()
+            return carry
+
+        lax.fori_loop(1, n_plane, send_plane, 0)
+
+    def plane_sum(z, local):
+        def arrive(m, carry):
+            plane_copy((ppos + m) % n_plane, z, (ppos + m) % n_plane).wait_recv()
+            return carry
+
+        lax.fori_loop(1, n_plane, arrive, 0)
+        local.wait()
+        total = inbox[z, 0].astype(jnp.float32)
+        for sender in range(1, n_plane):
+            total = total + inbox[z, sender].astype(jnp.float32)
+        return total
+
+    for z, local in zip(order[:-1], locals_[:-1]):
+        stage[z] = plane_sum(z, local).astype(stage.dtype)
+        col_copy(z, cpos).start()
+
+    result = x_ref[...].astype(jnp.float32) + plane_sum(cpos, locals_[-1])
 
     def finish_plane(m, carry):
         q = (ppos + m) % n_plane
-        plane_copy(q, ppos).wait_send()
-        plane_copy(q, q).wait_recv()
+        for z in order:
+            plane_copy(q, z, ppos).wait_send()
         return carry
 
     lax.fori_loop(1, n_plane, finish_plane, 0)
-    local.wait()
-
-    total = inbox[0].astype(jnp.float32)
-    for sender in range(1, n_plane):
-        total = total + inbox[sender].astype(jnp.float32)
-    stage[...] = total.astype(stage.dtype)
-
-    local2 = pltpu.make_async_copy(stage.at[cpos], inbox2.at[cpos], local2_sem)
-    local2.start()
-
-    def send_col(k, carry):
-        col_copy((cpos + k) % n_col, cpos).start()
-        return carry
-
-    lax.fori_loop(1, n_col, send_col, 0)
-
-    def finish_col(k, carry):
-        q = (cpos + k) % n_col
-        col_copy(q, cpos).wait_send()
-        col_copy(q, q).wait_recv()
-        return carry
-
-    lax.fori_loop(1, n_col, finish_col, 0)
-    local2.wait()
-
-    result = x_ref[...].astype(jnp.float32) + inbox2[0].astype(jnp.float32)
-    for sender in range(1, n_col):
-        result = result + inbox2[sender].astype(jnp.float32)
+
+    for z in order[:-1]:
+        col_copy(z, cpos).wait_send()
+        col_copy(z, z).wait_recv()
+        result = result + inbox2[z].astype(jnp.float32)
     out_ref[...] = result
 
 
@@ -374,13 +373,12 @@
         in_specs=[pl.BlockSpec(memory_space=pltpu.VMEM)] * 2,
         out_specs=pl.BlockSpec(memory_space=pltpu.VMEM),
         scratch_shapes=[
-            pltpu.VMEM((n_plane, n_col) + block, rows.dtype),
+            pltpu.VMEM((n_col, n_plane) + block, rows.dtype),
             pltpu.VMEM((n_col,) + block, rows.dtype),
             pltpu.VMEM((n_col,) + block, rows.dtype),
-            pltpu.SemaphoreType.DMA,
-            pltpu.SemaphoreType.DMA((n_plane,)),
-            pltpu.SemaphoreType.DMA((n_plane,)),
-            pltpu.SemaphoreType.DMA,
+            pltpu.SemaphoreType.DMA((n_col,)),
+            pltpu.SemaphoreType.DMA((n_col, n_plane)),
+            pltpu.SemaphoreType.DMA((n_col, n_plane)),
             pltpu.SemaphoreType.DMA((n_col,)),
             pltpu.SemaphoreType.DMA((n_col,)),
         ],

time: 109 us -> 104 us (0.954)
  Pallas kernels: 90.4 us -> 84.5 us
    pallas_call x1, Pallas kernels: 33.1 us -> 27.2 us  [reduce_rows(): pl.pallas_call(functools.partial(_reduce_kernel, n_col, n_plane, col, pla...]
where the time goes in v7:
time: 104 us; the launch traced here: 103 us
  Pallas kernels  84.5 us (81%)
  other arithmetic  9.18 us (9%)
  matrix products  5.34 us (5%)
  local copies, waits for them, and re-layouts  3.29 us (3%)
    pallas_call x1, Pallas kernels, gather_tokens(): pl.pallas_call(functools.partial(_gather_kernel, n_col, n_plane, col, pla...  33.5 us
    pallas_call x1, Pallas kernels, reduce_rows(): pl.pallas_call(functools.partial(_reduce_kernel, n_col, n_plane, col, pla...  27.2 us
    pallas_call x1, Pallas kernels, exchange_all(): pl.pallas_call(functools.partial(_exchange_kernel, tuple(plans), work, le...  23.8 us
    dot_general x1, matrix products, shards(): jnp.dot(attended, output_weight, preferred_element_type=jnp.float32)  3.32 us
    unnamed x16, local copies, waits for them, and re-layouts  2.17 us

profile of v7, /device:TPU:1, one launch (start us, length us, event | category | flops | bytes accessed | tf_op | source)
XLA Modules:
  0.0 103.1 jit_solution(5295218692108799140)
XLA Ops:
  0.6 0.0 copy-start
  0.6 0.0 copy-start.6
  0.7 0.9 convert_reduce_fusion.1
  1.6 0.7 multiply_add_fusion
  2.3 0.8 compare_reduce_fusion
  3.1 0.1 fusion.51
  3.2 0.3 reduce-window.9
  3.5 0.1 slice.46
  3.6 0.1 slice_reduce_fusion
  3.7 0.1 fusion.52
  3.8 33.5 %shard_map.104 = bf16[32,8,2048]{2,1,0:T(8,128)(2,1)} custom-call(bf16[8,2048]{1,0:T(8,128)(2,1)} %x_ref.3), custom_call_target="tpu_custom_call" | custom-call | tf_op jit(solution)/shard_map/pallas_call | solution.py:288
  37.3 0.0 copy-start.1
  37.3 1.5 %convert_reduce_fusion = f32[32,8]{1,0:T(8,128)S(1)} fusion(bf16[32,8,2048]{2,1,0:T(8,128)(2,1)} %shard_map.104), kind=kLoop, calls=%fused_computation.1 | loop fusion | flops 1048320 | bytes 1049600 | tf_op jit(solution)/shard_map/reduce_sum | solution.py:23
  38.9 0.1 div.19
  39.0 0.0 copy-start.5
  39.0 1.6 %fusion.8 = f32[32,8]{1,0:T(8,128)S(1)} fusion(bf16[32,8,2048]{2,1,0:T(8,128)(2,1)} %shard_map.104, f32[32,8]{1,0:T(8,128)S(1)} %broadcast_multiply_fusion), kind=kLoop, calls=%fused_computation.13 | loop fusion | flops 2096896 | bytes 1050624 | tf_op jit(solution)/shard_map/reduce_sum | solution.py:25
  40.6 0.1 rsqrt.13
  40.7 0.0 copy-done
  40.7 0.0 copy-done.6
  40.7 0.0 copy-done.1
  40.8 0.5 convolution_convert_fusion.1
  41.3 0.0 copy-done.5
  41.3 1.4 %fusion.6.refs_2_ = bf16[256,2048]{1,0:T(8,128)(2,1)} fusion(bf16[32,8,2048]{2,1,0:T(8,128)(2,1)S(1)} %copy-done.1, f32[2048]{0:T(1024)S(1)} %copy-done.5, f32[256]{0:T(256)S(1)} %rsqrt.13, f32[256]{0:T(256)S(1)} %div.19), kind=kLoop, calls=%fused_computation.11 | loop fusion | flops 2621440 | bytes 2107392 | tf_op jit(solution)/shard_map/convert_element_type | solution.py:26
  42.7 0.1 slice_convert_fusion.1
  42.8 0.6 fusion.33
  43.4 0.1 fusion.57
  43.5 0.0 copy-start.4
  43.5 0.7 pad_maximum_fusion
  44.3 0.2 convolution_convert_fusion
  44.5 0.7 reshape.106.refs_1_
  45.2 0.0 copy-start.2
  45.2 23.8 %shard_map.105 = (bf16[4,256,128]{2,1,0:T(8,128)(2,1)}, bf16[16,32,128]{2,1,0:T(8,128)(2,1)}, f32[256,2048]{1,0:T(8,128)}) custom-call(bf16[1,256,128]{2,1,0:T(8,128)(2,1)} %get-tuple-element.18.refs_0_, bf16[16,32,128]{2,1,0:T(8,128)(2,1)} %reshape.106.refs_1_, bf16[256,2048]{1,0:T(8,128)(2,1)} %fusion.6.refs_2_, bf16[2048,256]{1,0:T(8,128)(2,1)} %refs_3_.1, ...), custom_call_target="tpu_custom_call" | custom-call | tf_op jit(solution)/shard_map/pallas_call | solution.py:164
  69.0 0.0 copy-done.4
  69.0 1.3 %select_reduce_fusion = (f32[256]{0:T(256)S(1)}, f32[256,256]{0,1:T(8,128)S(1)}) fusion(s32[256]{0:T(256)S(1)} %bitcast.49, bf16[4,256,128]{2,1,0:T(8,128)(2,1)} %get-tuple-element.5), kind=kOutput, calls=%fused_computation.25 | convolution fusion | flops 33947392 | bytes 789504 | tf_op jit(solution)/shard_map/dot_general | solution.py:467
  70.3 0.1 fusion.28
  70.4 0.0 copy-done.2
  70.5 0.0 copy-start.3
  70.5 3.3 %fusion = bf16[256,2048]{1,0:T(8,128)(2,1)} fusion(f32[256,2048]{1,0:T(8,128)} %get-tuple-element.6, bf16[64,2048]{1,0:T(8,128)(2,1)S(1)} %copy-done.2, f32[256,256]{0,1:T(8,128)S(1)} %get-tuple-element.22, f32[256]{0:T(256)S(1)} %get-tuple-element.21, s32[256]{0:T(256)S(1)} %bitcast.51, f32[256]{0:T(256)S(1)} %fusion.28, ...), kind=kOutput, calls=%fused_computation.4 | convolution fusion | flops 76972032 | bytes 3739648 | tf_op jit(solution)/shard_map/dot_general | solution.py:476
  73.8 27.2 %shard_map.106 = f32[8,2048]{1,0:T(8,128)} custom-call(bf16[4,4,2,8,2048]{4,3,2,1,0:T(8,128)(2,1)} %bitcast.47, bf16[8,2048]{1,0:T(8,128)(2,1)} %x_ref.3), custom_call_target="tpu_custom_call" | custom-call | tf_op jit(solution)/shard_map/pallas_call | solution.py:370
  101.0 1.5 %copy.29 = f32[8,2048]{1,0:T(8,128)} copy(f32[8,2048]{1,0:T(8,128)} %shard_map.106) | data formatting | bytes 131072
  102.5 0.0 copy-done.3
  102.5 0.7 copy.30
  (5 shorter events, 0.1 us)
Async XLA Ops:
  0.6 40.1 %copy-start = (bf16[2048,192]{0,1:T(8,128)(2,1)S(1)}, bf16[2048,192]{0,1:T(8,128)(2,1)}, u32[]{:S(2)}) copy-start(bf16[2048,192]{0,1:T(8,128)(2,1)} %param.12) | copy-start | bytes 2359300
  0.6 40.1 %copy-start.6 = (f32[2048]{0:T(1024)S(1)}, f32[2048]{0:T(1024)}, u32[]{:S(2)}) copy-start(f32[2048]{0:T(1024)} %param.10) | copy-start | bytes 24580
  37.3 3.4 %copy-start.1 = (bf16[32,8,2048]{2,1,0:T(8,128)(2,1)S(1)}, bf16[32,8,2048]{2,1,0:T(8,128)(2,1)}, u32[]{:S(2)}) copy-start(bf16[32,8,2048]{2,1,0:T(8,128)(2,1)} %shard_map.104) | copy-start | bytes 3145732
  39.0 2.3 %copy-start.5 = (f32[2048]{0:T(1024)S(1)}, f32[2048]{0:T(1024)}, u32[]{:S(2)}) copy-start(f32[2048]{0:T(1024)} %param.11) | copy-start | bytes 24580
  43.5 25.5 %copy-start.4 = (s32[1,256]{1,0:T(1,128)S(1)}, s32[1,256]{1,0:T(1,128)}, u32[]{:S(2)}) copy-start(s32[1,256]{1,0:T(1,128)} %param.16) | copy-start | bytes 3076
  45.2 25.3 %copy-start.2 = (bf16[64,2048]{1,0:T(8,128)(2,1)S(1)}, bf16[64,2048]{1,0:T(8,128)(2,1)}, u32[]{:S(2)}) copy-start(bf16[64,2048]{1,0:T(8,128)(2,1)} %param.13) | copy-start | bytes 786436
  70.5 32.0 %copy-start.3 = (bf16[16,32,128]{2,1,0:T(8,128)(2,1)S(1)}, bf16[16,32,128]{2,1,0:T(8,128)(2,1)}, u32[]{:S(2)}) copy-start(bf16[16,32,128]{2,1,0:T(8,128)(2,1)} %get-tuple-element.7) | copy-start | bytes 393220

commit v8 on v7

--- a/solution.py
+++ b/solution.py
@@ -93,6 +93,7 @@
             src_ref.at[0] if shared else src_ref.at[pos], out_ref.at[pos], local_sem
         )
         steps.append((n, pos, peer_copy, local))
+    carried = work[0](*inputs) if work is not None else None
     pl.semaphore_wait(barrier, sum(plan[1] - 1 for plan in plans))
 
     for n, pos, peer_copy, local in steps:
@@ -105,7 +106,7 @@
         lax.fori_loop(1, n, send, 0)
 
     if work is not None:
-        work(*inputs, *results)
+        work[1](carried, *inputs, *results)
 
     for n, pos, peer_copy, local in steps:
 
@@ -175,13 +176,16 @@
     return exchange_all(collective_id, (blocks, axis, n, shared, group))[0]
 
 
-def _feedforward(normed_ref, upward_ref, downward_ref, out_ref):
+def _feedforward_up(normed_ref, upward_ref, downward_ref):
     upward = jnp.dot(normed_ref[...], upward_ref[...], preferred_element_type=jnp.float32)
-    hidden = (0.5 * upward * (1.0 + lax.erf(upward * math.sqrt(0.5)))).astype(jnp.bfloat16)
+    return (0.5 * upward * (1.0 + lax.erf(upward * math.sqrt(0.5)))).astype(jnp.bfloat16)
+
+
+def _feedforward_down(hidden, normed_ref, upward_ref, downward_ref, out_ref):
     out_ref[...] = jnp.dot(hidden, downward_ref[...], preferred_element_type=jnp.float32)
 
 
-def _greet(barrier, groups):
+def _greet(barrier, groups, extra=0):
     index = lax.axis_index("tensor")
     total = 0
     for n, position, member in groups:
@@ -198,7 +202,7 @@
 
         lax.fori_loop(1, n, greet, 0)
         total += n - 1
-    pl.semaphore_wait(barrier, total)
+    pl.semaphore_wait(barrier, total + extra)
 
 
 def _gather_kernel(n_col, n_plane, col, plane, slot, x_ref, out_ref, local_sem, send_sem, relay_sem, recv_sem):
@@ -300,12 +304,37 @@
     )(x)
 
 
-def _reduce_kernel(n_col, n_plane, col, plane, pick, rows_ref, x_ref, out_ref, inbox, stage, inbox2,
-                   local_sem, send_sem, recv_sem, send2_sem, recv2_sem):
+def _reduce_kernel(n_col, n_plane, n_dp, col, plane, pick, rows_ref, x_ref, pages_ref, out_ref,
+                   pages_out, inbox, stage, inbox2, local_sem, send_sem, recv_sem, send2_sem, recv2_sem,
+                   page_local_sem, page_send_sem, page_recv_sem):
     index = lax.axis_index("tensor")
     cpos, ppos = col[0](index), plane[0](index)
     mesh_ids = pl.DeviceIdType.MESH
-    _greet(pltpu.get_barrier_semaphore(), [(n_col, *col), (n_plane, *plane)])
+    barrier = pltpu.get_barrier_semaphore()
+    group = lax.axis_index("dp")
+
+    def page_copy(g, slot):
+        return pltpu.make_async_remote_copy(
+            pages_ref.at[g], pages_out.at[slot], page_send_sem.at[g], page_recv_sem.at[slot],
+            device_id={"dp": g}, device_id_type=mesh_ids,
+        )
+
+    def greet_group(k, carry):
+        pl.semaphore_signal(
+            barrier, inc=1, device_id={"dp": (group + k) % n_dp}, device_id_type=mesh_ids
+        )
+        return carry
+
+    lax.fori_loop(1, n_dp, greet_group, 0)
+    _greet(barrier, [(n_col, *col), (n_plane, *plane)], extra=n_dp - 1)
+    page_local = pltpu.make_async_copy(pages_ref.at[group], pages_out.at[group], page_local_sem)
+    page_local.start()
+
+    def send_pages(k, carry):
+        page_copy((group + k) % n_dp, group).start()
+        return carry
+
+    lax.fori_loop(1, n_dp, send_pages, 0)
 
     def plane_copy(q, z, slot):
         return pltpu.make_async_remote_copy(
@@ -364,14 +393,27 @@
         result = result + inbox2[z].astype(jnp.float32)
     out_ref[...] = result
 
-
-def reduce_rows(rows, x, col, plane, pick, n_col, n_plane, collective_id):
+    def finish_pages(k, carry):
+        g = (group + k) % n_dp
+        page_copy(g, group).wait_send()
+        page_copy(g, g).wait_recv()
+        return carry
+
+    lax.fori_loop(1, n_dp, finish_pages, 0)
+    page_local.wait()
+
+
+def reduce_rows(rows, x, pages, col, plane, pick, n_col, n_plane, collective_id):
     block = x.shape
+    n_dp = pages.shape[0]
     return pl.pallas_call(
-        functools.partial(_reduce_kernel, n_col, n_plane, col, plane, pick),
-        out_shape=jax.ShapeDtypeStruct(block, jnp.float32),
-        in_specs=[pl.BlockSpec(memory_space=pltpu.VMEM)] * 2,
-        out_specs=pl.BlockSpec(memory_space=pltpu.VMEM),
+        functools.partial(_reduce_kernel, n_col, n_plane, n_dp, col, plane, pick),
+        out_shape=(
+            jax.ShapeDtypeStruct(block, jnp.float32),
+            jax.ShapeDtypeStruct(pages.shape, pages.dtype),
+        ),
+        in_specs=[pl.BlockSpec(memory_space=pltpu.VMEM)] * 3,
+        out_specs=(pl.BlockSpec(memory_space=pltpu.VMEM), pl.BlockSpec(memory_space=pltpu.VMEM)),
         scratch_shapes=[
             pltpu.VMEM((n_col, n_plane) + block, rows.dtype),
             pltpu.VMEM((n_col,) + block, rows.dtype),
@@ -381,9 +423,12 @@
             pltpu.SemaphoreType.DMA((n_col, n_plane)),
             pltpu.SemaphoreType.DMA((n_col,)),
             pltpu.SemaphoreType.DMA((n_col,)),
+            pltpu.SemaphoreType.DMA,
+            pltpu.SemaphoreType.DMA((n_dp,)),
+            pltpu.SemaphoreType.DMA((n_dp,)),
         ],
         compiler_params=pltpu.CompilerParams(collective_id=collective_id, has_side_effects=True),
-    )(rows, x)
+    )(rows, x, pages)
 
 
 def shards(
@@ -453,11 +498,10 @@
     ).astype(jnp.bfloat16)
     outgoing = jnp.dot(placing, page_rows, preferred_element_type=jnp.float32).astype(jnp.bfloat16)
     outgoing = outgoing.reshape(replica_count, capacity * PAGE, 2 * quarter_width)
-    head_pieces, incoming, feedforward = exchange_all(
+    head_pieces, feedforward = exchange_all(
         1,
         (jnp.concatenate([query_piece, key_piece], 1)[None], "tensor", quarters, True, None),
-        (outgoing, "dp", replica_count, False, None),
-        work=_feedforward,
+        work=(_feedforward_up, _feedforward_down),
         inputs=(normed_feedforward, upward_weight, downward_weight),
         results=(jax.ShapeDtypeStruct((tokens_total, width), jnp.float32),),
     )
@@ -475,9 +519,10 @@
     partial = (
         jnp.dot(attended, output_weight, preferred_element_type=jnp.float32) + feedforward
     ).astype(jnp.bfloat16)
-    layer_output = reduce_rows(
+    layer_output, incoming = reduce_rows(
         partial.reshape(4, planes, 2, local_rows, width),
         hidden_states,
+        outgoing,
         (column_group, column_member),
         (plane_group, plane_member),
         plane_rows,

time: 104 us -> 100 us (0.962)
  other arithmetic: 9.18 us -> 7.03 us
  Pallas kernels: 84.5 us -> 82.5 us
    pallas_call x1, Pallas kernels: 23.8 us -> 22.1 us  [exchange_all(): pl.pallas_call(functools.partial(_exchange_kernel, tuple(plans), work, le...]
where the time goes in v8:
time: 100 us; the launch traced here: 99.8 us
  Pallas kernels  82.5 us (82%)
  other arithmetic  7.03 us (7%)
  matrix products  5.31 us (5%)
  local copies, waits for them, and re-layouts  4.2 us (4%)
    pallas_call x1, Pallas kernels, gather_tokens(): pl.pallas_call(functools.partial(_gather_kernel, n_col, n_plane, col, pla...  33.6 us
    pallas_call x1, Pallas kernels, reduce_rows(): pl.pallas_call(functools.partial(_reduce_kernel, n_col, n_plane, n_dp, co...  26.8 us
    pallas_call x1, Pallas kernels, exchange_all(): pl.pallas_call(functools.partial(_exchange_kernel, tuple(plans), work, le...  22.1 us
    dot_general x1, matrix products, shards(): jnp.dot(attended, output_weight, preferred_element_type=jnp.float32)  3.3 us
    unnamed x16, local copies, waits for them, and re-layouts  3.08 us

profile of v8, /device:TPU:1, one launch (start us, length us, event | category | flops | bytes accessed | tf_op | source)
XLA Modules:
  0.0 99.8 jit_solution(6473714131780158650)
XLA Ops:
  0.6 0.0 copy-start
  0.6 0.0 copy-start.5
  0.7 33.6 %shard_map.104 = bf16[32,8,2048]{2,1,0:T(8,128)(2,1)} custom-call(bf16[8,2048]{1,0:T(8,128)(2,1)} %x_ref.3), custom_call_target="tpu_custom_call" | custom-call | tf_op jit(solution)/shard_map/pallas_call | solution.py:292
  34.3 0.0 copy-start.1
  34.3 1.5 %convert_reduce_fusion = f32[32,8]{1,0:T(8,128)S(1)} fusion(bf16[32,8,2048]{2,1,0:T(8,128)(2,1)} %shard_map.104), kind=kLoop, calls=%fused_computation.1 | loop fusion | flops 1048320 | bytes 1049600 | tf_op jit(solution)/shard_map/reduce_sum | solution.py:23
  35.9 1.6 %fusion.8 = f32[32,8]{1,0:T(8,128)S(1)} fusion(bf16[32,8,2048]{2,1,0:T(8,128)(2,1)} %shard_map.104, f32[32,8]{1,0:T(8,128)S(1)} %broadcast_multiply_fusion), kind=kLoop, calls=%fused_computation.13 | loop fusion | flops 2096896 | bytes 1050624 | tf_op jit(solution)/shard_map/reduce_sum | solution.py:25
  37.5 0.0 copy-start.3
  37.5 0.1 rsqrt.13
  37.6 0.1 div.19
  37.7 0.0 copy-done
  37.7 0.0 copy-done.5
  37.7 0.0 copy-done.1
  37.7 0.0 copy-start.4
  37.7 0.5 convolution_convert_fusion.1
  38.3 0.1 slice_convert_fusion.1
  38.4 0.0 copy-done.3
  38.4 0.1 compare_reduce_fusion
  38.5 0.1 fusion.51
  38.5 0.3 reduce-window.9
  38.9 0.1 slice.46
  39.0 0.1 slice_reduce_fusion
  39.1 0.1 fusion.52
  39.2 0.6 fusion.33
  39.8 0.1 fusion.57
  39.9 0.7 pad_maximum_fusion
  40.7 0.0 copy-done.4
  40.7 1.4 %fusion.6.refs_1_ = bf16[256,2048]{1,0:T(8,128)(2,1)} fusion(bf16[32,8,2048]{2,1,0:T(8,128)(2,1)S(1)} %copy-done.1, f32[2048]{0:T(1024)S(1)} %copy-done.4, f32[256]{0:T(256)S(1)} %rsqrt.13, f32[256]{0:T(256)S(1)} %div.19), kind=kLoop, calls=%fused_computation.11 | loop fusion | flops 2621440 | bytes 2107392 | tf_op jit(solution)/shard_map/convert_element_type | solution.py:26
  42.0 0.0 copy-start.2
  42.0 22.1 %shard_map.105 = (bf16[4,256,128]{2,1,0:T(8,128)(2,1)}, f32[256,2048]{1,0:T(8,128)}) custom-call(bf16[1,256,128]{2,1,0:T(8,128)(2,1)} %get-tuple-element.20.refs_0_, bf16[256,2048]{1,0:T(8,128)(2,1)} %fusion.6.refs_1_, bf16[2048,256]{1,0:T(8,128)(2,1)} %refs_2_.1, bf16[256,2048]{1,0:T(8,128)(2,1)} %refs_3_.1), custom_call_target="tpu_custom_call" | custom-call | tf_op jit(solution)/shard_map/pallas_call | solution.py:165
  64.1 1.3 %select_reduce_fusion = (f32[256]{0:T(256)S(1)}, f32[256,256]{0,1:T(8,128)S(1)}) fusion(s32[256]{0:T(256)S(1)} %bitcast.49, bf16[4,256,128]{2,1,0:T(8,128)(2,1)} %get-tuple-element.6), kind=kOutput, calls=%fused_computation.25 | convolution fusion | flops 33947392 | bytes 789504 | tf_op jit(solution)/shard_map/dot_general | solution.py:511
  65.5 0.0 copy-start.6
  65.5 0.1 fusion.28
  65.6 0.0 copy-done.2
  65.6 3.3 %fusion = bf16[256,2048]{1,0:T(8,128)(2,1)} fusion(f32[256,2048]{1,0:T(8,128)} %get-tuple-element.7, bf16[64,2048]{1,0:T(8,128)(2,1)S(1)} %copy-done.2, f32[256,256]{0,1:T(8,128)S(1)} %get-tuple-element.24, f32[256]{0:T(256)S(1)} %get-tuple-element.23, s32[256]{0:T(256)S(1)} %bitcast.51, f32[256]{0:T(256)S(1)} %fusion.28, ...), kind=kOutput, calls=%fused_computation.4 | convolution fusion | flops 76972032 | bytes 3739648 | tf_op jit(solution)/shard_map/dot_general | solution.py:520
  68.9 0.0 copy-done.6
  68.9 0.2 convert_reduce_fusion.1
  69.1 0.2 convolution_convert_fusion
  69.3 0.7 reshape.107.pages_ref
  70.0 26.8 %shard_map.106 = (f32[8,2048]{1,0:T(8,128)}, bf16[16,32,128]{2,1,0:T(8,128)(2,1)}) custom-call(bf16[4,4,2,8,2048]{4,3,2,1,0:T(8,128)(2,1)} %bitcast.47, bf16[8,2048]{1,0:T(8,128)(2,1)} %x_ref.3, bf16[16,32,128]{2,1,0:T(8,128)(2,1)} %reshape.107.pages_ref), custom_call_target="tpu_custom_call" | custom-call | tf_op jit(solution)/shard_map/pallas_call | solution.py:409
  96.8 1.5 %copy.29 = f32[8,2048]{1,0:T(8,128)} copy(f32[8,2048]{1,0:T(8,128)} %get-tuple-element.27) | data formatting | bytes 131072
  98.3 1.6 %copy.30 = bf16[1,16,2,16,128]{4,3,2,1,0:T(8,128)(2,1)} copy(bf16[1,16,2,16,128]{4,3,2,1,0:T(8,128)(2,1)} %bitcast.48) | data formatting | bytes 262144
  (6 shorter events, 0.1 us)
Async XLA Ops:
  0.6 37.1 %copy-start = (bf16[2048,192]{0,1:T(8,128)(2,1)S(1)}, bf16[2048,192]{0,1:T(8,128)(2,1)}, u32[]{:S(2)}) copy-start(bf16[2048,192]{0,1:T(8,128)(2,1)} %param.12) | copy-start | bytes 2359300
  0.6 37.1 %copy-start.5 = (f32[2048]{0:T(1024)S(1)}, f32[2048]{0:T(1024)}, u32[]{:S(2)}) copy-start(f32[2048]{0:T(1024)} %param.10) | copy-start | bytes 24580
  34.3 3.4 %copy-start.1 = (bf16[32,8,2048]{2,1,0:T(8,128)(2,1)S(1)}, bf16[32,8,2048]{2,1,0:T(8,128)(2,1)}, u32[]{:S(2)}) copy-start(bf16[32,8,2048]{2,1,0:T(8,128)(2,1)} %shard_map.104) | copy-start | bytes 3145732
  37.5 0.9 copy-start.3
  37.7 2.9 %copy-start.4 = (f32[2048]{0:T(1024)S(1)}, f32[2048]{0:T(1024)}, u32[]{:S(2)}) copy-start(f32[2048]{0:T(1024)} %param.11) | copy-start | bytes 24580
  42.0 23.6 %copy-start.2 = (bf16[64,2048]{1,0:T(8,128)(2,1)S(1)}, bf16[64,2048]{1,0:T(8,128)(2,1)}, u32[]{:S(2)}) copy-start(bf16[64,2048]{1,0:T(8,128)(2,1)} %param.13) | copy-start | bytes 786436
  65.5 3.5 %copy-start.6 = (s32[16,1]{0,1:T(1,128)S(1)}, s32[16,1]{0,1:T(1,128)}, u32[]{:S(2)}) copy-start(s32[16,1]{0,1:T(1,128)} %param.17) | copy-start | bytes 196

commit v9 on v8

--- a/solution.py
+++ b/solution.py
@@ -183,6 +183,100 @@
 
 def _feedforward_down(hidden, normed_ref, upward_ref, downward_ref, out_ref):
     out_ref[...] = jnp.dot(hidden, downward_ref[...], preferred_element_type=jnp.float32)
+
+
+def _head_kernel(n, tokens_ref, gain_a_ref, gain_f_ref, wq_ref, wk_ref, wv_ref, cos_ref, sin_ref,
+                 turn_ref, up_ref, down_ref, pieces_ref, key_ref, value_ref, ff_ref, held_ref, normed_ref,
+                 local_sem, send_sem, recv_sem):
+    index = lax.axis_index("tensor")
+    pos = index % n
+    base = index - pos
+    mesh_ids = pl.DeviceIdType.MESH
+    barrier = pltpu.get_barrier_semaphore()
+
+    def greet(k, carry):
+        pl.semaphore_signal(
+            barrier, inc=1, device_id={"tensor": base + (pos + k) % n}, device_id_type=mesh_ids
+        )
+        return carry
+
+    lax.fori_loop(1, n, greet, 0)
+
+    floats = tokens_ref[...].astype(jnp.float32)
+    center = jnp.mean(floats, axis=-1, keepdims=True)
+    shifted = floats - center
+    spread = jnp.mean(shifted * shifted, axis=-1, keepdims=True)
+    scale = lax.rsqrt(spread + epsilon)
+    normed = (shifted * scale * gain_a_ref[...]).astype(jnp.bfloat16)
+    normed_ref[...] = (shifted * scale * gain_f_ref[...]).astype(jnp.bfloat16)
+
+    def project(w_ref):
+        return jnp.dot(normed, w_ref[...], preferred_element_type=jnp.float32).astype(jnp.bfloat16)
+
+    def rotate(piece):
+        turned = jnp.dot(piece, turn_ref[...], preferred_element_type=jnp.float32)
+        rotated = piece.astype(jnp.float32) * cos_ref[...] + turned * sin_ref[...]
+        return jnp.where(pos == 0, rotated.astype(jnp.bfloat16), piece)
+
+    held_ref[0] = rotate(project(wq_ref))
+    key = rotate(project(wk_ref))
+    held_ref[1] = key
+    key_ref[...] = key
+    value_ref[...] = project(wv_ref)
+    pl.semaphore_wait(barrier, n - 1)
+
+    def peer_copy(q, slot):
+        return pltpu.make_async_remote_copy(
+            held_ref, pieces_ref.at[slot], send_sem.at[q], recv_sem.at[slot],
+            device_id={"tensor": base + q}, device_id_type=mesh_ids,
+        )
+
+    local = pltpu.make_async_copy(held_ref, pieces_ref.at[pos], local_sem)
+    local.start()
+
+    def send(k, carry):
+        peer_copy((pos + k) % n, pos).start()
+        return carry
+
+    lax.fori_loop(1, n, send, 0)
+
+    upward = jnp.dot(normed_ref[...], up_ref[...], preferred_element_type=jnp.float32)
+    hidden = (0.5 * upward * (1.0 + lax.erf(upward * math.sqrt(0.5)))).astype(jnp.bfloat16)
+    ff_ref[...] = jnp.dot(hidden, down_ref[...], preferred_element_type=jnp.float32)
+
+    def finish(k, carry):
+        q = (pos + k) % n
+        peer_copy(q, pos).wait_send()
+        peer_copy(q, q).wait_recv()
+        return carry
+
+    lax.fori_loop(1, n, finish, 0)
+    local.wait()
+
+
+def head_stage(n, tokens, gains, weights, cosine, sine, turn, upward_weight, downward_weight):
+    rows = tokens.shape[0]
+    width = weights[0].shape[1]
+    operands = (tokens, *gains, *weights, cosine, sine, turn, upward_weight, downward_weight)
+    return pl.pallas_call(
+        functools.partial(_head_kernel, n),
+        out_shape=(
+            jax.ShapeDtypeStruct((n, 2, rows, width), jnp.bfloat16),
+            jax.ShapeDtypeStruct((rows, width), jnp.bfloat16),
+            jax.ShapeDtypeStruct((rows, width), jnp.bfloat16),
+            jax.ShapeDtypeStruct((rows, downward_weight.shape[1]), jnp.float32),
+        ),
+        in_specs=[pl.BlockSpec(memory_space=pltpu.VMEM)] * len(operands),
+        out_specs=tuple(pl.BlockSpec(memory_space=pltpu.VMEM) for _ in range(4)),
+        scratch_shapes=[
+            pltpu.VMEM((2, rows, width), jnp.bfloat16),
+            pltpu.VMEM(tokens.shape, jnp.bfloat16),
+            pltpu.SemaphoreType.DMA,
+            pltpu.SemaphoreType.DMA((n,)),
+            pltpu.SemaphoreType.DMA((n,)),
+        ],
+        compiler_params=pltpu.CompilerParams(collective_id=1, has_side_effects=True),
+    )(*operands)
 
 
 def _greet(barrier, groups, extra=0):
@@ -464,20 +558,37 @@
         0,
     )
     tokens = gathered.reshape(tokens_total, width)
-    normed_attention = layer_norm(tokens, attention_gain)
-    normed_feedforward = layer_norm(tokens, feedforward_gain)
-    joined = jnp.dot(normed_attention, heads_weight, preferred_element_type=jnp.float32).astype(
-        jnp.bfloat16
-    )
-
     indices, starting = positions_of(stream)
     offsets = indices - starting
-    query_piece = joined[:, :quarter_width]
-    key_piece = joined[:, quarter_width : 2 * quarter_width]
-    value_piece = joined[:, 2 * quarter_width :]
-    leading = quarter_index == 0
-    query_piece = jnp.where(leading, rotate_leading(query_piece, offsets, ROT), query_piece)
-    key_piece = jnp.where(leading, rotate_leading(key_piece, offsets, ROT), key_piece)
+    half = ROT // 2
+    frequency = jnp.exp(
+        jnp.arange(half, dtype=jnp.float32) * (-2.0 * math.log(rotary_base) / ROT)
+    )
+    angles = offsets.astype(jnp.float32)[:, None] * frequency[None, :]
+    cosine = jnp.tile(jnp.cos(angles), (1, 2))
+    sine = jnp.tile(jnp.sin(angles), (1, 2))
+    lanes = jnp.arange(quarter_width)
+    turn = (
+        jnp.where(lanes[:, None] == lanes[None, :] + half, -1.0, 0.0)
+        + jnp.where(lanes[:, None] + half == lanes[None, :], 1.0, 0.0)
+    ).astype(jnp.bfloat16)
+    pieces, key_piece, value_piece, feedforward = head_stage(
+        quarters,
+        tokens,
+        (attention_gain[None], feedforward_gain[None]),
+        (
+            heads_weight[:, :quarter_width],
+            heads_weight[:, quarter_width : 2 * quarter_width],
+            heads_weight[:, 2 * quarter_width :],
+        ),
+        cosine,
+        sine,
+        turn,
+        upward_weight,
+        downward_weight,
+    )
+    queries = pieces[:, 0].transpose(1, 0, 2).reshape(tokens_total, HD)
+    keys = pieces[:, 1].transpose(1, 0, 2).reshape(tokens_total, HD)
 
     page_count = tokens_total // PAGE
     page_rows = jnp.concatenate([key_piece, value_piece], 1).reshape(
@@ -498,16 +609,6 @@
     ).astype(jnp.bfloat16)
     outgoing = jnp.dot(placing, page_rows, preferred_element_type=jnp.float32).astype(jnp.bfloat16)
     outgoing = outgoing.reshape(replica_count, capacity * PAGE, 2 * quarter_width)
-    head_pieces, feedforward = exchange_all(
-        1,
-        (jnp.concatenate([query_piece, key_piece], 1)[None], "tensor", quarters, True, None),
-        work=(_feedforward_up, _feedforward_down),
-        inputs=(normed_feedforward, upward_weight, downward_weight),
-        results=(jax.ShapeDtypeStruct((tokens_total, width), jnp.float32),),
-    )
-    queries = head_pieces[:, :, :quarter_width].transpose(1, 0, 2).reshape(tokens_total, HD)
-    keys = head_pieces[:, :, quarter_width:].transpose(1, 0, 2).reshape(tokens_total, HD)
-
     scores = jnp.dot(queries, keys.T, preferred_element_type=jnp.float32) * HD ** (-0.5)
     allowed = (stream[None, :] == stream[:, None]) & (indices[None, :] <= indices[:, None])
     peak = jnp.max(jnp.where(allowed, scores, -jnp.inf), axis=1, keepdims=True)

time: 100 us -> 113 us (1.13)
  Pallas kernels: 82.5 us -> 94.2 us
  local copies, waits for them, and re-layouts: 4.2 us -> 9.7 us
  other arithmetic: 7.03 us -> 2.65 us
    pallas_call x1, Pallas kernels: 22.1 us -> 34.1 us  [head_stage(): pl.pallas_call(functools.partial(_head_kernel, n), out_shape=(jax.ShapeDt...]
    reduce_sum x2 -> x0, other arithmetic: 3.17 us -> none  [the longest x1 1.64 us: layer_norm(): spread = jnp.mean(shifted * shifted, axis=-1, keepdims=True)]
    unnamed x16 -> x15, local copies, waits for them, and re-layouts: 3.08 us -> 6.09 us
    another operation x1 -> x5, local copies, waits for them, and re-layouts: 0.12 us -> 1.62 us  [the longest x2 0.76 us: shards(): cosine = jnp.tile(jnp.cos(angles), (1, 2))]
    slice x1 -> x2, local copies, waits for them, and re-layouts: 0.07 us -> 1.23 us  [the longest x1 1.16 us: shards(): heads_weight[:, 2 * quarter_width:]]
where the time goes in v9:
time: 113 us; the launch traced here: 112 us
  Pallas kernels  94.2 us (83%)
  local copies, waits for them, and re-layouts  9.7 us (9%)
  matrix products  4.81 us (4%)
  other arithmetic  2.65 us (2%)
    pallas_call x1, Pallas kernels, head_stage(): pl.pallas_call(functools.partial(_head_kernel, n), out_shape=(jax.ShapeDt...  34.1 us
    pallas_call x1, Pallas kernels, gather_tokens(): pl.pallas_call(functools.partial(_gather_kernel, n_col, n_plane, col, pla...  33.5 us
    pallas_call x1, Pallas kernels, reduce_rows(): pl.pallas_call(functools.partial(_reduce_kernel, n_col, n_plane, n_dp, co...  26.6 us
    unnamed x15, local copies, waits for them, and re-layouts  6.09 us
    dot_general x1, matrix products, shards(): jnp.dot(attended, output_weight, preferred_element_type=jnp.float32)  3.33 us

profile of v9, /device:TPU:1, one launch (start us, length us, event | category | flops | bytes accessed | tf_op | source)
XLA Modules:
  0.0 112.2 jit_solution(2620653835894093422)
XLA Ops:
  0.6 0.0 copy-start
  0.6 0.8 compare_reduce_fusion
  1.5 0.1 fusion.23
  1.6 0.3 reduce-window.9
  1.9 0.1 slice.35
  2.0 0.1 slice_reduce_fusion
  2.1 0.1 fusion.24
  2.2 0.2 multiply_sine_fusion
  2.4 0.8 copy.26.cos_ref
  3.2 0.7 copy.27.sin_ref
  3.9 1.2 %fusion.27 = (bf16[2048,64]{0,1:T(8,128)(2,1)S(1)}, bf16[2048,64]{0,1:T(8,128)(2,1)S(1)}, bf16[2048,64]{0,1:T(8,128)(2,1)S(1)}) fusion(bf16[2048,192]{0,1:T(8,128)(2,1)} %param.12), kind=kLoop, calls=%fused_computation.43 | loop fusion | bytes 1572864 | tf_op jit(solution)/shard_map/slice | solution.py:582
  5.1 1.0 copy.32.wq_ref
  6.1 1.0 copy.33.wk_ref
  7.1 1.0 copy.34.wv_ref
  8.1 33.5 %shard_map.104 = bf16[32,8,2048]{2,1,0:T(8,128)(2,1)} custom-call(bf16[8,2048]{1,0:T(8,128)(2,1)} %x_ref.3), custom_call_target="tpu_custom_call" | custom-call | tf_op jit(solution)/shard_map/pallas_call | solution.py:386
  41.6 0.7 add_convert_fusion.turn_ref
  42.3 0.0 copy-start.3
  42.3 34.1 %shard_map.105 = (bf16[4,2,256,64]{3,2,1,0:T(8,128)(2,1)}, bf16[256,64]{1,0:T(8,128)(2,1)}, bf16[256,64]{1,0:T(8,128)(2,1)}, f32[256,2048]{1,0:T(8,128)}) custom-call(bf16[256,2048]{1,0:T(8,128)(2,1)} %bitcast.40, f32[1,2048]{1,0:T(1,128)} %bitcast.47, f32[1,2048]{1,0:T(1,128)} %bitcast.48, bf16[2048,64]{1,0:T(8,128)(2,1)} %copy.32.wq_ref, ...), custom_call_target="tpu_custom_call" | custom-call | tf_op jit(solution)/shard_map/pallas_call | solution.py:261
  76.4 0.0 copy-done.3
  76.4 1.3 %select_reduce_fusion = (f32[256]{0:T(256)S(1)}, f32[256,256]{0,1:T(8,128)S(1)}) fusion(s32[256]{0:T(256)S(1)} %bitcast.44, bf16[4,2,256,64]{3,2,1,0:T(8,128)(2,1)} %get-tuple-element.8), kind=kOutput, calls=%fused_computation.10 | convolution fusion | flops 33947392 | bytes 527360 | tf_op jit(solution)/shard_map/dot_general | solution.py:612
  77.7 0.0 copy-start.1
  77.8 0.0 copy-start.2
  77.8 0.1 fusion.8
  77.9 0.0 copy-start.4
  77.9 0.0 copy-done
  77.9 3.3 %fusion = bf16[256,2048]{1,0:T(8,128)(2,1)} fusion(f32[256,2048]{1,0:T(8,128)} %get-tuple-element.10, bf16[64,2048]{1,0:T(8,128)(2,1)S(1)} %copy-done, bf16[256,64]{1,0:T(8,128)(2,1)} %get-tuple-element.9, f32[256,256]{0,1:T(8,128)S(1)} %get-tuple-element.20, f32[256]{0:T(256)S(1)} %get-tuple-element.19, s32[256]{0:T(256)S(1)} %bitcast.46, f32[256]{0:T(256)S(1)} %fusion.8), kind=kOutput, calls=%fused_computation.1 | convolution fusion | flops 76972032 | bytes 3705856 | tf_op jit(solution)/shard_map/dot_general | solution.py:621
  81.2 0.0 copy-done.1
  81.2 0.0 copy-done.2
  81.2 0.1 pad_maximum_fusion
  81.4 0.0 copy-done.4
  81.4 0.2 convert_reduce_fusion
  81.6 0.2 convolution_convert_fusion
  81.7 0.7 reshape.143.pages_ref
  82.5 26.6 %shard_map.106 = (f32[8,2048]{1,0:T(8,128)}, bf16[16,32,128]{2,1,0:T(8,128)(2,1)}) custom-call(bf16[4,4,2,8,2048]{4,3,2,1,0:T(8,128)(2,1)} %bitcast.39, bf16[8,2048]{1,0:T(8,128)(2,1)} %x_ref.3, bf16[16,32,128]{2,1,0:T(8,128)(2,1)} %reshape.143.pages_ref), custom_call_target="tpu_custom_call" | custom-call | tf_op jit(solution)/shard_map/pallas_call | solution.py:503
  109.1 1.5 %copy.37 = f32[8,2048]{1,0:T(8,128)} copy(f32[8,2048]{1,0:T(8,128)} %get-tuple-element.23) | data formatting | bytes 131072
  110.6 1.6 %copy.38 = bf16[1,16,2,16,128]{4,3,2,1,0:T(8,128)(2,1)} copy(bf16[1,16,2,16,128]{4,3,2,1,0:T(8,128)(2,1)} %bitcast.43) | data formatting | bytes 262144
  (7 shorter events, 0.1 us)
Async XLA Ops:
  0.6 77.3 %copy-start = (bf16[64,2048]{1,0:T(8,128)(2,1)S(1)}, bf16[64,2048]{1,0:T(8,128)(2,1)}, u32[]{:S(2)}) copy-start(bf16[64,2048]{1,0:T(8,128)(2,1)} %param.13) | copy-start | bytes 786436
  42.3 34.1 %copy-start.3 = (s32[1,256]{1,0:T(1,128)S(1)}, s32[1,256]{1,0:T(1,128)}, u32[]{:S(2)}) copy-start(s32[1,256]{1,0:T(1,128)} %param.16) | copy-start | bytes 3076
  77.7 3.5 %copy-start.1 = (bf16[256,64]{1,0:T(8,128)(2,1)S(1)}, bf16[256,64]{1,0:T(8,128)(2,1)}, u32[]{:S(2)}) copy-start(bf16[256,64]{1,0:T(8,128)(2,1)} %get-tuple-element.9) | copy-start | bytes 98308
  77.8 3.5 %copy-start.2 = (bf16[256,64]{1,0:T(8,128)(2,1)S(1)}, bf16[256,64]{1,0:T(8,128)(2,1)}, u32[]{:S(2)}) copy-start(bf16[256,64]{1,0:T(8,128)(2,1)} %get-tuple-element.11) | copy-start | bytes 98308
  77.9 3.5 %copy-start.4 = (s32[16,1]{0,1:T(1,128)S(1)}, s32[16,1]{0,1:T(1,128)}, u32[]{:S(2)}) copy-start(s32[16,1]{0,1:T(1,128)} %param.17) | copy-start | bytes 196

commit v10 on v8

--- a/solution.py
+++ b/solution.py
@@ -205,45 +205,55 @@
     pl.semaphore_wait(barrier, total + extra)
 
 
-def _gather_kernel(n_col, n_plane, col, plane, slot, x_ref, out_ref, local_sem, send_sem, relay_sem, recv_sem):
+def _gather_kernel(n_col, n_plane, col, plane, slot, count, *refs):
+    x_refs, out_refs = refs[:count], refs[count : 2 * count]
+    local_sem, send_sem, relay_sem, recv_sem = refs[2 * count :]
     index = lax.axis_index("tensor")
     cpos, ppos = col[0](index), plane[0](index)
     mesh_ids = pl.DeviceIdType.MESH
     _greet(pltpu.get_barrier_semaphore(), [(n_col, *col), (n_plane, *plane)])
-
-    def col_copy(q):
-        return pltpu.make_async_remote_copy(
-            x_ref, out_ref.at[slot(cpos, ppos)], send_sem.at[q], recv_sem.at[cpos, ppos],
+    buffers = list(range(count))
+
+    def col_copy(b, q):
+        return pltpu.make_async_remote_copy(
+            x_refs[b], out_refs[b].at[slot(cpos, ppos)], send_sem.at[b, q], recv_sem.at[b, cpos, ppos],
             device_id={"tensor": col[1](index, q)}, device_id_type=mesh_ids,
         )
 
-    def plane_copy(q):
-        return pltpu.make_async_remote_copy(
-            x_ref, out_ref.at[slot(cpos, ppos)], send_sem.at[n_col + q], recv_sem.at[cpos, ppos],
+    def plane_copy(b, q):
+        return pltpu.make_async_remote_copy(
+            x_refs[b], out_refs[b].at[slot(cpos, ppos)], send_sem.at[b, n_col + q],
+            recv_sem.at[b, cpos, ppos],
             device_id={"tensor": plane[1](index, q)}, device_id_type=mesh_ids,
         )
 
-    def relay_copy(zc, q):
-        return pltpu.make_async_remote_copy(
-            out_ref.at[slot(zc, ppos)], out_ref.at[slot(zc, ppos)], relay_sem.at[zc, q], recv_sem.at[zc, ppos],
+    def relay_copy(b, zc, q):
+        return pltpu.make_async_remote_copy(
+            out_refs[b].at[slot(zc, ppos)], out_refs[b].at[slot(zc, ppos)], relay_sem.at[b, zc, q],
+            recv_sem.at[b, zc, ppos],
             device_id={"tensor": plane[1](index, q)}, device_id_type=mesh_ids,
         )
 
-    def arrival(zc, p):
-        return pltpu.make_async_remote_copy(
-            x_ref, out_ref.at[slot(zc, p)], send_sem.at[0], recv_sem.at[zc, p],
+    def arrival(b, zc, p):
+        return pltpu.make_async_remote_copy(
+            x_refs[b], out_refs[b].at[slot(zc, p)], send_sem.at[b, 0], recv_sem.at[b, zc, p],
             device_id={"tensor": index}, device_id_type=mesh_ids,
         )
 
-    local = pltpu.make_async_copy(x_ref, out_ref.at[slot(cpos, ppos)], local_sem)
-    local.start()
+    locals_ = []
+    for b in buffers:
+        local = pltpu.make_async_copy(x_refs[b], out_refs[b].at[slot(cpos, ppos)], local_sem.at[b])
+        local.start()
+        locals_.append(local)
 
     def send_col(k, carry):
-        col_copy((cpos + k) % n_col).start()
+        for b in buffers:
+            col_copy(b, (cpos + k) % n_col).start()
         return carry
 
     def send_plane(k, carry):
-        plane_copy((ppos + k) % n_plane).start()
+        for b in buffers:
+            plane_copy(b, (ppos + k) % n_plane).start()
         return carry
 
     lax.fori_loop(1, n_col, send_col, 0)
@@ -251,10 +261,12 @@
 
     def relay(k, carry):
         zc = (cpos + k) % n_col
-        arrival(zc, ppos).wait_recv()
+        for b in buffers:
+            arrival(b, zc, ppos).wait_recv()
 
         def forward(m, inner):
-            relay_copy(zc, (ppos + m) % n_plane).start()
+            for b in buffers:
+                relay_copy(b, zc, (ppos + m) % n_plane).start()
             return inner
 
         return lax.fori_loop(1, n_plane, forward, carry)
@@ -262,13 +274,15 @@
     lax.fori_loop(1, n_col, relay, 0)
 
     def finish_col(k, carry):
-        col_copy((cpos + k) % n_col).wait_send()
+        for b in buffers:
+            col_copy(b, (cpos + k) % n_col).wait_send()
         return carry
 
     def finish_plane(m, carry):
         q = (ppos + m) % n_plane
-        plane_copy(q).wait_send()
-        arrival(cpos, q).wait_recv()
+        for b in buffers:
+            plane_copy(b, q).wait_send()
+            arrival(b, cpos, q).wait_recv()
         return carry
 
     def finish_relay(k, carry):
@@ -276,8 +290,9 @@
 
         def inner(m, c):
             q = (ppos + m) % n_plane
-            relay_copy(zc, q).wait_send()
-            arrival(zc, q).wait_recv()
+            for b in buffers:
+                relay_copy(b, zc, q).wait_send()
+                arrival(b, zc, q).wait_recv()
             return c
 
         return lax.fori_loop(1, n_plane, inner, carry)
@@ -285,23 +300,27 @@
     lax.fori_loop(1, n_col, finish_col, 0)
     lax.fori_loop(1, n_plane, finish_plane, 0)
     lax.fori_loop(1, n_col, finish_relay, 0)
-    local.wait()
-
-
-def gather_tokens(x, col, plane, slot, n_col, n_plane, collective_id):
+    for local in locals_:
+        local.wait()
+
+
+def gather_tokens(blocks, col, plane, slot, n_col, n_plane, collective_id):
+    count = len(blocks)
     return pl.pallas_call(
-        functools.partial(_gather_kernel, n_col, n_plane, col, plane, slot),
-        out_shape=jax.ShapeDtypeStruct((n_col * n_plane,) + x.shape, x.dtype),
-        in_specs=[pl.BlockSpec(memory_space=pltpu.VMEM)],
-        out_specs=pl.BlockSpec(memory_space=pltpu.VMEM),
+        functools.partial(_gather_kernel, n_col, n_plane, col, plane, slot, count),
+        out_shape=tuple(
+            jax.ShapeDtypeStruct((n_col * n_plane,) + x.shape, x.dtype) for x in blocks
+        ),
+        in_specs=[pl.BlockSpec(memory_space=pltpu.VMEM)] * count,
+        out_specs=tuple(pl.BlockSpec(memory_space=pltpu.VMEM) for _ in blocks),
         scratch_shapes=[
-            pltpu.SemaphoreType.DMA,
-            pltpu.SemaphoreType.DMA((n_col + n_plane,)),
-            pltpu.SemaphoreType.DMA((n_col, n_plane)),
-            pltpu.SemaphoreType.DMA((n_col, n_plane)),
+            pltpu.SemaphoreType.DMA((count,)),
+            pltpu.SemaphoreType.DMA((count, n_col + n_plane)),
+            pltpu.SemaphoreType.DMA((count, n_col, n_plane)),
+            pltpu.SemaphoreType.DMA((count, n_col, n_plane)),
         ],
         compiler_params=pltpu.CompilerParams(collective_id=collective_id, has_side_effects=True),
-    )(x)
+    )(*blocks)
 
 
 def _reduce_kernel(n_col, n_plane, n_dp, col, plane, pick, rows_ref, x_ref, pages_ref, out_ref,
@@ -454,8 +473,12 @@
 
     width = hidden_states.shape[1]
     planes = tensor_count // 8
-    gathered = gather_tokens(
-        hidden_states,
+    own = hidden_states.astype(jnp.float32)
+    own_center = jnp.mean(own, axis=-1, keepdims=True)
+    own_shifted = own - own_center
+    own_scale = lax.rsqrt(jnp.mean(own_shifted * own_shifted, axis=-1, keepdims=True) + epsilon)
+    gathered, statistics = gather_tokens(
+        (hidden_states, jnp.concatenate([own_center, own_scale], 1)),
         (column_group, column_member),
         (plane_group, plane_member),
         token_block,
@@ -464,8 +487,11 @@
         0,
     )
     tokens = gathered.reshape(tokens_total, width)
-    normed_attention = layer_norm(tokens, attention_gain)
-    normed_feedforward = layer_norm(tokens, feedforward_gain)
+    statistics = statistics.reshape(tokens_total, 2)
+    shifted = tokens.astype(jnp.float32) - statistics[:, :1]
+    scaled = shifted * statistics[:, 1:]
+    normed_attention = (scaled * attention_gain).astype(jnp.bfloat16)
+    normed_feedforward = (scaled * feedforward_gain).astype(jnp.bfloat16)
     joined = jnp.dot(normed_attention, heads_weight, preferred_element_type=jnp.float32).astype(
         jnp.bfloat16
     )

time: 100 us -> 104 us (1.040)
  Pallas kernels: 82.5 us -> 84.8 us
  local copies, waits for them, and re-layouts: 4.2 us -> 5.93 us
  matrix products: 5.31 us -> 6.62 us
  other arithmetic: 7.03 us -> 5.79 us
    pallas_call x1, Pallas kernels: 33.6 us -> 35.4 us  [gather_tokens(): pl.pallas_call(functools.partial(_gather_kernel, n_col, n_plane, col, pla...]
    dot_general x1, matrix products: 0.53 us -> 1.84 us  [shards(): jnp.dot(normed_attention, heads_weight, preferred_element_type=jnp.float32)]
    reduce_sum x2, other arithmetic: 3.17 us -> 1.91 us  [the longest x1 0.96 us: shards(): own_center = jnp.mean(own, axis=-1, keepdims=True)]
    slice x1 -> x2, local copies, waits for them, and re-layouts: 0.07 us -> 1.15 us  [the longest x1 1.07 us: shards(): shifted = tokens.astype(jnp.float32) - statistics[:, :1]]
where the time goes in v10:
time: 104 us
  Pallas kernels  84.8 us (82%)
  matrix products  6.62 us (6%)
  local copies, waits for them, and re-layouts  5.93 us (6%)
  other arithmetic  5.79 us (6%)
    pallas_call x1, Pallas kernels, gather_tokens(): pl.pallas_call(functools.partial(_gather_kernel, n_col, n_plane, col, pla...  35.4 us
    pallas_call x1, Pallas kernels, reduce_rows(): pl.pallas_call(functools.partial(_reduce_kernel, n_col, n_plane, n_dp, co...  27.4 us
    pallas_call x1, Pallas kernels, exchange_all(): pl.pallas_call(functools.partial(_exchange_kernel, tuple(plans), work, le...  22 us
    dot_general x1, matrix products, shards(): jnp.dot(attended, output_weight, preferred_element_type=jnp.float32)  3.29 us
    unnamed x16, local copies, waits for them, and re-layouts  3.23 us

profile of v10, /device:TPU:1, one launch (start us, length us, event | category | flops | bytes accessed | tf_op | source)
XLA Modules:
  0.0 104.0 jit_solution(11093314583373045168)
XLA Ops:
  0.6 0.0 copy-start
  0.7 1.0 convert_reduce_fusion
  1.6 1.0 fusion.47
  2.6 0.7 copy.35.refs_1_
  3.3 35.4 %shard_map.104 = (bf16[32,8,2048]{2,1,0:T(8,128)(2,1)}, f32[32,8,2]{2,1,0:T(8,128)}) custom-call(bf16[8,2048]{1,0:T(8,128)(2,1)} %x_ref.1, f32[8,2]{1,0:T(8,128)} %copy.35.refs_1_), custom_call_target="tpu_custom_call" | custom-call | tf_op jit(solution)/shard_map/pallas_call | solution.py:309
  38.7 1.1 %fusion.59 = (f32[256,1]{1,0:T(8,128)S(1)}, f32[256,1]{1,0:T(8,128)S(1)}) fusion(f32[256,2]{1,0:T(8,128)} %bitcast.47), kind=kLoop, calls=%fused_computation.81 | loop fusion | bytes 4096 | tf_op jit(solution)/shard_map/slice | solution.py:491
  39.8 0.1 copy.45
  39.8 0.0 copy-start.3
  39.8 0.1 copy.46
  39.9 0.0 copy-done
  39.9 0.0 copy-start.1
  39.9 0.0 copy-start.4
  39.9 1.8 %convolution_convert_fusion.1 = bf16[256,192]{1,0:T(8,128)(2,1)S(1)} fusion(bf16[2048,192]{0,1:T(8,128)(2,1)S(1)} %copy-done, bf16[32,8,2048]{2,1,0:T(8,128)(2,1)} %get-tuple-element.8, f32[2048]{0:T(1024)} %param.10, f32[256]{0:T(256)S(1)} %bitcast.54, f32[256]{0:T(256)S(1)} %bitcast.52), kind=kOutput, calls=%fused_computation.11 | convolution fusion | flops 203997184 | bytes 1943552 | tf_op jit(solution)/shard_map/dot_general | solution.py:495
  41.8 0.1 slice_convert_fusion.1
  41.9 0.0 copy-done.3
  41.9 0.1 compare_reduce_fusion
  42.0 0.1 fusion.51
  42.1 0.3 reduce-window.9
  42.4 0.1 slice.54
  42.5 0.1 slice_reduce_fusion
  42.6 0.1 fusion.52
  42.7 0.6 fusion.31
  43.3 0.1 fusion.58
  43.4 0.7 pad_maximum_fusion
  44.2 0.0 copy-done.1
  44.2 0.0 copy-done.4
  44.2 1.4 %fusion.5.refs_1_ = bf16[256,2048]{1,0:T(8,128)(2,1)} fusion(bf16[32,8,2048]{2,1,0:T(8,128)(2,1)S(1)} %copy-done.1, f32[2048]{0:T(1024)S(1)} %copy-done.4, f32[256]{0:T(256)S(1)} %bitcast.55, f32[256]{0:T(256)S(1)} %bitcast.53), kind=kLoop, calls=%fused_computation.8 | loop fusion | flops 2621440 | bytes 2107392 | tf_op jit(solution)/shard_map/convert_element_type | solution.py:494
  45.5 0.0 copy-start.2
  45.5 22.0 %shard_map.105 = (bf16[4,256,128]{2,1,0:T(8,128)(2,1)}, f32[256,2048]{1,0:T(8,128)}) custom-call(bf16[1,256,128]{2,1,0:T(8,128)(2,1)} %get-tuple-element.26.refs_0_, bf16[256,2048]{1,0:T(8,128)(2,1)} %fusion.5.refs_1_, bf16[2048,256]{1,0:T(8,128)(2,1)} %refs_2_.1, bf16[256,2048]{1,0:T(8,128)(2,1)} %refs_3_.1), custom_call_target="tpu_custom_call" | custom-call | tf_op jit(solution)/shard_map/pallas_call | solution.py:165
  67.6 1.3 %select_reduce_fusion = (f32[256]{0:T(256)S(1)}, f32[256,256]{0,1:T(8,128)S(1)}) fusion(s32[256]{0:T(256)S(1)} %bitcast.49, bf16[4,256,128]{2,1,0:T(8,128)(2,1)} %get-tuple-element.10), kind=kOutput, calls=%fused_computation.21 | convolution fusion | flops 33947392 | bytes 789504 | tf_op jit(solution)/shard_map/dot_general | solution.py:537
  68.9 0.0 copy-start.5
  68.9 0.1 fusion.26
  69.0 0.0 copy-done.2
  69.0 3.3 %fusion = bf16[256,2048]{1,0:T(8,128)(2,1)} fusion(f32[256,2048]{1,0:T(8,128)} %get-tuple-element.11, bf16[64,2048]{1,0:T(8,128)(2,1)S(1)} %copy-done.2, f32[256,256]{0,1:T(8,128)S(1)} %get-tuple-element.32, f32[256]{0:T(256)S(1)} %get-tuple-element.31, s32[256]{0:T(256)S(1)} %bitcast.51, f32[256]{0:T(256)S(1)} %fusion.26, ...), kind=kOutput, calls=%fused_computation.1 | convolution fusion | flops 76972032 | bytes 3739648 | tf_op jit(solution)/shard_map/dot_general | solution.py:546
  72.4 0.0 copy-done.5
  72.4 0.2 convert_reduce_fusion.1
  72.6 0.2 convolution_convert_fusion
  72.7 0.7 reshape.110.pages_ref
  73.5 27.4 %shard_map.106 = (f32[8,2048]{1,0:T(8,128)}, bf16[16,32,128]{2,1,0:T(8,128)(2,1)}) custom-call(bf16[4,4,2,8,2048]{4,3,2,1,0:T(8,128)(2,1)} %bitcast.46, bf16[8,2048]{1,0:T(8,128)(2,1)} %x_ref.1, bf16[16,32,128]{2,1,0:T(8,128)(2,1)} %reshape.110.pages_ref), custom_call_target="tpu_custom_call" | custom-call | tf_op jit(solution)/shard_map/pallas_call | solution.py:428
  100.9 1.5 %copy.49 = f32[8,2048]{1,0:T(8,128)} copy(f32[8,2048]{1,0:T(8,128)} %get-tuple-element.35) | data formatting | bytes 131072
  102.4 1.6 %copy.50 = bf16[1,16,2,16,128]{4,3,2,1,0:T(8,128)(2,1)} copy(bf16[1,16,2,16,128]{4,3,2,1,0:T(8,128)(2,1)} %bitcast.48) | data formatting | bytes 262144
  (7 shorter events, 0.1 us)
Async XLA Ops:
  0.6 39.3 %copy-start = (bf16[2048,192]{0,1:T(8,128)(2,1)S(1)}, bf16[2048,192]{0,1:T(8,128)(2,1)}, u32[]{:S(2)}) copy-start(bf16[2048,192]{0,1:T(8,128)(2,1)} %param.12) | copy-start | bytes 2359300
  39.8 2.0 %copy-start.3 = (s32[1,256]{1,0:T(1,128)S(1)}, s32[1,256]{1,0:T(1,128)}, u32[]{:S(2)}) copy-start(s32[1,256]{1,0:T(1,128)} %param.16) | copy-start | bytes 3076
  39.9 4.2 %copy-start.1 = (bf16[32,8,2048]{2,1,0:T(8,128)(2,1)S(1)}, bf16[32,8,2048]{2,1,0:T(8,128)(2,1)}, u32[]{:S(2)}) copy-start(bf16[32,8,2048]{2,1,0:T(8,128)(2,1)} %get-tuple-element.8) | copy-start | bytes 3145732
  39.9 4.2 %copy-start.4 = (f32[2048]{0:T(1024)S(1)}, f32[2048]{0:T(1024)}, u32[]{:S(2)}) copy-start(f32[2048]{0:T(1024)} %param.11) | copy-start | bytes 24580
  45.5 23.5 %copy-start.2 = (bf16[64,2048]{1,0:T(8,128)(2,1)S(1)}, bf16[64,2048]{1,0:T(8,128)(2,1)}, u32[]{:S(2)}) copy-start(bf16[64,2048]{1,0:T(8,128)(2,1)} %param.13) | copy-start | bytes 786436
  68.9 3.5 %copy-start.5 = (s32[16,1]{0,1:T(1,128)S(1)}, s32[16,1]{0,1:T(1,128)}, u32[]{:S(2)}) copy-start(s32[16,1]{0,1:T(1,128)} %param.17) | copy-start | bytes 196

commit v11 on v8

--- a/solution.py
+++ b/solution.py
@@ -304,11 +304,11 @@
     )(x)
 
 
-def _reduce_kernel(n_col, n_plane, n_dp, col, plane, pick, rows_ref, x_ref, pages_ref, out_ref,
-                   pages_out, inbox, stage, inbox2, local_sem, send_sem, recv_sem, send2_sem, recv2_sem,
-                   page_local_sem, page_send_sem, page_recv_sem):
+def _reduce_kernel(n_col, n_y, n_dp, col, ygroup, rows_ref, x_ref, pages_ref, out_ref, pages_out,
+                   inbox0, chip, inbox1, stage, inbox2, sem0, local_sem, send_sem, recv_sem,
+                   send2_sem, recv2_sem, page_local_sem, page_send_sem, page_recv_sem):
     index = lax.axis_index("tensor")
-    cpos, ppos = col[0](index), plane[0](index)
+    cpos, ypos, core = col[0](index), ygroup[0](index), index % 2
     mesh_ids = pl.DeviceIdType.MESH
     barrier = pltpu.get_barrier_semaphore()
     group = lax.axis_index("dp")
@@ -326,7 +326,8 @@
         return carry
 
     lax.fori_loop(1, n_dp, greet_group, 0)
-    _greet(barrier, [(n_col, *col), (n_plane, *plane)], extra=n_dp - 1)
+    sibling = (2, lambda t: t % 2, lambda t, q: t - t % 2 + q)
+    _greet(barrier, [sibling, (n_y, *ygroup), (n_col, *col)], extra=n_dp - 1)
     page_local = pltpu.make_async_copy(pages_ref.at[group], pages_out.at[group], page_local_sem)
     page_local.start()
 
@@ -336,10 +337,23 @@
 
     lax.fori_loop(1, n_dp, send_pages, 0)
 
+    pair = pltpu.make_async_remote_copy(
+        rows_ref.at[:, :, 1 - core], inbox0, sem0.at[0], sem0.at[1],
+        device_id={"tensor": index - core + 1 - core}, device_id_type=mesh_ids,
+    )
+    pair.start()
+    pair.wait_send()
+    pair.wait_recv()
+    for y in range(n_y):
+        for z in range(n_col):
+            chip[y, z] = (
+                rows_ref[y, z, core].astype(jnp.float32) + inbox0[y, z].astype(jnp.float32)
+            ).astype(chip.dtype)
+
     def plane_copy(q, z, slot):
         return pltpu.make_async_remote_copy(
-            pick(rows_ref, q, z), inbox.at[z, slot], send_sem.at[z, q], recv_sem.at[z, slot],
-            device_id={"tensor": plane[1](index, q)}, device_id_type=mesh_ids,
+            chip.at[q, z], inbox1.at[z, slot], send_sem.at[z, q], recv_sem.at[z, slot],
+            device_id={"tensor": ygroup[1](index, q)}, device_id_type=mesh_ids,
         )
 
     def col_copy(q, slot):
@@ -351,26 +365,26 @@
     order = [(cpos + 1 + k) % n_col for k in range(n_col)]
     locals_ = []
     for z in order:
-        local = pltpu.make_async_copy(pick(rows_ref, ppos, z), inbox.at[z, ppos], local_sem.at[z])
+        local = pltpu.make_async_copy(chip.at[ypos, z], inbox1.at[z, ypos], local_sem.at[z])
         local.start()
         locals_.append(local)
 
         def send_plane(m, carry, z=z):
-            plane_copy((ppos + m) % n_plane, z, ppos).start()
+            plane_copy((ypos + m) % n_y, z, ypos).start()
             return carry
 
-        lax.fori_loop(1, n_plane, send_plane, 0)
+        lax.fori_loop(1, n_y, send_plane, 0)
 
     def plane_sum(z, local):
         def arrive(m, carry):
-            plane_copy((ppos + m) % n_plane, z, (ppos + m) % n_plane).wait_recv()
+            plane_copy((ypos + m) % n_y, z, (ypos + m) % n_y).wait_recv()
             return carry
 
-        lax.fori_loop(1, n_plane, arrive, 0)
+        lax.fori_loop(1, n_y, arrive, 0)
         local.wait()
-        total = inbox[z, 0].astype(jnp.float32)
-        for sender in range(1, n_plane):
-            total = total + inbox[z, sender].astype(jnp.float32)
+        total = inbox1[z, 0].astype(jnp.float32)
+        for sender in range(1, n_y):
+            total = total + inbox1[z, sender].astype(jnp.float32)
         return total
 
     for z, local in zip(order[:-1], locals_[:-1]):
@@ -380,12 +394,12 @@
     result = x_ref[...].astype(jnp.float32) + plane_sum(cpos, locals_[-1])
 
     def finish_plane(m, carry):
-        q = (ppos + m) % n_plane
+        q = (ypos + m) % n_y
         for z in order:
-            plane_copy(q, z, ppos).wait_send()
-        return carry
-
-    lax.fori_loop(1, n_plane, finish_plane, 0)
+            plane_copy(q, z, ypos).wait_send()
+        return carry
+
+    lax.fori_loop(1, n_y, finish_plane, 0)
 
     for z in order[:-1]:
         col_copy(z, cpos).wait_send()
@@ -403,11 +417,12 @@
     page_local.wait()
 
 
-def reduce_rows(rows, x, pages, col, plane, pick, n_col, n_plane, collective_id):
+def reduce_rows(rows, x, pages, col, ygroup, collective_id):
+    n_y, n_col = rows.shape[0], rows.shape[1]
     block = x.shape
     n_dp = pages.shape[0]
     return pl.pallas_call(
-        functools.partial(_reduce_kernel, n_col, n_plane, n_dp, col, plane, pick),
+        functools.partial(_reduce_kernel, n_col, n_y, n_dp, col, ygroup),
         out_shape=(
             jax.ShapeDtypeStruct(block, jnp.float32),
             jax.ShapeDtypeStruct(pages.shape, pages.dtype),
@@ -415,12 +430,15 @@
         in_specs=[pl.BlockSpec(memory_space=pltpu.VMEM)] * 3,
         out_specs=(pl.BlockSpec(memory_space=pltpu.VMEM), pl.BlockSpec(memory_space=pltpu.VMEM)),
         scratch_shapes=[
-            pltpu.VMEM((n_col, n_plane) + block, rows.dtype),
+            pltpu.VMEM((n_y, n_col) + block, rows.dtype),
+            pltpu.VMEM((n_y, n_col) + block, rows.dtype),
+            pltpu.VMEM((n_col, n_y) + block, rows.dtype),
             pltpu.VMEM((n_col,) + block, rows.dtype),
             pltpu.VMEM((n_col,) + block, rows.dtype),
+            pltpu.SemaphoreType.DMA((2,)),
             pltpu.SemaphoreType.DMA((n_col,)),
-            pltpu.SemaphoreType.DMA((n_col, n_plane)),
-            pltpu.SemaphoreType.DMA((n_col, n_plane)),
+            pltpu.SemaphoreType.DMA((n_col, n_y)),
+            pltpu.SemaphoreType.DMA((n_col, n_y)),
             pltpu.SemaphoreType.DMA((n_col,)),
             pltpu.SemaphoreType.DMA((n_col,)),
             pltpu.SemaphoreType.DMA,
@@ -429,6 +447,14 @@
         ],
         compiler_params=pltpu.CompilerParams(collective_id=collective_id, has_side_effects=True),
     )(rows, x, pages)
+
+
+def same_core_group(index):
+    return index // 8
+
+
+def same_core_member(index, q):
+    return q * 8 + index % 8
 
 
 def shards(
@@ -524,10 +550,7 @@
         hidden_states,
         outgoing,
         (column_group, column_member),
-        (plane_group, plane_member),
-        plane_rows,
-        planes,
-        8,
+        (same_core_group, same_core_member),
         2,
     )
 

time: 100 us -> 97.4 us (0.974)
  the two profiles are of different devices: /device:TPU:1 before, /device:TPU:6 now
where the time goes in v11:
time: 97.4 us; the launch traced here: 97 us
  Pallas kernels  79.7 us (82%)
  other arithmetic  7.03 us (7%)
  matrix products  5.31 us (5%)
  local copies, waits for them, and re-layouts  4.2 us (4%)
    pallas_call x1, Pallas kernels, gather_tokens(): pl.pallas_call(functools.partial(_gather_kernel, n_col, n_plane, col, pla...  32.5 us
    pallas_call x1, Pallas kernels, reduce_rows(): pl.pallas_call(functools.partial(_reduce_kernel, n_col, n_y, n_dp, col, y...  25.7 us
    pallas_call x1, Pallas kernels, exchange_all(): pl.pallas_call(functools.partial(_exchange_kernel, tuple(plans), work, le...  21.5 us
    dot_general x1, matrix products, shards(): jnp.dot(attended, output_weight, preferred_element_type=jnp.float32)  3.29 us
    unnamed x16, local copies, waits for them, and re-layouts  3.08 us

profile of v11, /device:TPU:6, one launch (start us, length us, event | category | flops | bytes accessed | tf_op | source)
XLA Modules:
  0.0 97.0 jit_solution(3078809713272893462)
XLA Ops:
  0.6 0.0 copy-start
  0.6 0.0 copy-start.5
  0.7 32.5 %shard_map.104 = bf16[32,8,2048]{2,1,0:T(8,128)(2,1)} custom-call(bf16[8,2048]{1,0:T(8,128)(2,1)} %x_ref.3), custom_call_target="tpu_custom_call" | custom-call | tf_op jit(solution)/shard_map/pallas_call | solution.py:292
  33.1 0.0 copy-start.1
  33.2 1.5 %convert_reduce_fusion = f32[32,8]{1,0:T(8,128)S(1)} fusion(bf16[32,8,2048]{2,1,0:T(8,128)(2,1)} %shard_map.104), kind=kLoop, calls=%fused_computation.1 | loop fusion | flops 1048320 | bytes 1049600 | tf_op jit(solution)/shard_map/reduce_sum | solution.py:23
  34.7 1.6 %fusion.8 = f32[32,8]{1,0:T(8,128)S(1)} fusion(bf16[32,8,2048]{2,1,0:T(8,128)(2,1)} %shard_map.104, f32[32,8]{1,0:T(8,128)S(1)} %broadcast_multiply_fusion), kind=kLoop, calls=%fused_computation.13 | loop fusion | flops 2096896 | bytes 1050624 | tf_op jit(solution)/shard_map/reduce_sum | solution.py:25
  36.3 0.0 copy-start.3
  36.3 0.1 rsqrt.13
  36.4 0.1 div.19
  36.5 0.0 copy-done
  36.5 0.0 copy-done.5
  36.5 0.0 copy-done.1
  36.6 0.0 copy-start.4
  36.6 0.5 convolution_convert_fusion.1
  37.1 0.1 slice_convert_fusion.1
  37.2 0.0 copy-done.3
  37.2 0.1 compare_reduce_fusion
  37.3 0.1 fusion.51
  37.4 0.3 reduce-window.9
  37.7 0.1 slice.46
  37.8 0.1 slice_reduce_fusion
  37.9 0.1 fusion.52
  38.0 0.6 fusion.33
  38.6 0.1 fusion.57
  38.8 0.7 pad_maximum_fusion
  39.5 0.0 copy-done.4
  39.5 1.4 %fusion.6.refs_1_ = bf16[256,2048]{1,0:T(8,128)(2,1)} fusion(bf16[32,8,2048]{2,1,0:T(8,128)(2,1)S(1)} %copy-done.1, f32[2048]{0:T(1024)S(1)} %copy-done.4, f32[256]{0:T(256)S(1)} %rsqrt.13, f32[256]{0:T(256)S(1)} %div.19), kind=kLoop, calls=%fused_computation.11 | loop fusion | flops 2621440 | bytes 2107392 | tf_op jit(solution)/shard_map/convert_element_type | solution.py:26
  40.9 0.0 copy-start.2
  40.9 21.5 %shard_map.105 = (bf16[4,256,128]{2,1,0:T(8,128)(2,1)}, f32[256,2048]{1,0:T(8,128)}) custom-call(bf16[1,256,128]{2,1,0:T(8,128)(2,1)} %get-tuple-element.20.refs_0_, bf16[256,2048]{1,0:T(8,128)(2,1)} %fusion.6.refs_1_, bf16[2048,256]{1,0:T(8,128)(2,1)} %refs_2_.1, bf16[256,2048]{1,0:T(8,128)(2,1)} %refs_3_.1), custom_call_target="tpu_custom_call" | custom-call | tf_op jit(solution)/shard_map/pallas_call | solution.py:165
  62.4 1.3 %select_reduce_fusion = (f32[256]{0:T(256)S(1)}, f32[256,256]{0,1:T(8,128)S(1)}) fusion(s32[256]{0:T(256)S(1)} %bitcast.49, bf16[4,256,128]{2,1,0:T(8,128)(2,1)} %get-tuple-element.6), kind=kOutput, calls=%fused_computation.25 | convolution fusion | flops 33947392 | bytes 789504 | tf_op jit(solution)/shard_map/dot_general | solution.py:537
  63.7 0.0 copy-start.6
  63.7 0.1 fusion.28
  63.9 0.0 copy-done.2
  63.9 3.3 %fusion = bf16[256,2048]{1,0:T(8,128)(2,1)} fusion(f32[256,2048]{1,0:T(8,128)} %get-tuple-element.7, bf16[64,2048]{1,0:T(8,128)(2,1)S(1)} %copy-done.2, f32[256,256]{0,1:T(8,128)S(1)} %get-tuple-element.24, f32[256]{0:T(256)S(1)} %get-tuple-element.23, s32[256]{0:T(256)S(1)} %bitcast.51, f32[256]{0:T(256)S(1)} %fusion.28, ...), kind=kOutput, calls=%fused_computation.4 | convolution fusion | flops 76972032 | bytes 3739648 | tf_op jit(solution)/shard_map/dot_general | solution.py:546
  67.2 0.0 copy-done.6
  67.2 0.2 convert_reduce_fusion.1
  67.4 0.2 convolution_convert_fusion
  67.5 0.7 reshape.107.pages_ref
  68.3 25.7 %shard_map.106 = (f32[8,2048]{1,0:T(8,128)}, bf16[16,32,128]{2,1,0:T(8,128)(2,1)}) custom-call(bf16[4,4,2,8,2048]{4,3,2,1,0:T(8,128)(2,1)} %bitcast.47, bf16[8,2048]{1,0:T(8,128)(2,1)} %x_ref.3, bf16[16,32,128]{2,1,0:T(8,128)(2,1)} %reshape.107.pages_ref), custom_call_target="tpu_custom_call" | custom-call | tf_op jit(solution)/shard_map/pallas_call | solution.py:424
  93.9 1.5 %copy.29 = f32[8,2048]{1,0:T(8,128)} copy(f32[8,2048]{1,0:T(8,128)} %get-tuple-element.27) | data formatting | bytes 131072
  95.4 1.6 %copy.30 = bf16[1,16,2,16,128]{4,3,2,1,0:T(8,128)(2,1)} copy(bf16[1,16,2,16,128]{4,3,2,1,0:T(8,128)(2,1)} %bitcast.48) | data formatting | bytes 262144
  (6 shorter events, 0.1 us)
Async XLA Ops:
  0.6 35.9 %copy-start = (bf16[2048,192]{0,1:T(8,128)(2,1)S(1)}, bf16[2048,192]{0,1:T(8,128)(2,1)}, u32[]{:S(2)}) copy-start(bf16[2048,192]{0,1:T(8,128)(2,1)} %param.12) | copy-start | bytes 2359300
  0.6 35.9 %copy-start.5 = (f32[2048]{0:T(1024)S(1)}, f32[2048]{0:T(1024)}, u32[]{:S(2)}) copy-start(f32[2048]{0:T(1024)} %param.10) | copy-start | bytes 24580
  33.1 3.4 %copy-start.1 = (bf16[32,8,2048]{2,1,0:T(8,128)(2,1)S(1)}, bf16[32,8,2048]{2,1,0:T(8,128)(2,1)}, u32[]{:S(2)}) copy-start(bf16[32,8,2048]{2,1,0:T(8,128)(2,1)} %shard_map.104) | copy-start | bytes 3145732
  36.3 0.9 copy-start.3
  36.6 2.9 %copy-start.4 = (f32[2048]{0:T(1024)S(1)}, f32[2048]{0:T(1024)}, u32[]{:S(2)}) copy-start(f32[2048]{0:T(1024)} %param.11) | copy-start | bytes 24580
  40.9 23.0 %copy-start.2 = (bf16[64,2048]{1,0:T(8,128)(2,1)S(1)}, bf16[64,2048]{1,0:T(8,128)(2,1)}, u32[]{:S(2)}) copy-start(bf16[64,2048]{1,0:T(8,128)(2,1)} %param.13) | copy-start | bytes 786436
  63.7 3.5 %copy-start.6 = (s32[16,1]{0,1:T(1,128)S(1)}, s32[16,1]{0,1:T(1,128)}, u32[]{:S(2)}) copy-start(s32[16,1]{0,1:T(1,128)} %param.17) | copy-start | bytes 196

commit v12 on v11

--- a/solution.py
+++ b/solution.py
@@ -205,103 +205,132 @@
     pl.semaphore_wait(barrier, total + extra)
 
 
-def _gather_kernel(n_col, n_plane, col, plane, slot, x_ref, out_ref, local_sem, send_sem, relay_sem, recv_sem):
+def _gather_kernel(n_col, n_y, col, ygroup, slot, x_ref, out_ref, local_sem, col_sem, y_sem, pair_sem,
+                   recv_sem):
     index = lax.axis_index("tensor")
-    cpos, ppos = col[0](index), plane[0](index)
+    z0, y0, c0 = col[0](index), ygroup[0](index), index % 2
     mesh_ids = pl.DeviceIdType.MESH
-    _greet(pltpu.get_barrier_semaphore(), [(n_col, *col), (n_plane, *plane)])
+    sibling = (2, lambda t: t % 2, lambda t, q: t - t % 2 + q)
+    _greet(pltpu.get_barrier_semaphore(), [(n_col, *col), (n_y, *ygroup), sibling])
+    partner = index - c0 + 1 - c0
+
+    def block(y, z, c):
+        return out_ref.at[slot(y, z, c)]
 
     def col_copy(q):
         return pltpu.make_async_remote_copy(
-            x_ref, out_ref.at[slot(cpos, ppos)], send_sem.at[q], recv_sem.at[cpos, ppos],
+            x_ref, block(y0, z0, c0), col_sem.at[q], recv_sem.at[y0, z0, c0],
             device_id={"tensor": col[1](index, q)}, device_id_type=mesh_ids,
         )
 
-    def plane_copy(q):
+    def y_copy(z, q):
         return pltpu.make_async_remote_copy(
-            x_ref, out_ref.at[slot(cpos, ppos)], send_sem.at[n_col + q], recv_sem.at[cpos, ppos],
-            device_id={"tensor": plane[1](index, q)}, device_id_type=mesh_ids,
-        )
-
-    def relay_copy(zc, q):
+            block(y0, z, c0), block(y0, z, c0), y_sem.at[z, q], recv_sem.at[y0, z, c0],
+            device_id={"tensor": ygroup[1](index, q)}, device_id_type=mesh_ids,
+        )
+
+    def pair_copy(y, z):
         return pltpu.make_async_remote_copy(
-            out_ref.at[slot(zc, ppos)], out_ref.at[slot(zc, ppos)], relay_sem.at[zc, q], recv_sem.at[zc, ppos],
-            device_id={"tensor": plane[1](index, q)}, device_id_type=mesh_ids,
-        )
-
-    def arrival(zc, p):
+            block(y, z, c0), block(y, z, c0), pair_sem.at[y, z], recv_sem.at[y, z, c0],
+            device_id={"tensor": partner}, device_id_type=mesh_ids,
+        )
+
+    def arrival(y, z, c):
         return pltpu.make_async_remote_copy(
-            x_ref, out_ref.at[slot(zc, p)], send_sem.at[0], recv_sem.at[zc, p],
+            x_ref, block(y, z, c), col_sem.at[0], recv_sem.at[y, z, c],
             device_id={"tensor": index}, device_id_type=mesh_ids,
         )
 
-    local = pltpu.make_async_copy(x_ref, out_ref.at[slot(cpos, ppos)], local_sem)
+    def spread(z):
+        def send_y(m, carry):
+            y_copy(z, (y0 + m) % n_y).start()
+            return carry
+
+        lax.fori_loop(1, n_y, send_y, 0)
+        pair_copy(y0, z).start()
+
+    local = pltpu.make_async_copy(x_ref, block(y0, z0, c0), local_sem)
     local.start()
 
     def send_col(k, carry):
-        col_copy((cpos + k) % n_col).start()
+        col_copy((z0 + k) % n_col).start()
         return carry
 
-    def send_plane(k, carry):
-        plane_copy((ppos + k) % n_plane).start()
+    lax.fori_loop(1, n_col, send_col, 0)
+    local.wait()
+    spread(z0)
+
+    def relay_col(k, carry):
+        z = (z0 + k) % n_col
+        arrival(y0, z, c0).wait_recv()
+        spread(z)
         return carry
 
-    lax.fori_loop(1, n_col, send_col, 0)
-    lax.fori_loop(1, n_plane, send_plane, 0)
-
-    def relay(k, carry):
-        zc = (cpos + k) % n_col
-        arrival(zc, ppos).wait_recv()
-
-        def forward(m, inner):
-            relay_copy(zc, (ppos + m) % n_plane).start()
+    lax.fori_loop(1, n_col, relay_col, 0)
+
+    def relay_y(m, carry):
+        y = (y0 + m) % n_y
+
+        def each(k, inner):
+            z = (z0 + k) % n_col
+            arrival(y, z, c0).wait_recv()
+            pair_copy(y, z).start()
             return inner
 
-        return lax.fori_loop(1, n_plane, forward, carry)
-
-    lax.fori_loop(1, n_col, relay, 0)
+        return lax.fori_loop(0, n_col, each, carry)
+
+    lax.fori_loop(1, n_y, relay_y, 0)
 
     def finish_col(k, carry):
-        col_copy((cpos + k) % n_col).wait_send()
+        col_copy((z0 + k) % n_col).wait_send()
         return carry
 
-    def finish_plane(m, carry):
-        q = (ppos + m) % n_plane
-        plane_copy(q).wait_send()
-        arrival(cpos, q).wait_recv()
-        return carry
-
-    def finish_relay(k, carry):
-        zc = (cpos + k) % n_col
-
-        def inner(m, c):
-            q = (ppos + m) % n_plane
-            relay_copy(zc, q).wait_send()
-            arrival(zc, q).wait_recv()
-            return c
-
-        return lax.fori_loop(1, n_plane, inner, carry)
-
     lax.fori_loop(1, n_col, finish_col, 0)
-    lax.fori_loop(1, n_plane, finish_plane, 0)
-    lax.fori_loop(1, n_col, finish_relay, 0)
-    local.wait()
-
-
-def gather_tokens(x, col, plane, slot, n_col, n_plane, collective_id):
+
+    def finish_y(k, carry):
+        z = (z0 + k) % n_col
+
+        def each(m, inner):
+            y_copy(z, (y0 + m) % n_y).wait_send()
+            return inner
+
+        return lax.fori_loop(1, n_y, each, carry)
+
+    lax.fori_loop(0, n_col, finish_y, 0)
+
+    def finish_pair(m, carry):
+        y = (y0 + m) % n_y
+
+        def each(k, inner):
+            z = (z0 + k) % n_col
+            pair_copy(y, z).wait_send()
+            arrival(y, z, 1 - c0).wait_recv()
+            return inner
+
+        return lax.fori_loop(0, n_col, each, carry)
+
+    lax.fori_loop(0, n_y, finish_pair, 0)
+
+
+def gather_tokens(x, col, ygroup, slot, n_col, n_y, collective_id):
     return pl.pallas_call(
-        functools.partial(_gather_kernel, n_col, n_plane, col, plane, slot),
-        out_shape=jax.ShapeDtypeStruct((n_col * n_plane,) + x.shape, x.dtype),
+        functools.partial(_gather_kernel, n_col, n_y, col, ygroup, slot),
+        out_shape=jax.ShapeDtypeStruct((n_col * n_y * 2,) + x.shape, x.dtype),
         in_specs=[pl.BlockSpec(memory_space=pltpu.VMEM)],
         out_specs=pl.BlockSpec(memory_space=pltpu.VMEM),
         scratch_shapes=[
             pltpu.SemaphoreType.DMA,
-            pltpu.SemaphoreType.DMA((n_col + n_plane,)),
-            pltpu.SemaphoreType.DMA((n_col, n_plane)),
-            pltpu.SemaphoreType.DMA((n_col, n_plane)),
+            pltpu.SemaphoreType.DMA((n_col,)),
+            pltpu.SemaphoreType.DMA((n_col, n_y)),
+            pltpu.SemaphoreType.DMA((n_y, n_col)),
+            pltpu.SemaphoreType.DMA((n_y, n_col, 2)),
         ],
         compiler_params=pltpu.CompilerParams(collective_id=collective_id, has_side_effects=True),
     )(x)
+
+
+def token_slot(y, z, c):
+    return (y * 4 + z) * 2 + c
 
 
 def _reduce_kernel(n_col, n_y, n_dp, col, ygroup, rows_ref, x_ref, pages_ref, out_ref, pages_out,
@@ -483,10 +512,10 @@
     gathered = gather_tokens(
         hidden_states,
         (column_group, column_member),
-        (plane_group, plane_member),
-        token_block,
+        (same_core_group, same_core_member),
+        token_slot,
         planes,
-        8,
+        4,
         0,
     )
     tokens = gathered.reshape(tokens_total, width)

time: 97.4 us -> 96.5 us (level)
  the two profiles are of different devices: /device:TPU:6 before, /device:TPU:2 now
where the time goes in v12:
time: 96.5 us; the launch traced here: 96.1 us
  Pallas kernels  78.8 us (82%)
  other arithmetic  7.03 us (7%)
  matrix products  5.31 us (6%)
  local copies, waits for them, and re-layouts  4.2 us (4%)
    pallas_call x1, Pallas kernels, gather_tokens(): pl.pallas_call(functools.partial(_gather_kernel, n_col, n_y, col, ygroup,...  31.1 us
    pallas_call x1, Pallas kernels, reduce_rows(): pl.pallas_call(functools.partial(_reduce_kernel, n_col, n_y, n_dp, col, y...  26.1 us
    pallas_call x1, Pallas kernels, exchange_all(): pl.pallas_call(functools.partial(_exchange_kernel, tuple(plans), work, le...  21.5 us
    dot_general x1, matrix products, shards(): jnp.dot(attended, output_weight, preferred_element_type=jnp.float32)  3.3 us
    unnamed x16, local copies, waits for them, and re-layouts  3.08 us

profile of v12, /device:TPU:2, one launch (start us, length us, event | category | flops | bytes accessed | tf_op | source)
XLA Modules:
  0.0 96.1 jit_solution(4373044107398999425)
XLA Ops:
  0.6 0.0 copy-start
  0.6 0.0 copy-start.5
  0.7 31.1 %shard_map.104 = bf16[32,8,2048]{2,1,0:T(8,128)(2,1)} custom-call(bf16[8,2048]{1,0:T(8,128)(2,1)} %x_ref.3), custom_call_target="tpu_custom_call" | custom-call | tf_op jit(solution)/shard_map/pallas_call | solution.py:316
  31.8 0.0 copy-start.1
  31.8 1.5 %convert_reduce_fusion = f32[32,8]{1,0:T(8,128)S(1)} fusion(bf16[32,8,2048]{2,1,0:T(8,128)(2,1)} %shard_map.104), kind=kLoop, calls=%fused_computation.1 | loop fusion | flops 1048320 | bytes 1049600 | tf_op jit(solution)/shard_map/reduce_sum | solution.py:23
  33.3 1.6 %fusion.8 = f32[32,8]{1,0:T(8,128)S(1)} fusion(bf16[32,8,2048]{2,1,0:T(8,128)(2,1)} %shard_map.104, f32[32,8]{1,0:T(8,128)S(1)} %broadcast_multiply_fusion), kind=kLoop, calls=%fused_computation.13 | loop fusion | flops 2096896 | bytes 1050624 | tf_op jit(solution)/shard_map/reduce_sum | solution.py:25
  35.0 0.0 copy-start.3
  35.0 0.1 rsqrt.13
  35.1 0.1 div.19
  35.2 0.0 copy-done
  35.2 0.0 copy-done.5
  35.2 0.0 copy-done.1
  35.2 0.0 copy-start.4
  35.2 0.5 convolution_convert_fusion.1
  35.8 0.1 slice_convert_fusion.1
  35.8 0.0 copy-done.3
  35.9 0.1 compare_reduce_fusion
  35.9 0.1 fusion.51
  36.0 0.3 reduce-window.9
  36.3 0.1 slice.46
  36.5 0.1 slice_reduce_fusion
  36.6 0.1 fusion.52
  36.7 0.6 fusion.33
  37.3 0.1 fusion.57
  37.4 0.7 pad_maximum_fusion
  38.1 0.0 copy-done.4
  38.1 1.4 %fusion.6.refs_1_ = bf16[256,2048]{1,0:T(8,128)(2,1)} fusion(bf16[32,8,2048]{2,1,0:T(8,128)(2,1)S(1)} %copy-done.1, f32[2048]{0:T(1024)S(1)} %copy-done.4, f32[256]{0:T(256)S(1)} %rsqrt.13, f32[256]{0:T(256)S(1)} %div.19), kind=kLoop, calls=%fused_computation.11 | loop fusion | flops 2621440 | bytes 2107392 | tf_op jit(solution)/shard_map/convert_element_type | solution.py:26
  39.5 0.0 copy-start.2
  39.5 21.5 %shard_map.105 = (bf16[4,256,128]{2,1,0:T(8,128)(2,1)}, f32[256,2048]{1,0:T(8,128)}) custom-call(bf16[1,256,128]{2,1,0:T(8,128)(2,1)} %get-tuple-element.20.refs_0_, bf16[256,2048]{1,0:T(8,128)(2,1)} %fusion.6.refs_1_, bf16[2048,256]{1,0:T(8,128)(2,1)} %refs_2_.1, bf16[256,2048]{1,0:T(8,128)(2,1)} %refs_3_.1), custom_call_target="tpu_custom_call" | custom-call | tf_op jit(solution)/shard_map/pallas_call | solution.py:165
  61.0 1.3 %select_reduce_fusion = (f32[256]{0:T(256)S(1)}, f32[256,256]{0,1:T(8,128)S(1)}) fusion(s32[256]{0:T(256)S(1)} %bitcast.49, bf16[4,256,128]{2,1,0:T(8,128)(2,1)} %get-tuple-element.6), kind=kOutput, calls=%fused_computation.25 | convolution fusion | flops 33947392 | bytes 789504 | tf_op jit(solution)/shard_map/dot_general | solution.py:566
  62.4 0.0 copy-start.6
  62.4 0.1 fusion.28
  62.5 0.0 copy-done.2
  62.5 3.3 %fusion = bf16[256,2048]{1,0:T(8,128)(2,1)} fusion(f32[256,2048]{1,0:T(8,128)} %get-tuple-element.7, bf16[64,2048]{1,0:T(8,128)(2,1)S(1)} %copy-done.2, f32[256,256]{0,1:T(8,128)S(1)} %get-tuple-element.24, f32[256]{0:T(256)S(1)} %get-tuple-element.23, s32[256]{0:T(256)S(1)} %bitcast.51, f32[256]{0:T(256)S(1)} %fusion.28, ...), kind=kOutput, calls=%fused_computation.4 | convolution fusion | flops 76972032 | bytes 3739648 | tf_op jit(solution)/shard_map/dot_general | solution.py:575
  65.8 0.0 copy-done.6
  65.9 0.2 convert_reduce_fusion.1
  66.0 0.2 convolution_convert_fusion
  66.2 0.7 reshape.107.pages_ref
  66.9 26.1 %shard_map.106 = (f32[8,2048]{1,0:T(8,128)}, bf16[16,32,128]{2,1,0:T(8,128)(2,1)}) custom-call(bf16[4,4,2,8,2048]{4,3,2,1,0:T(8,128)(2,1)} %bitcast.47, bf16[8,2048]{1,0:T(8,128)(2,1)} %x_ref.3, bf16[16,32,128]{2,1,0:T(8,128)(2,1)} %reshape.107.pages_ref), custom_call_target="tpu_custom_call" | custom-call | tf_op jit(solution)/shard_map/pallas_call | solution.py:453
  93.1 1.5 %copy.29 = f32[8,2048]{1,0:T(8,128)} copy(f32[8,2048]{1,0:T(8,128)} %get-tuple-element.27) | data formatting | bytes 131072
  94.5 1.6 %copy.30 = bf16[1,16,2,16,128]{4,3,2,1,0:T(8,128)(2,1)} copy(bf16[1,16,2,16,128]{4,3,2,1,0:T(8,128)(2,1)} %bitcast.48) | data formatting | bytes 262144
  (6 shorter events, 0.1 us)
Async XLA Ops:
  0.6 34.6 %copy-start = (bf16[2048,192]{0,1:T(8,128)(2,1)S(1)}, bf16[2048,192]{0,1:T(8,128)(2,1)}, u32[]{:S(2)}) copy-start(bf16[2048,192]{0,1:T(8,128)(2,1)} %param.12) | copy-start | bytes 2359300
  0.6 34.5 %copy-start.5 = (f32[2048]{0:T(1024)S(1)}, f32[2048]{0:T(1024)}, u32[]{:S(2)}) copy-start(f32[2048]{0:T(1024)} %param.10) | copy-start | bytes 24580
  31.8 3.4 %copy-start.1 = (bf16[32,8,2048]{2,1,0:T(8,128)(2,1)S(1)}, bf16[32,8,2048]{2,1,0:T(8,128)(2,1)}, u32[]{:S(2)}) copy-start(bf16[32,8,2048]{2,1,0:T(8,128)(2,1)} %shard_map.104) | copy-start | bytes 3145732
  35.0 0.9 copy-start.3
  35.2 2.9 %copy-start.4 = (f32[2048]{0:T(1024)S(1)}, f32[2048]{0:T(1024)}, u32[]{:S(2)}) copy-start(f32[2048]{0:T(1024)} %param.11) | copy-start | bytes 24580
  39.5 23.0 %copy-start.2 = (bf16[64,2048]{1,0:T(8,128)(2,1)S(1)}, bf16[64,2048]{1,0:T(8,128)(2,1)}, u32[]{:S(2)}) copy-start(bf16[64,2048]{1,0:T(8,128)(2,1)} %param.13) | copy-start | bytes 786436
  62.4 3.5 %copy-start.6 = (s32[16,1]{0,1:T(1,128)S(1)}, s32[16,1]{0,1:T(1,128)}, u32[]{:S(2)}) copy-start(s32[16,1]{0,1:T(1,128)} %param.17) | copy-start | bytes 196

commit v13 on v12

--- a/solution.py
+++ b/solution.py
@@ -185,6 +185,26 @@
     out_ref[...] = jnp.dot(hidden, downward_ref[...], preferred_element_type=jnp.float32)
 
 
+def _signal(barrier, groups):
+    index = lax.axis_index("tensor")
+    total = 0
+    for n, position, member in groups:
+        pos = position(index)
+
+        def greet(k, carry, n=n, pos=pos, member=member):
+            pl.semaphore_signal(
+                barrier,
+                inc=1,
+                device_id={"tensor": member(index, (pos + k) % n)},
+                device_id_type=pl.DeviceIdType.MESH,
+            )
+            return carry
+
+        lax.fori_loop(1, n, greet, 0)
+        total += n - 1
+    return total
+
+
 def _greet(barrier, groups, extra=0):
     index = lax.axis_index("tensor")
     total = 0
@@ -333,9 +353,10 @@
     return (y * 4 + z) * 2 + c
 
 
-def _reduce_kernel(n_col, n_y, n_dp, col, ygroup, rows_ref, x_ref, pages_ref, out_ref, pages_out,
-                   inbox0, chip, inbox1, stage, inbox2, sem0, local_sem, send_sem, recv_sem,
-                   send2_sem, recv2_sem, page_local_sem, page_send_sem, page_recv_sem):
+def _reduce_kernel(n_col, n_y, n_dp, col, ygroup, attended_ref, output_ref, feedforward_ref, x_ref,
+                   pages_ref, out_ref, pages_out, rows_ref, inbox0, chip, inbox1, stage, inbox2, sem0,
+                   local_sem, send_sem, recv_sem, send2_sem, recv2_sem, page_local_sem, page_send_sem,
+                   page_recv_sem):
     index = lax.axis_index("tensor")
     cpos, ypos, core = col[0](index), ygroup[0](index), index % 2
     mesh_ids = pl.DeviceIdType.MESH
@@ -356,7 +377,18 @@
 
     lax.fori_loop(1, n_dp, greet_group, 0)
     sibling = (2, lambda t: t % 2, lambda t, q: t - t % 2 + q)
-    _greet(barrier, [sibling, (n_y, *ygroup), (n_col, *col)], extra=n_dp - 1)
+    total = _signal(barrier, [sibling, (n_y, *ygroup), (n_col, *col)])
+
+    product = (
+        jnp.dot(attended_ref[...], output_ref[...], preferred_element_type=jnp.float32)
+        + feedforward_ref[...]
+    )
+    rows = x_ref.shape[0]
+    for owner in range(n_y * n_col * 2):
+        rows_ref[owner // (2 * n_col), (owner // 2) % n_col, owner % 2] = product[
+            owner * rows : (owner + 1) * rows
+        ].astype(rows_ref.dtype)
+    pl.semaphore_wait(barrier, total + n_dp - 1)
     page_local = pltpu.make_async_copy(pages_ref.at[group], pages_out.at[group], page_local_sem)
     page_local.start()
 
@@ -446,24 +478,25 @@
     page_local.wait()
 
 
-def reduce_rows(rows, x, pages, col, ygroup, collective_id):
-    n_y, n_col = rows.shape[0], rows.shape[1]
+def reduce_rows(attended, output_weight, feedforward, x, pages, col, ygroup, n_y, n_col, collective_id):
     block = x.shape
     n_dp = pages.shape[0]
+    operands = (attended, output_weight, feedforward, x, pages)
     return pl.pallas_call(
         functools.partial(_reduce_kernel, n_col, n_y, n_dp, col, ygroup),
         out_shape=(
             jax.ShapeDtypeStruct(block, jnp.float32),
             jax.ShapeDtypeStruct(pages.shape, pages.dtype),
         ),
-        in_specs=[pl.BlockSpec(memory_space=pltpu.VMEM)] * 3,
+        in_specs=[pl.BlockSpec(memory_space=pltpu.VMEM)] * len(operands),
         out_specs=(pl.BlockSpec(memory_space=pltpu.VMEM), pl.BlockSpec(memory_space=pltpu.VMEM)),
         scratch_shapes=[
-            pltpu.VMEM((n_y, n_col) + block, rows.dtype),
-            pltpu.VMEM((n_y, n_col) + block, rows.dtype),
-            pltpu.VMEM((n_col, n_y) + block, rows.dtype),
-            pltpu.VMEM((n_col,) + block, rows.dtype),
-            pltpu.VMEM((n_col,) + block, rows.dtype),
+            pltpu.VMEM((n_y, n_col, 2) + block, x.dtype),
+            pltpu.VMEM((n_y, n_col) + block, x.dtype),
+            pltpu.VMEM((n_y, n_col) + block, x.dtype),
+            pltpu.VMEM((n_col, n_y) + block, x.dtype),
+            pltpu.VMEM((n_col,) + block, x.dtype),
+            pltpu.VMEM((n_col,) + block, x.dtype),
             pltpu.SemaphoreType.DMA((2,)),
             pltpu.SemaphoreType.DMA((n_col,)),
             pltpu.SemaphoreType.DMA((n_col, n_y)),
@@ -475,7 +508,7 @@
             pltpu.SemaphoreType.DMA((n_dp,)),
         ],
         compiler_params=pltpu.CompilerParams(collective_id=collective_id, has_side_effects=True),
-    )(rows, x, pages)
+    )(*operands)
 
 
 def same_core_group(index):
@@ -571,15 +604,16 @@
     mixed = jnp.dot(weights.astype(jnp.bfloat16), value_piece, preferred_element_type=jnp.float32)
     attended = (mixed / weight_sum).astype(jnp.bfloat16)
 
-    partial = (
-        jnp.dot(attended, output_weight, preferred_element_type=jnp.float32) + feedforward
-    ).astype(jnp.bfloat16)
     layer_output, incoming = reduce_rows(
-        partial.reshape(4, planes, 2, local_rows, width),
+        attended,
+        output_weight,
+        feedforward,
         hidden_states,
         outgoing,
         (column_group, column_member),
         (same_core_group, same_core_member),
+        4,
+        planes,
         2,
     )
 

time: 96.5 us -> 94.6 us (0.980)
  matrix products: 5.31 us -> 2.97 us
    dot_general x1, matrix products: 3.3 us -> 0.95 us  [shards(): jnp.dot(weights.astype(jnp.bfloat16), value_piece, preferred_element_type...]
    unnamed x16 -> x14, local copies, waits for them, and re-layouts: 3.08 us -> 3.07 us
where the time goes in v13:
time: 94.6 us; the launch traced here: 94.1 us
  Pallas kernels  79.2 us (84%)
  other arithmetic  7.03 us (7%)
  local copies, waits for them, and re-layouts  4.19 us (4%)
  matrix products  2.97 us (3%)
    pallas_call x1, Pallas kernels, gather_tokens(): pl.pallas_call(functools.partial(_gather_kernel, n_col, n_y, col, ygroup,...  31.1 us
    pallas_call x1, Pallas kernels, reduce_rows(): pl.pallas_call(functools.partial(_reduce_kernel, n_col, n_y, n_dp, col, y...  26.6 us
    pallas_call x1, Pallas kernels, exchange_all(): pl.pallas_call(functools.partial(_exchange_kernel, tuple(plans), work, le...  21.4 us
    unnamed x14, local copies, waits for them, and re-layouts  3.07 us

profile of v13, /device:TPU:2, one launch (start us, length us, event | category | flops | bytes accessed | tf_op | source)
XLA Modules:
  0.0 94.1 jit_solution(7044137434340890436)
XLA Ops:
  0.6 0.0 copy-start
  0.6 0.0 copy-start.4
  0.7 31.1 %shard_map.104 = bf16[32,8,2048]{2,1,0:T(8,128)(2,1)} custom-call(bf16[8,2048]{1,0:T(8,128)(2,1)} %x_ref.3), custom_call_target="tpu_custom_call" | custom-call | tf_op jit(solution)/shard_map/pallas_call | solution.py:336
  31.8 0.0 copy-start.1
  31.8 1.5 %convert_reduce_fusion = f32[32,8]{1,0:T(8,128)S(1)} fusion(bf16[32,8,2048]{2,1,0:T(8,128)(2,1)} %shard_map.104), kind=kLoop, calls=%fused_computation.1 | loop fusion | flops 1048320 | bytes 1049600 | tf_op jit(solution)/shard_map/reduce_sum | solution.py:23
  33.3 1.6 %fusion.7 = f32[32,8]{1,0:T(8,128)S(1)} fusion(bf16[32,8,2048]{2,1,0:T(8,128)(2,1)} %shard_map.104, f32[32,8]{1,0:T(8,128)S(1)} %broadcast_multiply_fusion), kind=kLoop, calls=%fused_computation.11 | loop fusion | flops 2096896 | bytes 1050624 | tf_op jit(solution)/shard_map/reduce_sum | solution.py:25
  35.0 0.0 copy-start.2
  35.0 0.1 rsqrt.13
  35.1 0.1 div.19
  35.2 0.0 copy-done
  35.2 0.0 copy-done.4
  35.2 0.0 copy-done.1
  35.2 0.0 copy-start.3
  35.2 0.5 convolution_convert_fusion.1
  35.8 0.1 slice_convert_fusion.1
  35.8 0.0 copy-done.2
  35.9 0.1 compare_reduce_fusion
  35.9 0.1 fusion.44
  36.0 0.3 reduce-window.9
  36.3 0.1 slice.46
  36.5 0.1 slice_reduce_fusion
  36.6 0.1 fusion.45
  36.7 0.6 fusion.31
  37.3 0.1 fusion.48
  37.4 0.7 pad_maximum_fusion
  38.1 0.0 copy-done.3
  38.1 1.4 %fusion.5.refs_1_ = bf16[256,2048]{1,0:T(8,128)(2,1)} fusion(bf16[32,8,2048]{2,1,0:T(8,128)(2,1)S(1)} %copy-done.1, f32[2048]{0:T(1024)S(1)} %copy-done.3, f32[256]{0:T(256)S(1)} %rsqrt.13, f32[256]{0:T(256)S(1)} %div.19), kind=kLoop, calls=%fused_computation.9 | loop fusion | flops 2621440 | bytes 2107392 | tf_op jit(solution)/shard_map/convert_element_type | solution.py:26
  39.5 21.4 %shard_map.105 = (bf16[4,256,128]{2,1,0:T(8,128)(2,1)}, f32[256,2048]{1,0:T(8,128)}) custom-call(bf16[1,256,128]{2,1,0:T(8,128)(2,1)} %get-tuple-element.20.refs_0_, bf16[256,2048]{1,0:T(8,128)(2,1)} %fusion.5.refs_1_, bf16[2048,256]{1,0:T(8,128)(2,1)} %refs_2_.1, bf16[256,2048]{1,0:T(8,128)(2,1)} %refs_3_.1), custom_call_target="tpu_custom_call" | custom-call | tf_op jit(solution)/shard_map/pallas_call | solution.py:165
  60.9 0.0 copy-start.5
  60.9 1.3 %select_reduce_fusion = (f32[256]{0:T(256)S(1)}, f32[256,256]{0,1:T(8,128)S(1)}) fusion(s32[256]{0:T(256)S(1)} %bitcast.46, bf16[4,256,128]{2,1,0:T(8,128)(2,1)} %get-tuple-element.6), kind=kOutput, calls=%fused_computation.23 | convolution fusion | flops 33947392 | bytes 789504 | tf_op jit(solution)/shard_map/dot_general | solution.py:599
  62.3 0.1 fusion.27
  62.4 0.9 %fusion.9.attended_ref = bf16[256,64]{1,0:T(8,128)(2,1)} fusion(f32[256,256]{0,1:T(8,128)S(1)} %get-tuple-element.24, f32[256]{0:T(256)S(1)} %get-tuple-element.23, s32[256]{0:T(256)S(1)} %bitcast.48, f32[256]{0:T(256)S(1)} %fusion.27, bf16[256,192]{1,0:T(8,128)(2,1)S(1)} %convolution_convert_fusion.1), kind=kOutput, calls=%fused_computation.16 | convolution fusion | flops 8814592 | bytes 364544 | tf_op jit(solution)/shard_map/dot_general | solution.py:604
  63.4 0.0 copy-done.5
  63.4 0.2 convert_reduce_fusion.1
  63.6 0.2 convolution_convert_fusion
  63.7 0.7 reshape.103.pages_ref
  64.5 26.6 %shard_map.106 = (f32[8,2048]{1,0:T(8,128)}, bf16[16,32,128]{2,1,0:T(8,128)(2,1)}) custom-call(bf16[256,64]{1,0:T(8,128)(2,1)} %fusion.9.attended_ref, bf16[64,2048]{1,0:T(8,128)(2,1)} %output_ref.1, f32[256,2048]{1,0:T(8,128)} %get-tuple-element.7.feedforward_ref, bf16[8,2048]{1,0:T(8,128)(2,1)} %x_ref.3, bf16[16,32,128]{2,1,0:T(8,128)(2,1)} %reshape.103.pages_ref), custom_call_target="tpu_custom_call" | custom-call | tf_op jit(solution)/shard_map/pallas_call | solution.py:485
  91.1 1.5 %copy.35 = f32[8,2048]{1,0:T(8,128)} copy(f32[8,2048]{1,0:T(8,128)} %get-tuple-element.27) | data formatting | bytes 131072
  92.6 1.6 %copy.36 = bf16[1,16,2,16,128]{4,3,2,1,0:T(8,128)(2,1)} copy(bf16[1,16,2,16,128]{4,3,2,1,0:T(8,128)(2,1)} %bitcast.45) | data formatting | bytes 262144
  (6 shorter events, 0.1 us)
Async XLA Ops:
  0.6 34.6 %copy-start = (bf16[2048,192]{0,1:T(8,128)(2,1)S(1)}, bf16[2048,192]{0,1:T(8,128)(2,1)}, u32[]{:S(2)}) copy-start(bf16[2048,192]{0,1:T(8,128)(2,1)} %param.12) | copy-start | bytes 2359300
  0.6 34.5 %copy-start.4 = (f32[2048]{0:T(1024)S(1)}, f32[2048]{0:T(1024)}, u32[]{:S(2)}) copy-start(f32[2048]{0:T(1024)} %param.10) | copy-start | bytes 24580
  31.8 3.4 %copy-start.1 = (bf16[32,8,2048]{2,1,0:T(8,128)(2,1)S(1)}, bf16[32,8,2048]{2,1,0:T(8,128)(2,1)}, u32[]{:S(2)}) copy-start(bf16[32,8,2048]{2,1,0:T(8,128)(2,1)} %shard_map.104) | copy-start | bytes 3145732
  35.0 0.9 copy-start.2
  35.2 2.9 %copy-start.3 = (f32[2048]{0:T(1024)S(1)}, f32[2048]{0:T(1024)}, u32[]{:S(2)}) copy-start(f32[2048]{0:T(1024)} %param.11) | copy-start | bytes 24580
  60.9 2.5 %copy-start.5 = (s32[16,1]{0,1:T(1,128)S(1)}, s32[16,1]{0,1:T(1,128)}, u32[]{:S(2)}) copy-start(s32[16,1]{0,1:T(1,128)} %param.17) | copy-start | bytes 196

commit v14 on v13

--- a/solution.py
+++ b/solution.py
@@ -353,7 +353,8 @@
     return (y * 4 + z) * 2 + c
 
 
-def _reduce_kernel(n_col, n_y, n_dp, col, ygroup, attended_ref, output_ref, feedforward_ref, x_ref,
+def _reduce_kernel(n_col, n_y, n_dp, col, ygroup, queries_ref, keys_ref, values_ref, seg_col_ref,
+                   seg_row_ref, output_ref, feedforward_ref, x_ref,
                    pages_ref, out_ref, pages_out, rows_ref, inbox0, chip, inbox1, stage, inbox2, sem0,
                    local_sem, send_sem, recv_sem, send2_sem, recv2_sem, page_local_sem, page_send_sem,
                    page_recv_sem):
@@ -379,8 +380,20 @@
     sibling = (2, lambda t: t % 2, lambda t, q: t - t % 2 + q)
     total = _signal(barrier, [sibling, (n_y, *ygroup), (n_col, *col)])
 
+    scores = lax.dot_general(
+        queries_ref[...], keys_ref[...], (((1,), (1,)), ((), ())), preferred_element_type=jnp.float32
+    ) * (queries_ref.shape[1] ** -0.5)
+    shape = scores.shape
+    allowed = (seg_col_ref[...] == seg_row_ref[...]) & (
+        lax.broadcasted_iota(jnp.int32, shape, 1) <= lax.broadcasted_iota(jnp.int32, shape, 0)
+    )
+    peak = jnp.max(jnp.where(allowed, scores, -jnp.inf), axis=1, keepdims=True)
+    weights = jnp.where(allowed, jnp.exp(scores - peak), 0.0)
+    weight_sum = jnp.sum(weights, axis=1, keepdims=True)
+    mixed = jnp.dot(weights.astype(jnp.bfloat16), values_ref[...], preferred_element_type=jnp.float32)
+    attended = (mixed / weight_sum).astype(jnp.bfloat16)
     product = (
-        jnp.dot(attended_ref[...], output_ref[...], preferred_element_type=jnp.float32)
+        jnp.dot(attended, output_ref[...], preferred_element_type=jnp.float32)
         + feedforward_ref[...]
     )
     rows = x_ref.shape[0]
@@ -478,10 +491,10 @@
     page_local.wait()
 
 
-def reduce_rows(attended, output_weight, feedforward, x, pages, col, ygroup, n_y, n_col, collective_id):
+def reduce_rows(attention, output_weight, feedforward, x, pages, col, ygroup, n_y, n_col, collective_id):
     block = x.shape
     n_dp = pages.shape[0]
-    operands = (attended, output_weight, feedforward, x, pages)
+    operands = (*attention, output_weight, feedforward, x, pages)
     return pl.pallas_call(
         functools.partial(_reduce_kernel, n_col, n_y, n_dp, col, ygroup),
         out_shape=(
@@ -596,16 +609,8 @@
     queries = head_pieces[:, :, :quarter_width].transpose(1, 0, 2).reshape(tokens_total, HD)
     keys = head_pieces[:, :, quarter_width:].transpose(1, 0, 2).reshape(tokens_total, HD)
 
-    scores = jnp.dot(queries, keys.T, preferred_element_type=jnp.float32) * HD ** (-0.5)
-    allowed = (stream[None, :] == stream[:, None]) & (indices[None, :] <= indices[:, None])
-    peak = jnp.max(jnp.where(allowed, scores, -jnp.inf), axis=1, keepdims=True)
-    weights = jnp.where(allowed, jnp.exp(scores - peak), 0.0)
-    weight_sum = jnp.sum(weights, axis=1, keepdims=True)
-    mixed = jnp.dot(weights.astype(jnp.bfloat16), value_piece, preferred_element_type=jnp.float32)
-    attended = (mixed / weight_sum).astype(jnp.bfloat16)
-
     layer_output, incoming = reduce_rows(
-        attended,
+        (queries, keys, value_piece, stream[:, None], stream[None, :]),
         output_weight,
         feedforward,
         hidden_states,

time: 94.6 us -> 96.2 us (1.017)
  local copies, waits for them, and re-layouts: 4.19 us -> 7.91 us
  matrix products: 2.97 us -> 0.69 us
    dot_general x2 -> x0, matrix products: 2.28 us -> none  [the longest x1 1.33 us: shards(): jnp.dot(queries, keys.T, preferred_element_type=jnp.float32) * HD ** (-0.5)]
    reshape x0 -> x2, local copies, waits for them, and re-layouts: none -> 1.52 us  [the longest x1 0.76 us: shards(): head_pieces[:, :, :quarter_width].transpose(1, 0, 2)]
    transpose x0 -> x3, local copies, waits for them, and re-layouts: none -> 1.42 us  [the longest x2 1.29 us: shards(): head_pieces[:, :, quarter_width:].transpose(1, 0, 2)]
    unnamed x14 -> x16, local copies, waits for them, and re-layouts: 3.07 us -> 3.08 us
where the time goes in v14:
time: 96.2 us; the launch traced here: 95.8 us
  Pallas kernels  79.5 us (83%)
  local copies, waits for them, and re-layouts  7.91 us (8%)
  other arithmetic  6.9 us (7%)
    pallas_call x1, Pallas kernels, gather_tokens(): pl.pallas_call(functools.partial(_gather_kernel, n_col, n_y, col, ygroup,...  31.1 us
    pallas_call x1, Pallas kernels, reduce_rows(): pl.pallas_call(functools.partial(_reduce_kernel, n_col, n_y, n_dp, col, y...  26.8 us
    pallas_call x1, Pallas kernels, exchange_all(): pl.pallas_call(functools.partial(_exchange_kernel, tuple(plans), work, le...  21.5 us
    unnamed x16, local copies, waits for them, and re-layouts  3.08 us

profile of v14, /device:TPU:2, one launch (start us, length us, event | category | flops | bytes accessed | tf_op | source)
XLA Modules:
  0.0 95.8 jit_solution(7213563161132831932)
XLA Ops:
  0.6 0.0 copy-start
  0.6 0.0 copy-start.5
  0.7 31.1 %shard_map.104 = bf16[32,8,2048]{2,1,0:T(8,128)(2,1)} custom-call(bf16[8,2048]{1,0:T(8,128)(2,1)} %x_ref.3), custom_call_target="tpu_custom_call" | custom-call | tf_op jit(solution)/shard_map/pallas_call | solution.py:336
  31.8 0.0 copy-start.1
  31.8 1.5 %convert_reduce_fusion = f32[32,8]{1,0:T(8,128)S(1)} fusion(bf16[32,8,2048]{2,1,0:T(8,128)(2,1)} %shard_map.104), kind=kLoop, calls=%fused_computation.1 | loop fusion | flops 1048320 | bytes 1049600 | tf_op jit(solution)/shard_map/reduce_sum | solution.py:23
  33.3 1.6 %fusion.7 = f32[32,8]{1,0:T(8,128)S(1)} fusion(bf16[32,8,2048]{2,1,0:T(8,128)(2,1)} %shard_map.104, f32[32,8]{1,0:T(8,128)S(1)} %broadcast_multiply_fusion), kind=kLoop, calls=%fused_computation.11 | loop fusion | flops 2096896 | bytes 1050624 | tf_op jit(solution)/shard_map/reduce_sum | solution.py:25
  35.0 0.0 copy-start.3
  35.0 0.1 rsqrt.13
  35.1 0.1 div.11
  35.2 0.0 copy-done
  35.2 0.0 copy-done.5
  35.2 0.0 copy-done.1
  35.2 0.0 copy-start.4
  35.2 0.5 convolution_convert_fusion.1
  35.8 0.1 slice_convert_fusion.1
  35.8 0.0 copy-done.3
  35.9 0.1 compare_reduce_fusion
  35.9 0.1 fusion.30
  36.0 0.3 reduce-window.9
  36.3 0.1 slice.46
  36.5 0.1 slice_reduce_fusion
  36.6 0.1 fusion.31
  36.7 0.6 fusion.21
  37.3 0.1 fusion.32
  37.4 0.0 copy-start.2
  37.4 0.7 pad_maximum_fusion
  38.2 0.0 copy-done.4
  38.2 1.4 %fusion.5.refs_1_ = bf16[256,2048]{1,0:T(8,128)(2,1)} fusion(bf16[32,8,2048]{2,1,0:T(8,128)(2,1)S(1)} %copy-done.1, f32[2048]{0:T(1024)S(1)} %copy-done.4, f32[256]{0:T(256)S(1)} %rsqrt.13, f32[256]{0:T(256)S(1)} %div.11), kind=kLoop, calls=%fused_computation.9 | loop fusion | flops 2621440 | bytes 2107392 | tf_op jit(solution)/shard_map/convert_element_type | solution.py:26
  39.5 0.0 copy-start.6
  39.5 21.5 %shard_map.105 = (bf16[4,256,128]{2,1,0:T(8,128)(2,1)}, f32[256,2048]{1,0:T(8,128)}) custom-call(bf16[1,256,128]{2,1,0:T(8,128)(2,1)} %get-tuple-element.22.refs_0_, bf16[256,2048]{1,0:T(8,128)(2,1)} %fusion.5.refs_1_, bf16[2048,256]{1,0:T(8,128)(2,1)} %refs_2_.1, bf16[256,2048]{1,0:T(8,128)(2,1)} %refs_3_.1), custom_call_target="tpu_custom_call" | custom-call | tf_op jit(solution)/shard_map/pallas_call | solution.py:165
  61.1 0.0 copy-done.2
  61.1 1.2 %slice_bitcast_fusion = (bf16[256,4,64]{2,0,1:T(8,128)(2,1)S(1)}, bf16[256,4,64]{2,0,1:T(8,128)(2,1)S(1)}) fusion(bf16[4,256,128]{2,1,0:T(8,128)(2,1)} %get-tuple-element.6), kind=kLoop, calls=%fused_computation.16 | loop fusion | bytes 524288 | tf_op jit(solution)/shard_map/transpose | solution.py:610
  62.2 0.1 copy.28
  62.4 0.8 copy.30.queries_ref
  63.1 0.1 copy.29
  63.3 0.8 copy.31.keys_ref
  64.1 0.0 copy-done.6
  64.1 0.2 convert_reduce_fusion.1
  64.3 0.2 convolution_convert_fusion
  64.4 0.7 reshape.106.pages_ref
  65.1 0.8 copy.32.seg_col_ref
  65.9 26.8 %shard_map.106 = (f32[8,2048]{1,0:T(8,128)}, bf16[16,32,128]{2,1,0:T(8,128)(2,1)}) custom-call(bf16[256,256]{1,0:T(8,128)(2,1)} %copy.30.queries_ref, bf16[256,256]{1,0:T(8,128)(2,1)} %copy.31.keys_ref, bf16[256,64]{1,0:T(8,128)(2,1)} %copy-done.2, s32[256,1]{1,0:T(8,128)} %copy.32.seg_col_ref, s32[1,256]{1,0:T(1,128)} %seg_row_ref.1, ...), custom_call_target="tpu_custom_call" | custom-call | tf_op jit(solution)/shard_map/pallas_call | solution.py:498
  92.7 1.5 %copy.36 = f32[8,2048]{1,0:T(8,128)} copy(f32[8,2048]{1,0:T(8,128)} %get-tuple-element.27) | data formatting | bytes 131072
  94.2 1.6 %copy.37 = bf16[1,16,2,16,128]{4,3,2,1,0:T(8,128)(2,1)} copy(bf16[1,16,2,16,128]{4,3,2,1,0:T(8,128)(2,1)} %bitcast.39) | data formatting | bytes 262144
  (6 shorter events, 0.1 us)
Async XLA Ops:
  0.6 34.6 %copy-start = (bf16[2048,192]{0,1:T(8,128)(2,1)S(1)}, bf16[2048,192]{0,1:T(8,128)(2,1)}, u32[]{:S(2)}) copy-start(bf16[2048,192]{0,1:T(8,128)(2,1)} %param.12) | copy-start | bytes 2359300
  0.6 34.5 %copy-start.5 = (f32[2048]{0:T(1024)S(1)}, f32[2048]{0:T(1024)}, u32[]{:S(2)}) copy-start(f32[2048]{0:T(1024)} %param.10) | copy-start | bytes 24580
  31.8 3.4 %copy-start.1 = (bf16[32,8,2048]{2,1,0:T(8,128)(2,1)S(1)}, bf16[32,8,2048]{2,1,0:T(8,128)(2,1)}, u32[]{:S(2)}) copy-start(bf16[32,8,2048]{2,1,0:T(8,128)(2,1)} %shard_map.104) | copy-start | bytes 3145732
  35.0 0.9 copy-start.3
  35.2 2.9 %copy-start.4 = (f32[2048]{0:T(1024)S(1)}, f32[2048]{0:T(1024)}, u32[]{:S(2)}) copy-start(f32[2048]{0:T(1024)} %param.11) | copy-start | bytes 24580
  37.4 23.6 %copy-start.2 = (bf16[256,64]{1,0:T(8,128)(2,1)}, bf16[256,64]{1,0:T(8,128)(2,1)S(1)}, u32[]{:S(2)}) copy-start(bf16[256,64]{1,0:T(8,128)(2,1)S(1)} %get-tuple-element.16.values_ref) | copy-start | bytes 98308
  39.5 24.5 %copy-start.6 = (s32[16,1]{0,1:T(1,128)S(1)}, s32[16,1]{0,1:T(1,128)}, u32[]{:S(2)}) copy-start(s32[16,1]{0,1:T(1,128)} %param.17) | copy-start | bytes 196

commit v15 on v14

--- a/solution.py
+++ b/solution.py
@@ -353,7 +353,7 @@
     return (y * 4 + z) * 2 + c
 
 
-def _reduce_kernel(n_col, n_y, n_dp, col, ygroup, queries_ref, keys_ref, values_ref, seg_col_ref,
+def _reduce_kernel(n_col, n_y, n_dp, col, ygroup, pieces_ref, values_ref, seg_col_ref,
                    seg_row_ref, output_ref, feedforward_ref, x_ref,
                    pages_ref, out_ref, pages_out, rows_ref, inbox0, chip, inbox1, stage, inbox2, sem0,
                    local_sem, send_sem, recv_sem, send2_sem, recv2_sem, page_local_sem, page_send_sem,
@@ -380,9 +380,16 @@
     sibling = (2, lambda t: t % 2, lambda t, q: t - t % 2 + q)
     total = _signal(barrier, [sibling, (n_y, *ygroup), (n_col, *col)])
 
+    quarter_count, head_dims = pieces_ref.shape[0], pieces_ref.shape[0] * pieces_ref.shape[3]
     scores = lax.dot_general(
-        queries_ref[...], keys_ref[...], (((1,), (1,)), ((), ())), preferred_element_type=jnp.float32
-    ) * (queries_ref.shape[1] ** -0.5)
+        pieces_ref[0, 0], pieces_ref[0, 1], (((1,), (1,)), ((), ())), preferred_element_type=jnp.float32
+    )
+    for quarter in range(1, quarter_count):
+        scores = scores + lax.dot_general(
+            pieces_ref[quarter, 0], pieces_ref[quarter, 1], (((1,), (1,)), ((), ())),
+            preferred_element_type=jnp.float32,
+        )
+    scores = scores * (head_dims ** -0.5)
     shape = scores.shape
     allowed = (seg_col_ref[...] == seg_row_ref[...]) & (
         lax.broadcasted_iota(jnp.int32, shape, 1) <= lax.broadcasted_iota(jnp.int32, shape, 0)
@@ -601,16 +608,14 @@
     outgoing = outgoing.reshape(replica_count, capacity * PAGE, 2 * quarter_width)
     head_pieces, feedforward = exchange_all(
         1,
-        (jnp.concatenate([query_piece, key_piece], 1)[None], "tensor", quarters, True, None),
+        (jnp.stack([query_piece, key_piece])[None], "tensor", quarters, True, None),
         work=(_feedforward_up, _feedforward_down),
         inputs=(normed_feedforward, upward_weight, downward_weight),
         results=(jax.ShapeDtypeStruct((tokens_total, width), jnp.float32),),
     )
-    queries = head_pieces[:, :, :quarter_width].transpose(1, 0, 2).reshape(tokens_total, HD)
-    keys = head_pieces[:, :, quarter_width:].transpose(1, 0, 2).reshape(tokens_total, HD)
 
     layer_output, incoming = reduce_rows(
-        (queries, keys, value_piece, stream[:, None], stream[None, :]),
+        (head_pieces, value_piece, stream[:, None], stream[None, :]),
         output_weight,
         feedforward,
         hidden_states,

time: 96.2 us -> 103 us (1.071)
  the two profiles are of different devices: /device:TPU:2 before, /device:TPU:1 now
where the time goes in v15:
time: 103 us; the launch traced here: 102 us
  Pallas kernels  88.5 us (86%)
  other arithmetic  6.95 us (7%)
  local copies, waits for them, and re-layouts  5 us (5%)
    pallas_call x1, Pallas kernels, exchange_all(): pl.pallas_call(functools.partial(_exchange_kernel, tuple(plans), work, le...  33.3 us
    pallas_call x1, Pallas kernels, gather_tokens(): pl.pallas_call(functools.partial(_gather_kernel, n_col, n_y, col, ygroup,...  32.5 us
    pallas_call x1, Pallas kernels, reduce_rows(): pl.pallas_call(functools.partial(_reduce_kernel, n_col, n_y, n_dp, col, y...  22.7 us
    unnamed x16, local copies, waits for them, and re-layouts  3.08 us

profile of v15, /device:TPU:1, one launch (start us, length us, event | category | flops | bytes accessed | tf_op | source)
XLA Modules:
  0.0 101.9 jit_solution(7733645957027113373)
XLA Ops:
  0.6 0.0 copy-start
  0.6 0.0 copy-start.5
  0.7 32.5 %shard_map.104 = bf16[32,8,2048]{2,1,0:T(8,128)(2,1)} custom-call(bf16[8,2048]{1,0:T(8,128)(2,1)} %x_ref.3), custom_call_target="tpu_custom_call" | custom-call | tf_op jit(solution)/shard_map/pallas_call | solution.py:336
  33.2 0.0 copy-start.1
  33.2 1.5 %convert_reduce_fusion = f32[32,8]{1,0:T(8,128)S(1)} fusion(bf16[32,8,2048]{2,1,0:T(8,128)(2,1)} %shard_map.104), kind=kLoop, calls=%fused_computation.1 | loop fusion | flops 1048320 | bytes 1049600 | tf_op jit(solution)/shard_map/reduce_sum | solution.py:23
  34.7 1.6 %fusion.7 = f32[32,8]{1,0:T(8,128)S(1)} fusion(bf16[32,8,2048]{2,1,0:T(8,128)(2,1)} %shard_map.104, f32[32,8]{1,0:T(8,128)S(1)} %broadcast_multiply_fusion), kind=kLoop, calls=%fused_computation.11 | loop fusion | flops 2096896 | bytes 1050624 | tf_op jit(solution)/shard_map/reduce_sum | solution.py:25
  36.3 0.0 copy-start.3
  36.4 0.1 rsqrt.13
  36.4 0.1 div.11
  36.5 0.0 copy-done
  36.5 0.0 copy-done.5
  36.6 0.0 copy-done.1
  36.6 0.0 copy-start.4
  36.6 0.5 convolution_convert_fusion.1
  37.1 0.1 slice_convert_fusion.1
  37.2 0.0 copy-done.3
  37.2 0.1 compare_reduce_fusion
  37.3 0.1 fusion.31
  37.4 0.3 reduce-window.9
  37.7 0.1 slice.40
  37.8 0.1 slice_reduce_fusion
  37.9 0.1 fusion.32
  38.0 0.6 fusion.21
  38.6 0.1 fusion.33
  38.8 0.0 copy-start.2
  38.8 0.7 maximum_bitcast_fusion.refs_0_
  39.5 0.0 copy-done.4
  39.5 1.4 %fusion.5.refs_1_ = bf16[256,2048]{1,0:T(8,128)(2,1)} fusion(bf16[32,8,2048]{2,1,0:T(8,128)(2,1)S(1)} %copy-done.1, f32[2048]{0:T(1024)S(1)} %copy-done.4, f32[256]{0:T(256)S(1)} %rsqrt.13, f32[256]{0:T(256)S(1)} %div.11), kind=kLoop, calls=%fused_computation.9 | loop fusion | flops 2621440 | bytes 2107392 | tf_op jit(solution)/shard_map/convert_element_type | solution.py:26
  40.8 0.0 copy-start.6
  40.8 33.3 %shard_map.105 = (bf16[4,2,256,64]{3,2,1,0:T(8,128)(2,1)}, f32[256,2048]{1,0:T(8,128)}) custom-call(bf16[1,2,256,64]{3,2,1,0:T(8,128)(2,1)} %maximum_bitcast_fusion.refs_0_, bf16[256,2048]{1,0:T(8,128)(2,1)} %fusion.5.refs_1_, bf16[2048,256]{1,0:T(8,128)(2,1)} %refs_2_.1, bf16[256,2048]{1,0:T(8,128)(2,1)} %refs_3_.1), custom_call_target="tpu_custom_call" | custom-call | tf_op jit(solution)/shard_map/pallas_call | solution.py:165
  74.2 0.0 copy-done.2
  74.2 0.1 pad_maximum_fusion
  74.3 0.0 copy-done.6
  74.3 0.2 convert_reduce_fusion.1
  74.5 0.2 convolution_convert_fusion
  74.7 0.7 reshape.98.pages_ref
  75.4 0.8 copy.18.seg_col_ref
  76.2 22.7 %shard_map.106 = (f32[8,2048]{1,0:T(8,128)}, bf16[16,32,128]{2,1,0:T(8,128)(2,1)}) custom-call(bf16[4,2,256,64]{3,2,1,0:T(8,128)(2,1)} %get-tuple-element.6.pieces_ref, bf16[256,64]{1,0:T(8,128)(2,1)} %copy-done.2, s32[256,1]{1,0:T(8,128)} %copy.18.seg_col_ref, s32[1,256]{1,0:T(1,128)} %seg_row_ref.1, bf16[64,2048]{1,0:T(8,128)(2,1)} %output_ref.1, ...), custom_call_target="tpu_custom_call" | custom-call | tf_op jit(solution)/shard_map/pallas_call | solution.py:505
  98.9 1.5 %copy.22 = f32[8,2048]{1,0:T(8,128)} copy(f32[8,2048]{1,0:T(8,128)} %get-tuple-element.23) | data formatting | bytes 131072
  100.3 1.6 %copy.23 = bf16[1,16,2,16,128]{4,3,2,1,0:T(8,128)(2,1)} copy(bf16[1,16,2,16,128]{4,3,2,1,0:T(8,128)(2,1)} %bitcast.35) | data formatting | bytes 262144
  (6 shorter events, 0.1 us)
Async XLA Ops:
  0.6 35.9 %copy-start = (bf16[2048,192]{0,1:T(8,128)(2,1)S(1)}, bf16[2048,192]{0,1:T(8,128)(2,1)}, u32[]{:S(2)}) copy-start(bf16[2048,192]{0,1:T(8,128)(2,1)} %param.12) | copy-start | bytes 2359300
  0.6 35.9 %copy-start.5 = (f32[2048]{0:T(1024)S(1)}, f32[2048]{0:T(1024)}, u32[]{:S(2)}) copy-start(f32[2048]{0:T(1024)} %param.10) | copy-start | bytes 24580
  33.2 3.4 %copy-start.1 = (bf16[32,8,2048]{2,1,0:T(8,128)(2,1)S(1)}, bf16[32,8,2048]{2,1,0:T(8,128)(2,1)}, u32[]{:S(2)}) copy-start(bf16[32,8,2048]{2,1,0:T(8,128)(2,1)} %shard_map.104) | copy-start | bytes 3145732
  36.3 0.9 copy-start.3
  36.6 2.9 %copy-start.4 = (f32[2048]{0:T(1024)S(1)}, f32[2048]{0:T(1024)}, u32[]{:S(2)}) copy-start(f32[2048]{0:T(1024)} %param.11) | copy-start | bytes 24580
  38.8 35.4 %copy-start.2 = (bf16[256,64]{1,0:T(8,128)(2,1)}, bf16[256,64]{1,0:T(8,128)(2,1)S(1)}, u32[]{:S(2)}) copy-start(bf16[256,64]{1,0:T(8,128)(2,1)S(1)} %get-tuple-element.14.values_ref) | copy-start | bytes 98308
  40.8 33.5 %copy-start.6 = (s32[16,1]{0,1:T(1,128)S(1)}, s32[16,1]{0,1:T(1,128)}, u32[]{:S(2)}) copy-start(s32[16,1]{0,1:T(1,128)} %param.17) | copy-start | bytes 196

commit v16 on v13

--- a/solution.py
+++ b/solution.py
@@ -568,9 +568,7 @@
     key_piece = jnp.where(leading, rotate_leading(key_piece, offsets, ROT), key_piece)
 
     page_count = tokens_total // PAGE
-    page_rows = jnp.concatenate([key_piece, value_piece], 1).reshape(
-        page_count, PAGE * 2 * quarter_width
-    )
+    page_rows = jnp.concatenate([key_piece, value_piece], 1)
     targets = page_targets[:, 0]
     page_numbers = jnp.arange(page_count, dtype=jnp.int32)
     earlier = jnp.sum(
@@ -581,8 +579,12 @@
     )
     capacity = 2 * page_count // replica_count
     slot_numbers = targets * capacity + earlier
+    token_slots = jnp.repeat(slot_numbers, PAGE)
+    slot_rows = jnp.arange(replica_count * capacity * PAGE, dtype=jnp.int32)
+    token_numbers = jnp.arange(tokens_total, dtype=jnp.int32)
     placing = (
-        jnp.arange(replica_count * capacity, dtype=jnp.int32)[:, None] == slot_numbers[None, :]
+        (token_slots[None, :] == slot_rows[:, None] // PAGE)
+        & (token_numbers[None, :] % PAGE == slot_rows[:, None] % PAGE)
     ).astype(jnp.bfloat16)
     outgoing = jnp.dot(placing, page_rows, preferred_element_type=jnp.float32).astype(jnp.bfloat16)
     outgoing = outgoing.reshape(replica_count, capacity * PAGE, 2 * quarter_width)

time: 94.6 us -> 96.9 us (1.024)
  other arithmetic: 7.03 us -> 9.18 us
    unnamed x14 -> x12, local copies, waits for them, and re-layouts: 3.07 us -> 3.07 us
where the time goes in v16:
time: 96.9 us; the launch traced here: 96.4 us
  Pallas kernels  79 us (82%)
  other arithmetic  9.18 us (9%)
  matrix products  3.82 us (4%)
  local copies, waits for them, and re-layouts  3.59 us (4%)
    pallas_call x1, Pallas kernels, gather_tokens(): pl.pallas_call(functools.partial(_gather_kernel, n_col, n_y, col, ygroup,...  31 us
    pallas_call x1, Pallas kernels, reduce_rows(): pl.pallas_call(functools.partial(_reduce_kernel, n_col, n_y, n_dp, col, y...  26.6 us
    pallas_call x1, Pallas kernels, exchange_all(): pl.pallas_call(functools.partial(_exchange_kernel, tuple(plans), work, le...  21.4 us
    unnamed x12, local copies, waits for them, and re-layouts  3.07 us

profile of v16, /device:TPU:2, one launch (start us, length us, event | category | flops | bytes accessed | tf_op | source)
XLA Modules:
  0.0 96.4 jit_solution(226143032677015413)
XLA Ops:
  0.6 0.0 copy-start
  0.6 0.0 copy-start.4
  0.7 0.9 convert_reduce_fusion.1
  1.6 0.7 multiply_add_fusion
  2.3 0.8 compare_reduce_fusion
  3.1 0.1 fusion.60
  3.2 0.3 reduce-window.9
  3.5 0.1 slice.46
  3.6 0.1 slice_reduce_fusion
  3.7 0.1 fusion.61
  3.8 0.1 broadcast_in_dim.16
  3.9 0.1 eq.73
  4.0 31.0 %shard_map.104 = bf16[32,8,2048]{2,1,0:T(8,128)(2,1)} custom-call(bf16[8,2048]{1,0:T(8,128)(2,1)} %x_ref.3), custom_call_target="tpu_custom_call" | custom-call | tf_op jit(solution)/shard_map/pallas_call | solution.py:336
  35.0 0.0 copy-start.1
  35.0 1.5 %convert_reduce_fusion = f32[32,8]{1,0:T(8,128)S(1)} fusion(bf16[32,8,2048]{2,1,0:T(8,128)(2,1)} %shard_map.104), kind=kLoop, calls=%fused_computation.1 | loop fusion | flops 1048320 | bytes 1049600 | tf_op jit(solution)/shard_map/reduce_sum | solution.py:23
  36.5 0.1 div.27
  36.6 0.0 copy-start.3
  36.6 1.6 %fusion.7 = f32[32,8]{1,0:T(8,128)S(1)} fusion(bf16[32,8,2048]{2,1,0:T(8,128)(2,1)} %shard_map.104, f32[32,8]{1,0:T(8,128)S(1)} %broadcast_multiply_fusion), kind=kLoop, calls=%fused_computation.10 | loop fusion | flops 2096896 | bytes 1050624 | tf_op jit(solution)/shard_map/reduce_sum | solution.py:25
  38.3 0.1 rsqrt.13
  38.4 0.0 copy-done
  38.4 0.0 copy-done.4
  38.4 0.0 copy-done.1
  38.4 0.5 convolution_convert_fusion.1
  38.9 0.0 copy-done.3
  38.9 1.4 %fusion.5.refs_1_ = bf16[256,2048]{1,0:T(8,128)(2,1)} fusion(bf16[32,8,2048]{2,1,0:T(8,128)(2,1)S(1)} %copy-done.1, f32[2048]{0:T(1024)S(1)} %copy-done.3, f32[256]{0:T(256)S(1)} %rsqrt.13, f32[256]{0:T(256)S(1)} %div.27), kind=kLoop, calls=%fused_computation.8 | loop fusion | flops 2621440 | bytes 2107392 | tf_op jit(solution)/shard_map/convert_element_type | solution.py:26
  40.3 0.1 slice_convert_fusion.1
  40.4 0.6 fusion.38
  41.0 0.1 fusion.65
  41.2 0.0 copy-start.2
  41.2 1.0 %convolution_convert_fusion = bf16[512,128]{1,0:T(8,128)(2,1)} fusion(s32[256]{0:T(256)S(1)} %and_select_fusion, s32[256]{0:T(256)S(1)} %eq.73, s32[512]{0:T(512)S(1)} %get-tuple-element.23, s32[512]{0:T(512)S(1)} %get-tuple-element.24, bf16[256,64]{1,0:T(8,128)(2,1)S(1)} %get-tuple-element.14, bf16[256,64]{1,0:T(8,128)(2,1)S(1)} %get-tuple-element.16), kind=kOutput, calls=%fused_computation.13 | convolution fusion | flops 34144256 | bytes 202752 | tf_op jit(solution)/shard_map/dot_general | solution.py:589
  42.2 0.7 maximum_bitcast_fusion.refs_0_
  42.9 21.4 %shard_map.105 = (bf16[4,256,128]{2,1,0:T(8,128)(2,1)}, f32[256,2048]{1,0:T(8,128)}) custom-call(bf16[1,256,128]{2,1,0:T(8,128)(2,1)} %maximum_bitcast_fusion.refs_0_, bf16[256,2048]{1,0:T(8,128)(2,1)} %fusion.5.refs_1_, bf16[2048,256]{1,0:T(8,128)(2,1)} %refs_2_.1, bf16[256,2048]{1,0:T(8,128)(2,1)} %refs_3_.1), custom_call_target="tpu_custom_call" | custom-call | tf_op jit(solution)/shard_map/pallas_call | solution.py:165
  64.3 0.0 copy-done.2
  64.3 1.3 %select_reduce_fusion = (f32[256]{0:T(256)S(1)}, f32[256,256]{0,1:T(8,128)S(1)}) fusion(s32[256]{0:T(256)S(1)} %bitcast.47, bf16[4,256,128]{2,1,0:T(8,128)(2,1)} %get-tuple-element.6), kind=kOutput, calls=%fused_computation.28 | convolution fusion | flops 33947392 | bytes 789504 | tf_op jit(solution)/shard_map/dot_general | solution.py:601
  65.6 0.1 fusion.34
  65.8 0.9 fusion.9.attended_ref
  66.7 26.6 %shard_map.106 = (f32[8,2048]{1,0:T(8,128)}, bf16[16,32,128]{2,1,0:T(8,128)(2,1)}) custom-call(bf16[256,64]{1,0:T(8,128)(2,1)} %fusion.9.attended_ref, bf16[64,2048]{1,0:T(8,128)(2,1)} %output_ref.1, f32[256,2048]{1,0:T(8,128)} %get-tuple-element.7.feedforward_ref, bf16[8,2048]{1,0:T(8,128)(2,1)} %x_ref.3, bf16[16,32,128]{2,1,0:T(8,128)(2,1)} %bitcast.45), custom_call_target="tpu_custom_call" | custom-call | tf_op jit(solution)/shard_map/pallas_call | solution.py:485
  93.4 1.5 %copy.35 = f32[8,2048]{1,0:T(8,128)} copy(f32[8,2048]{1,0:T(8,128)} %get-tuple-element.27) | data formatting | bytes 131072
  94.8 1.6 %copy.36 = bf16[1,16,2,16,128]{4,3,2,1,0:T(8,128)(2,1)} copy(bf16[1,16,2,16,128]{4,3,2,1,0:T(8,128)(2,1)} %bitcast.46) | data formatting | bytes 262144
  (6 shorter events, 0.1 us)
Async XLA Ops:
  0.6 37.7 %copy-start = (bf16[2048,192]{0,1:T(8,128)(2,1)S(1)}, bf16[2048,192]{0,1:T(8,128)(2,1)}, u32[]{:S(2)}) copy-start(bf16[2048,192]{0,1:T(8,128)(2,1)} %param.12) | copy-start | bytes 2359300
  0.6 37.7 %copy-start.4 = (f32[2048]{0:T(1024)S(1)}, f32[2048]{0:T(1024)}, u32[]{:S(2)}) copy-start(f32[2048]{0:T(1024)} %param.10) | copy-start | bytes 24580
  35.0 3.4 %copy-start.1 = (bf16[32,8,2048]{2,1,0:T(8,128)(2,1)S(1)}, bf16[32,8,2048]{2,1,0:T(8,128)(2,1)}, u32[]{:S(2)}) copy-start(bf16[32,8,2048]{2,1,0:T(8,128)(2,1)} %shard_map.104) | copy-start | bytes 3145732
  36.6 2.3 %copy-start.3 = (f32[2048]{0:T(1024)S(1)}, f32[2048]{0:T(1024)}, u32[]{:S(2)}) copy-start(f32[2048]{0:T(1024)} %param.11) | copy-start | bytes 24580
  41.2 23.1 %copy-start.2 = (s32[1,256]{1,0:T(1,128)S(1)}, s32[1,256]{1,0:T(1,128)}, u32[]{:S(2)}) copy-start(s32[1,256]{1,0:T(1,128)} %param.16) | copy-start | bytes 3076

commit v17 on v13

--- a/solution.py
+++ b/solution.py
@@ -552,8 +552,21 @@
         0,
     )
     tokens = gathered.reshape(tokens_total, width)
-    normed_attention = layer_norm(tokens, attention_gain)
-    normed_feedforward = layer_norm(tokens, feedforward_gain)
+    ones = jnp.ones((width, 1), jnp.bfloat16)
+    center = jnp.dot(tokens, ones, preferred_element_type=jnp.float32) / width
+    shifted = tokens.astype(jnp.float32) - center
+    spread = (
+        jnp.dot(
+            shifted * shifted,
+            ones.astype(jnp.float32),
+            precision=lax.Precision.HIGHEST,
+            preferred_element_type=jnp.float32,
+        )
+        / width
+    )
+    scaled = shifted * lax.rsqrt(spread + epsilon)
+    normed_attention = (scaled * attention_gain).astype(jnp.bfloat16)
+    normed_feedforward = (scaled * feedforward_gain).astype(jnp.bfloat16)
     joined = jnp.dot(normed_attention, heads_weight, preferred_element_type=jnp.float32).astype(
         jnp.bfloat16
     )

time: 94.6 us -> 96.1 us (1.016)
  matrix products: 2.97 us -> 7.76 us
  other arithmetic: 7.03 us -> 3.87 us
    dot_general x0 -> x2, matrix products: none -> 4.79 us  [the longest x1 3.11 us: shards(): jnp.dot(shifted * shifted, ones.astype(jnp.float32), precision=lax.Precis...]
    reduce_sum x2 -> x0, other arithmetic: 3.17 us -> none  [the longest x1 1.64 us: layer_norm(): spread = jnp.mean(shifted * shifted, axis=-1, keepdims=True)]
where the time goes in v17:
time: 96.1 us; the launch traced here: 95.7 us
  Pallas kernels  79.2 us (82%)
  matrix products  7.76 us (8%)
  local copies, waits for them, and re-layouts  4.11 us (4%)
  other arithmetic  3.87 us (4%)
    pallas_call x1, Pallas kernels, gather_tokens(): pl.pallas_call(functools.partial(_gather_kernel, n_col, n_y, col, ygroup,...  31.1 us
    pallas_call x1, Pallas kernels, reduce_rows(): pl.pallas_call(functools.partial(_reduce_kernel, n_col, n_y, n_dp, col, y...  26.6 us
    pallas_call x1, Pallas kernels, exchange_all(): pl.pallas_call(functools.partial(_exchange_kernel, tuple(plans), work, le...  21.4 us
    dot_general x1, matrix products, shards(): jnp.dot(shifted * shifted, ones.astype(jnp.float32), precision=lax.Precis...  3.11 us
    unnamed x14, local copies, waits for them, and re-layouts  3.08 us

profile of v17, /device:TPU:2, one launch (start us, length us, event | category | flops | bytes accessed | tf_op | source)
XLA Modules:
  0.0 95.7 jit_solution(13462025973999332559)
XLA Ops:
  0.6 0.0 copy-start
  0.6 0.0 copy-start.4
  0.7 31.1 %shard_map.104 = bf16[32,8,2048]{2,1,0:T(8,128)(2,1)} custom-call(bf16[8,2048]{1,0:T(8,128)(2,1)} %x_ref.3), custom_call_target="tpu_custom_call" | custom-call | tf_op jit(solution)/shard_map/pallas_call | solution.py:336
  31.8 0.0 copy-start.1
  31.8 1.7 %fusion.7 = f32[1,256]{1,0:T(1,128)S(1)} fusion(bf16[32,8,2048]{2,1,0:T(8,128)(2,1)} %shard_map.104), kind=kOutput, calls=%fused_computation.14 | convolution fusion | flops 1048576 | bytes 1049600 | tf_op jit(solution)/shard_map/dot_general | solution.py:556
  33.5 0.1 sub.38
  33.6 3.1 %fusion = f32[1,256]{1,0:T(1,128)S(1)} fusion(bf16[32,8,2048]{2,1,0:T(8,128)(2,1)} %shard_map.104, f32[32,8]{1,0:T(8,128)S(1)} %sub.38), kind=kOutput, calls=%fused_computation.1 | convolution fusion | flops 7864320 | bytes 1050624 | tf_op jit(solution)/shard_map/dot_general | solution.py:559
  36.7 0.0 copy-start.2
  36.7 0.0 copy-done
  36.7 0.0 copy-done.4
  36.7 0.0 copy-done.1
  36.7 0.0 copy-start.3
  36.8 0.5 convolution_convert_fusion.1
  37.3 0.1 slice_convert_fusion.1
  37.4 0.0 copy-done.2
  37.4 0.1 compare_reduce_fusion
  37.5 0.1 fusion.46
  37.6 0.3 reduce-window.9
  37.9 0.1 slice.46
  38.0 0.1 slice_reduce_fusion
  38.1 0.1 fusion.47
  38.2 0.6 fusion.31
  38.8 0.1 fusion.52
  38.9 0.7 pad_maximum_fusion
  39.7 0.0 copy-done.3
  39.7 1.4 %multiply_convert_fusion.refs_1_ = bf16[256,2048]{1,0:T(8,128)(2,1)} fusion(bf16[32,8,2048]{2,1,0:T(8,128)(2,1)S(1)} %copy-done.1, f32[2048]{0:T(1024)S(1)} %copy-done.3, f32[256]{0:T(256)S(1)} %add_rsqrt_fusion, f32[256]{0:T(256)S(1)} %broadcast_multiply_fusion), kind=kLoop, calls=%fused_computation.3 | loop fusion | flops 2621440 | bytes 2107392 | tf_op jit(solution)/shard_map/convert_element_type | solution.py:569
  41.1 21.4 %shard_map.105 = (bf16[4,256,128]{2,1,0:T(8,128)(2,1)}, f32[256,2048]{1,0:T(8,128)}) custom-call(bf16[1,256,128]{2,1,0:T(8,128)(2,1)} %get-tuple-element.20.refs_0_, bf16[256,2048]{1,0:T(8,128)(2,1)} %multiply_convert_fusion.refs_1_, bf16[2048,256]{1,0:T(8,128)(2,1)} %refs_2_.1, bf16[256,2048]{1,0:T(8,128)(2,1)} %refs_3_.1), custom_call_target="tpu_custom_call" | custom-call | tf_op jit(solution)/shard_map/pallas_call | solution.py:165
  62.5 0.0 copy-start.5
  62.5 1.3 %select_reduce_fusion = (f32[256]{0:T(256)S(1)}, f32[256,256]{0,1:T(8,128)S(1)}) fusion(s32[256]{0:T(256)S(1)} %bitcast.44, bf16[4,256,128]{2,1,0:T(8,128)(2,1)} %get-tuple-element.6), kind=kOutput, calls=%fused_computation.24 | convolution fusion | flops 33947392 | bytes 789504 | tf_op jit(solution)/shard_map/dot_general | solution.py:612
  63.8 0.1 fusion.27
  63.9 0.9 fusion.6.attended_ref
  64.9 0.0 copy-done.5
  64.9 0.2 convert_reduce_fusion
  65.1 0.2 convolution_convert_fusion
  65.3 0.7 reshape.87.pages_ref
  66.0 26.6 %shard_map.106 = (f32[8,2048]{1,0:T(8,128)}, bf16[16,32,128]{2,1,0:T(8,128)(2,1)}) custom-call(bf16[256,64]{1,0:T(8,128)(2,1)} %fusion.6.attended_ref, bf16[64,2048]{1,0:T(8,128)(2,1)} %output_ref.1, f32[256,2048]{1,0:T(8,128)} %get-tuple-element.7.feedforward_ref, bf16[8,2048]{1,0:T(8,128)(2,1)} %x_ref.3, bf16[16,32,128]{2,1,0:T(8,128)(2,1)} %reshape.87.pages_ref), custom_call_target="tpu_custom_call" | custom-call | tf_op jit(solution)/shard_map/pallas_call | solution.py:485
  92.6 1.5 %copy.35 = f32[8,2048]{1,0:T(8,128)} copy(f32[8,2048]{1,0:T(8,128)} %get-tuple-element.27) | data formatting | bytes 131072
  94.1 1.6 %copy.36 = bf16[1,16,2,16,128]{4,3,2,1,0:T(8,128)(2,1)} copy(bf16[1,16,2,16,128]{4,3,2,1,0:T(8,128)(2,1)} %bitcast.43) | data formatting | bytes 262144
  (6 shorter events, 0.1 us)
Async XLA Ops:
  0.6 36.1 %copy-start = (bf16[2048,192]{0,1:T(8,128)(2,1)S(1)}, bf16[2048,192]{0,1:T(8,128)(2,1)}, u32[]{:S(2)}) copy-start(bf16[2048,192]{0,1:T(8,128)(2,1)} %param.12) | copy-start | bytes 2359300
  0.6 36.1 %copy-start.4 = (f32[2048]{0:T(1024)S(1)}, f32[2048]{0:T(1024)}, u32[]{:S(2)}) copy-start(f32[2048]{0:T(1024)} %param.10) | copy-start | bytes 24580
  31.8 4.9 %copy-start.1 = (bf16[32,8,2048]{2,1,0:T(8,128)(2,1)S(1)}, bf16[32,8,2048]{2,1,0:T(8,128)(2,1)}, u32[]{:S(2)}) copy-start(bf16[32,8,2048]{2,1,0:T(8,128)(2,1)} %shard_map.104) | copy-start | bytes 3145732
  36.7 0.7 copy-start.2
  36.7 2.9 %copy-start.3 = (f32[2048]{0:T(1024)S(1)}, f32[2048]{0:T(1024)}, u32[]{:S(2)}) copy-start(f32[2048]{0:T(1024)} %param.11) | copy-start | bytes 24580
  62.5 2.5 %copy-start.5 = (s32[16,1]{0,1:T(1,128)S(1)}, s32[16,1]{0,1:T(1,128)}, u32[]{:S(2)}) copy-start(s32[16,1]{0,1:T(1,128)} %param.17) | copy-start | bytes 196

commit v18 on v13

--- a/solution.py
+++ b/solution.py
@@ -389,14 +389,6 @@
             owner * rows : (owner + 1) * rows
         ].astype(rows_ref.dtype)
     pl.semaphore_wait(barrier, total + n_dp - 1)
-    page_local = pltpu.make_async_copy(pages_ref.at[group], pages_out.at[group], page_local_sem)
-    page_local.start()
-
-    def send_pages(k, carry):
-        page_copy((group + k) % n_dp, group).start()
-        return carry
-
-    lax.fori_loop(1, n_dp, send_pages, 0)
 
     pair = pltpu.make_async_remote_copy(
         rows_ref.at[:, :, 1 - core], inbox0, sem0.at[0], sem0.at[1],
@@ -451,6 +443,15 @@
     for z, local in zip(order[:-1], locals_[:-1]):
         stage[z] = plane_sum(z, local).astype(stage.dtype)
         col_copy(z, cpos).start()
+
+    page_local = pltpu.make_async_copy(pages_ref.at[group], pages_out.at[group], page_local_sem)
+    page_local.start()
+
+    def send_pages(k, carry):
+        page_copy((group + k) % n_dp, group).start()
+        return carry
+
+    lax.fori_loop(1, n_dp, send_pages, 0)
 
     result = x_ref[...].astype(jnp.float32) + plane_sum(cpos, locals_[-1])
 

time: 94.6 us -> 94.8 us (level)
  the two profiles are of different devices: /device:TPU:2 before, /device:TPU:32 now
where the time goes in v18:
time: 94.8 us; the launch traced here: 94.4 us
  Pallas kernels  79.4 us (84%)
  other arithmetic  7.03 us (7%)
  local copies, waits for them, and re-layouts  4.19 us (4%)
  matrix products  2.97 us (3%)
    pallas_call x1, Pallas kernels, gather_tokens(): pl.pallas_call(functools.partial(_gather_kernel, n_col, n_y, col, ygroup,...  32.6 us
    pallas_call x1, Pallas kernels, reduce_rows(): pl.pallas_call(functools.partial(_reduce_kernel, n_col, n_y, n_dp, col, y...  30.8 us
    pallas_call x1, Pallas kernels, exchange_all(): pl.pallas_call(functools.partial(_exchange_kernel, tuple(plans), work, le...  15.9 us
    unnamed x14, local copies, waits for them, and re-layouts  3.07 us

profile of v18, /device:TPU:32, one launch (start us, length us, event | category | flops | bytes accessed | tf_op | source)
XLA Modules:
  0.0 94.4 jit_solution(17042932411516764264)
XLA Ops:
  0.6 0.0 copy-start
  0.6 0.0 copy-start.4
  0.7 32.6 %shard_map.104 = bf16[32,8,2048]{2,1,0:T(8,128)(2,1)} custom-call(bf16[8,2048]{1,0:T(8,128)(2,1)} %x_ref.3), custom_call_target="tpu_custom_call" | custom-call | tf_op jit(solution)/shard_map/pallas_call | solution.py:336
  33.3 0.0 copy-start.1
  33.3 1.5 %convert_reduce_fusion = f32[32,8]{1,0:T(8,128)S(1)} fusion(bf16[32,8,2048]{2,1,0:T(8,128)(2,1)} %shard_map.104), kind=kLoop, calls=%fused_computation.1 | loop fusion | flops 1048320 | bytes 1049600 | tf_op jit(solution)/shard_map/reduce_sum | solution.py:23
  34.9 1.6 %fusion.7 = f32[32,8]{1,0:T(8,128)S(1)} fusion(bf16[32,8,2048]{2,1,0:T(8,128)(2,1)} %shard_map.104, f32[32,8]{1,0:T(8,128)S(1)} %broadcast_multiply_fusion), kind=kLoop, calls=%fused_computation.11 | loop fusion | flops 2096896 | bytes 1050624 | tf_op jit(solution)/shard_map/reduce_sum | solution.py:25
  36.5 0.0 copy-start.2
  36.5 0.1 rsqrt.13
  36.6 0.1 div.19
  36.7 0.0 copy-done
  36.7 0.0 copy-done.4
  36.7 0.0 copy-done.1
  36.7 0.0 copy-start.3
  36.7 0.5 convolution_convert_fusion.1
  37.3 0.1 slice_convert_fusion.1
  37.4 0.0 copy-done.2
  37.4 0.1 compare_reduce_fusion
  37.5 0.1 fusion.44
  37.5 0.3 reduce-window.9
  37.9 0.1 slice.46
  38.0 0.1 slice_reduce_fusion
  38.1 0.1 fusion.45
  38.2 0.6 fusion.31
  38.8 0.1 fusion.48
  38.9 0.7 pad_maximum_fusion
  39.7 0.0 copy-done.3
  39.7 1.4 %fusion.5.refs_1_ = bf16[256,2048]{1,0:T(8,128)(2,1)} fusion(bf16[32,8,2048]{2,1,0:T(8,128)(2,1)S(1)} %copy-done.1, f32[2048]{0:T(1024)S(1)} %copy-done.3, f32[256]{0:T(256)S(1)} %rsqrt.13, f32[256]{0:T(256)S(1)} %div.19), kind=kLoop, calls=%fused_computation.9 | loop fusion | flops 2621440 | bytes 2107392 | tf_op jit(solution)/shard_map/convert_element_type | solution.py:26
  41.0 15.9 %shard_map.105 = (bf16[4,256,128]{2,1,0:T(8,128)(2,1)}, f32[256,2048]{1,0:T(8,128)}) custom-call(bf16[1,256,128]{2,1,0:T(8,128)(2,1)} %get-tuple-element.20.refs_0_, bf16[256,2048]{1,0:T(8,128)(2,1)} %fusion.5.refs_1_, bf16[2048,256]{1,0:T(8,128)(2,1)} %refs_2_.1, bf16[256,2048]{1,0:T(8,128)(2,1)} %refs_3_.1), custom_call_target="tpu_custom_call" | custom-call | tf_op jit(solution)/shard_map/pallas_call | solution.py:165
  56.9 0.0 copy-start.5
  56.9 1.3 %select_reduce_fusion = (f32[256]{0:T(256)S(1)}, f32[256,256]{0,1:T(8,128)S(1)}) fusion(s32[256]{0:T(256)S(1)} %bitcast.46, bf16[4,256,128]{2,1,0:T(8,128)(2,1)} %get-tuple-element.6), kind=kOutput, calls=%fused_computation.23 | convolution fusion | flops 33947392 | bytes 789504 | tf_op jit(solution)/shard_map/dot_general | solution.py:600
  58.3 0.1 fusion.27
  58.4 0.9 %fusion.9.attended_ref = bf16[256,64]{1,0:T(8,128)(2,1)} fusion(f32[256,256]{0,1:T(8,128)S(1)} %get-tuple-element.24, f32[256]{0:T(256)S(1)} %get-tuple-element.23, s32[256]{0:T(256)S(1)} %bitcast.48, f32[256]{0:T(256)S(1)} %fusion.27, bf16[256,192]{1,0:T(8,128)(2,1)S(1)} %convolution_convert_fusion.1), kind=kOutput, calls=%fused_computation.16 | convolution fusion | flops 8814592 | bytes 364544 | tf_op jit(solution)/shard_map/dot_general | solution.py:605
  59.4 0.0 copy-done.5
  59.4 0.2 convert_reduce_fusion.1
  59.6 0.2 convolution_convert_fusion
  59.8 0.7 reshape.103.pages_ref
  60.5 30.8 %shard_map.106 = (f32[8,2048]{1,0:T(8,128)}, bf16[16,32,128]{2,1,0:T(8,128)(2,1)}) custom-call(bf16[256,64]{1,0:T(8,128)(2,1)} %fusion.9.attended_ref, bf16[64,2048]{1,0:T(8,128)(2,1)} %output_ref.1, f32[256,2048]{1,0:T(8,128)} %get-tuple-element.7.feedforward_ref, bf16[8,2048]{1,0:T(8,128)(2,1)} %x_ref.3, bf16[16,32,128]{2,1,0:T(8,128)(2,1)} %reshape.103.pages_ref), custom_call_target="tpu_custom_call" | custom-call | tf_op jit(solution)/shard_map/pallas_call | solution.py:486
  91.3 1.5 %copy.35 = f32[8,2048]{1,0:T(8,128)} copy(f32[8,2048]{1,0:T(8,128)} %get-tuple-element.27) | data formatting | bytes 131072
  92.8 1.6 %copy.36 = bf16[1,16,2,16,128]{4,3,2,1,0:T(8,128)(2,1)} copy(bf16[1,16,2,16,128]{4,3,2,1,0:T(8,128)(2,1)} %bitcast.45) | data formatting | bytes 262144
  (6 shorter events, 0.1 us)
Async XLA Ops:
  0.6 36.1 %copy-start = (bf16[2048,192]{0,1:T(8,128)(2,1)S(1)}, bf16[2048,192]{0,1:T(8,128)(2,1)}, u32[]{:S(2)}) copy-start(bf16[2048,192]{0,1:T(8,128)(2,1)} %param.12) | copy-start | bytes 2359300
  0.6 36.1 %copy-start.4 = (f32[2048]{0:T(1024)S(1)}, f32[2048]{0:T(1024)}, u32[]{:S(2)}) copy-start(f32[2048]{0:T(1024)} %param.10) | copy-start | bytes 24580
  33.3 3.4 %copy-start.1 = (bf16[32,8,2048]{2,1,0:T(8,128)(2,1)S(1)}, bf16[32,8,2048]{2,1,0:T(8,128)(2,1)}, u32[]{:S(2)}) copy-start(bf16[32,8,2048]{2,1,0:T(8,128)(2,1)} %shard_map.104) | copy-start | bytes 3145732
  36.5 0.9 copy-start.2
  36.7 2.9 %copy-start.3 = (f32[2048]{0:T(1024)S(1)}, f32[2048]{0:T(1024)}, u32[]{:S(2)}) copy-start(f32[2048]{0:T(1024)} %param.11) | copy-start | bytes 24580
  56.9 2.5 %copy-start.5 = (s32[16,1]{0,1:T(1,128)S(1)}, s32[16,1]{0,1:T(1,128)}, u32[]{:S(2)}) copy-start(s32[16,1]{0,1:T(1,128)} %param.17) | copy-start | bytes 196

commit v19 on v13

--- a/solution.py
+++ b/solution.py
@@ -398,34 +398,36 @@
 
     lax.fori_loop(1, n_dp, send_pages, 0)
 
-    pair = pltpu.make_async_remote_copy(
-        rows_ref.at[:, :, 1 - core], inbox0, sem0.at[0], sem0.at[1],
-        device_id={"tensor": index - core + 1 - core}, device_id_type=mesh_ids,
-    )
-    pair.start()
-    pair.wait_send()
-    pair.wait_recv()
-    for y in range(n_y):
-        for z in range(n_col):
+    def pair_copy(z):
+        return pltpu.make_async_remote_copy(
+            rows_ref.at[:, z, 1 - core], inbox0.at[:, z], sem0.at[0, z], sem0.at[1, z],
+            device_id={"tensor": index - core + 1 - core}, device_id_type=mesh_ids,
+        )
+
+    order = [(cpos + 1 + k) % n_col for k in range(n_col)]
+    for z in order:
+        pair_copy(z).start()
+
+    def plane_copy(q, z, slot):
+        return pltpu.make_async_remote_copy(
+            chip.at[q, z], inbox1.at[z, slot], send_sem.at[z, q], recv_sem.at[z, slot],
+            device_id={"tensor": ygroup[1](index, q)}, device_id_type=mesh_ids,
+        )
+
+    def col_copy(q, slot):
+        return pltpu.make_async_remote_copy(
+            stage.at[q], inbox2.at[slot], send2_sem.at[q], recv2_sem.at[slot],
+            device_id={"tensor": col[1](index, q)}, device_id_type=mesh_ids,
+        )
+
+    locals_ = []
+    for z in order:
+        pair_copy(z).wait_send()
+        pair_copy(z).wait_recv()
+        for y in range(n_y):
             chip[y, z] = (
                 rows_ref[y, z, core].astype(jnp.float32) + inbox0[y, z].astype(jnp.float32)
             ).astype(chip.dtype)
-
-    def plane_copy(q, z, slot):
-        return pltpu.make_async_remote_copy(
-            chip.at[q, z], inbox1.at[z, slot], send_sem.at[z, q], recv_sem.at[z, slot],
-            device_id={"tensor": ygroup[1](index, q)}, device_id_type=mesh_ids,
-        )
-
-    def col_copy(q, slot):
-        return pltpu.make_async_remote_copy(
-            stage.at[q], inbox2.at[slot], send2_sem.at[q], recv2_sem.at[slot],
-            device_id={"tensor": col[1](index, q)}, device_id_type=mesh_ids,
-        )
-
-    order = [(cpos + 1 + k) % n_col for k in range(n_col)]
-    locals_ = []
-    for z in order:
         local = pltpu.make_async_copy(chip.at[ypos, z], inbox1.at[z, ypos], local_sem.at[z])
         local.start()
         locals_.append(local)
@@ -497,7 +499,7 @@
             pltpu.VMEM((n_col, n_y) + block, x.dtype),
             pltpu.VMEM((n_col,) + block, x.dtype),
             pltpu.VMEM((n_col,) + block, x.dtype),
-            pltpu.SemaphoreType.DMA((2,)),
+            pltpu.SemaphoreType.DMA((2, n_col)),
             pltpu.SemaphoreType.DMA((n_col,)),
             pltpu.SemaphoreType.DMA((n_col, n_y)),
             pltpu.SemaphoreType.DMA((n_col, n_y)),

time: 94.6 us -> 93.7 us (level)
  the two profiles are of different devices: /device:TPU:2 before, /device:TPU:16 now
where the time goes in v19:
time: 93.7 us; the launch traced here: 93.3 us
  Pallas kernels  78.3 us (84%)
  other arithmetic  7.03 us (8%)
  local copies, waits for them, and re-layouts  4.19 us (4%)
  matrix products  2.97 us (3%)
    pallas_call x1, Pallas kernels, gather_tokens(): pl.pallas_call(functools.partial(_gather_kernel, n_col, n_y, col, ygroup,...  29.4 us
    pallas_call x1, Pallas kernels, reduce_rows(): pl.pallas_call(functools.partial(_reduce_kernel, n_col, n_y, n_dp, col, y...  27.5 us
    pallas_call x1, Pallas kernels, exchange_all(): pl.pallas_call(functools.partial(_exchange_kernel, tuple(plans), work, le...  21.4 us
    unnamed x14, local copies, waits for them, and re-layouts  3.07 us

profile of v19, /device:TPU:16, one launch (start us, length us, event | category | flops | bytes accessed | tf_op | source)
XLA Modules:
  0.0 93.3 jit_solution(4096330876700376317)
XLA Ops:
  0.6 0.0 copy-start
  0.6 0.0 copy-start.4
  0.7 29.4 %shard_map.104 = bf16[32,8,2048]{2,1,0:T(8,128)(2,1)} custom-call(bf16[8,2048]{1,0:T(8,128)(2,1)} %x_ref.3), custom_call_target="tpu_custom_call" | custom-call | tf_op jit(solution)/shard_map/pallas_call | solution.py:336
  30.1 0.0 copy-start.1
  30.1 1.5 %convert_reduce_fusion = f32[32,8]{1,0:T(8,128)S(1)} fusion(bf16[32,8,2048]{2,1,0:T(8,128)(2,1)} %shard_map.104), kind=kLoop, calls=%fused_computation.1 | loop fusion | flops 1048320 | bytes 1049600 | tf_op jit(solution)/shard_map/reduce_sum | solution.py:23
  31.6 1.6 %fusion.7 = f32[32,8]{1,0:T(8,128)S(1)} fusion(bf16[32,8,2048]{2,1,0:T(8,128)(2,1)} %shard_map.104, f32[32,8]{1,0:T(8,128)S(1)} %broadcast_multiply_fusion), kind=kLoop, calls=%fused_computation.11 | loop fusion | flops 2096896 | bytes 1050624 | tf_op jit(solution)/shard_map/reduce_sum | solution.py:25
  33.3 0.0 copy-start.2
  33.3 0.1 rsqrt.13
  33.4 0.1 div.19
  33.4 0.0 copy-done
  33.5 0.0 copy-done.4
  33.5 0.0 copy-done.1
  33.5 0.0 copy-start.3
  33.5 0.5 convolution_convert_fusion.1
  34.0 0.1 slice_convert_fusion.1
  34.1 0.0 copy-done.2
  34.1 0.1 compare_reduce_fusion
  34.2 0.1 fusion.44
  34.3 0.3 reduce-window.9
  34.6 0.1 slice.46
  34.7 0.1 slice_reduce_fusion
  34.8 0.1 fusion.45
  34.9 0.6 fusion.31
  35.5 0.1 fusion.48
  35.7 0.7 pad_maximum_fusion
  36.4 0.0 copy-done.3
  36.4 1.4 %fusion.5.refs_1_ = bf16[256,2048]{1,0:T(8,128)(2,1)} fusion(bf16[32,8,2048]{2,1,0:T(8,128)(2,1)S(1)} %copy-done.1, f32[2048]{0:T(1024)S(1)} %copy-done.3, f32[256]{0:T(256)S(1)} %rsqrt.13, f32[256]{0:T(256)S(1)} %div.19), kind=kLoop, calls=%fused_computation.9 | loop fusion | flops 2621440 | bytes 2107392 | tf_op jit(solution)/shard_map/convert_element_type | solution.py:26
  37.8 21.4 %shard_map.105 = (bf16[4,256,128]{2,1,0:T(8,128)(2,1)}, f32[256,2048]{1,0:T(8,128)}) custom-call(bf16[1,256,128]{2,1,0:T(8,128)(2,1)} %get-tuple-element.20.refs_0_, bf16[256,2048]{1,0:T(8,128)(2,1)} %fusion.5.refs_1_, bf16[2048,256]{1,0:T(8,128)(2,1)} %refs_2_.1, bf16[256,2048]{1,0:T(8,128)(2,1)} %refs_3_.1), custom_call_target="tpu_custom_call" | custom-call | tf_op jit(solution)/shard_map/pallas_call | solution.py:165
  59.2 0.0 copy-start.5
  59.2 1.3 %select_reduce_fusion = (f32[256]{0:T(256)S(1)}, f32[256,256]{0,1:T(8,128)S(1)}) fusion(s32[256]{0:T(256)S(1)} %bitcast.46, bf16[4,256,128]{2,1,0:T(8,128)(2,1)} %get-tuple-element.6), kind=kOutput, calls=%fused_computation.23 | convolution fusion | flops 33947392 | bytes 789504 | tf_op jit(solution)/shard_map/dot_general | solution.py:601
  60.5 0.1 fusion.27
  60.7 0.9 %fusion.9.attended_ref = bf16[256,64]{1,0:T(8,128)(2,1)} fusion(f32[256,256]{0,1:T(8,128)S(1)} %get-tuple-element.24, f32[256]{0:T(256)S(1)} %get-tuple-element.23, s32[256]{0:T(256)S(1)} %bitcast.48, f32[256]{0:T(256)S(1)} %fusion.27, bf16[256,192]{1,0:T(8,128)(2,1)S(1)} %convolution_convert_fusion.1), kind=kOutput, calls=%fused_computation.16 | convolution fusion | flops 8814592 | bytes 364544 | tf_op jit(solution)/shard_map/dot_general | solution.py:606
  61.7 0.0 copy-done.5
  61.7 0.2 convert_reduce_fusion.1
  61.9 0.2 convolution_convert_fusion
  62.0 0.7 reshape.103.pages_ref
  62.7 27.5 %shard_map.106 = (f32[8,2048]{1,0:T(8,128)}, bf16[16,32,128]{2,1,0:T(8,128)(2,1)}) custom-call(bf16[256,64]{1,0:T(8,128)(2,1)} %fusion.9.attended_ref, bf16[64,2048]{1,0:T(8,128)(2,1)} %output_ref.1, f32[256,2048]{1,0:T(8,128)} %get-tuple-element.7.feedforward_ref, bf16[8,2048]{1,0:T(8,128)(2,1)} %x_ref.3, bf16[16,32,128]{2,1,0:T(8,128)(2,1)} %reshape.103.pages_ref), custom_call_target="tpu_custom_call" | custom-call | tf_op jit(solution)/shard_map/pallas_call | solution.py:487
  90.2 1.5 %copy.35 = f32[8,2048]{1,0:T(8,128)} copy(f32[8,2048]{1,0:T(8,128)} %get-tuple-element.27) | data formatting | bytes 131072
  91.7 1.6 %copy.36 = bf16[1,16,2,16,128]{4,3,2,1,0:T(8,128)(2,1)} copy(bf16[1,16,2,16,128]{4,3,2,1,0:T(8,128)(2,1)} %bitcast.45) | data formatting | bytes 262144
  (6 shorter events, 0.1 us)
Async XLA Ops:
  0.6 32.8 %copy-start = (bf16[2048,192]{0,1:T(8,128)(2,1)S(1)}, bf16[2048,192]{0,1:T(8,128)(2,1)}, u32[]{:S(2)}) copy-start(bf16[2048,192]{0,1:T(8,128)(2,1)} %param.12) | copy-start | bytes 2359300
  0.6 32.8 %copy-start.4 = (f32[2048]{0:T(1024)S(1)}, f32[2048]{0:T(1024)}, u32[]{:S(2)}) copy-start(f32[2048]{0:T(1024)} %param.10) | copy-start | bytes 24580
  30.1 3.4 %copy-start.1 = (bf16[32,8,2048]{2,1,0:T(8,128)(2,1)S(1)}, bf16[32,8,2048]{2,1,0:T(8,128)(2,1)}, u32[]{:S(2)}) copy-start(bf16[32,8,2048]{2,1,0:T(8,128)(2,1)} %shard_map.104) | copy-start | bytes 3145732
  33.3 0.9 copy-start.2
  33.5 2.9 %copy-start.3 = (f32[2048]{0:T(1024)S(1)}, f32[2048]{0:T(1024)}, u32[]{:S(2)}) copy-start(f32[2048]{0:T(1024)} %param.11) | copy-start | bytes 24580
  59.2 2.5 %copy-start.5 = (s32[16,1]{0,1:T(1,128)S(1)}, s32[16,1]{0,1:T(1,128)}, u32[]{:S(2)}) copy-start(s32[16,1]{0,1:T(1,128)} %param.17) | copy-start | bytes 196
